TPU v7x, 256 devices: a whole 4x4x8 slice. The times are simulated.
256 devices in a mesh: seq: 32 (over z, y), head: 8 (over x, core).
Axes of the slice: x: 4, y: 4, z: 8, core: 2. Of those that a mesh axis runs over, the one named last changes fastest.
Arguments:
- query: bfloat16 [16384, 6144], P('seq', 'head'), may hold values from -6 to 6
- key: bfloat16 [16384, 6144], P('seq', 'head'), may hold values from -6 to 6
- value: bfloat16 [16384, 6144], P('seq', 'head'), may hold values from -6 to 6
- init_state: float32 [48, 128, 128], P('head'), may hold values from -768 to 768
- out_weight: bfloat16 [6144, 6144], P(('head', 'seq')), may hold values from -0.078125 to 0.078125
- out_grad: bfloat16 [16384, 6144], P('seq'), may hold values from -24 to 24
Outputs:
- mixed: bfloat16 [16384, 6144], P('seq', 'head')
- grad_query: bfloat16 [16384, 6144], P('seq', 'head')
- grad_key: bfloat16 [16384, 6144], P('seq', 'head')
- grad_value: bfloat16 [16384, 6144], P('seq', 'head')
- init_grad: float32 [48, 128, 128], P('head')
All inputs are finite; a program needn't handle non-finite values.
Results may differ from a plain program's by a relative error of at most 0.017.
Values may be sent and summed in bfloat16 or wider, within the bound.
A program may use at most 128 MiB of HBM per device.

v0:
```python
import jax
import jax.numpy as jnp
from jax import lax
from jax.sharding import PartitionSpec as P

EPS = 1e-06


def prefix(value, axis, join, neutral, backward):
    count = lax.axis_size(axis)
    place = lax.axis_index(axis)
    ahead = count - 1 - place if backward else place
    gathered = lax.all_gather(value.astype(jnp.bfloat16), axis)
    state = jnp.zeros_like(value) + jnp.asarray(neutral, value.dtype)

    def one(turn, state):
        source = count - 1 - turn if backward else turn
        return join(state, lax.dynamic_index_in_dim(gathered, source, 0, False).astype(value.dtype))

    return lax.fori_loop(0, ahead, one, state)


def normalize(attended):
    return attended * lax.rsqrt(jnp.mean(attended * attended, axis=-1, keepdims=True) + EPS)


def add_states(earlier, later):
    return earlier + later


def shards(query, key, value, init_state, out_weight, out_grad):
    tok_rows = query.shape[0]
    width = query.shape[1]
    heads_here = init_state.shape[0]
    head_dim = init_state.shape[2]
    queries = query.reshape(tok_rows, heads_here, head_dim)
    key_rows = key.reshape(tok_rows, heads_here, head_dim)
    val_rows = value.reshape(tok_rows, heads_here, head_dim)
    local_state = jnp.einsum("thi,thj->hij", key_rows, val_rows, preferred_element_type=jnp.float32)
    zero_state = jnp.zeros_like(local_state)
    earlier = prefix(local_state, "seq", add_states, zero_state, False)
    state_half = (init_state + earlier).astype(jnp.bfloat16)
    row_index = lax.broadcasted_iota(jnp.int32, (tok_rows, tok_rows), 0)
    col_index = lax.broadcasted_iota(jnp.int32, (tok_rows, tok_rows), 1)
    causal = col_index <= row_index
    scores = jnp.einsum("thi,shi->hts", queries, key_rows, preferred_element_type=jnp.float32)
    attn_weights = jnp.where(causal, scores, 0.0).astype(jnp.bfloat16)
    attended = jnp.einsum(
        "hts,shj->thj", attn_weights, val_rows, preferred_element_type=jnp.float32
    )
    attended = attended + jnp.einsum(
        "thi,hij->thj", queries, state_half, preferred_element_type=jnp.float32
    )
    normed = normalize(attended).astype(jnp.bfloat16).reshape(tok_rows, width)
    weight_rows = lax.all_gather(out_weight, "seq", axis=0, tiled=True)
    projected = jnp.dot(normed, weight_rows, preferred_element_type=jnp.float32)
    grad_normed = lax.dot_general(
        out_grad, weight_rows, (((1,), (1,)), ((), ())), preferred_element_type=jnp.float32
    )
    mixed = lax.psum_scatter(
        projected.astype(jnp.bfloat16), "head", scatter_dimension=1, tiled=True
    )
    _, norm_back = jax.vjp(normalize, attended)
    grad_att = norm_back(grad_normed.reshape(tok_rows, heads_here, head_dim))[0].astype(
        jnp.bfloat16
    )
    grad_scores = jnp.einsum("thj,shj->hts", grad_att, val_rows, preferred_element_type=jnp.float32)
    grad_scores = jnp.where(causal, grad_scores, 0.0).astype(jnp.bfloat16)
    own_adjoint = jnp.einsum("thi,thj->hij", queries, grad_att, preferred_element_type=jnp.float32)
    later = prefix(own_adjoint, "seq", add_states, zero_state, True)
    later_half = later.astype(jnp.bfloat16)
    grad_query = jnp.einsum(
        "hts,shi->thi", grad_scores, key_rows, preferred_element_type=jnp.float32
    )
    grad_query = grad_query + jnp.einsum(
        "thj,hij->thi", grad_att, state_half, preferred_element_type=jnp.float32
    )
    grad_key = jnp.einsum("hts,thi->shi", grad_scores, queries, preferred_element_type=jnp.float32)
    grad_key = grad_key + jnp.einsum(
        "thj,hij->thi", val_rows, later_half, preferred_element_type=jnp.float32
    )
    grad_value = jnp.einsum(
        "hts,thj->shj", attn_weights, grad_att, preferred_element_type=jnp.float32
    )
    grad_value = grad_value + jnp.einsum(
        "thi,hij->thj", key_rows, later_half, preferred_element_type=jnp.float32
    )
    init_grad = lax.psum(own_adjoint.astype(jnp.bfloat16), "seq").astype(jnp.float32)
    return (
        mixed,
        grad_query.reshape(tok_rows, width).astype(jnp.bfloat16),
        grad_key.reshape(tok_rows, width).astype(jnp.bfloat16),
        grad_value.reshape(tok_rows, width).astype(jnp.bfloat16),
        init_grad,
    )


def solution(mesh):
    return jax.shard_map(
        shards,
        mesh=mesh,
        in_specs=(
            P("seq", "head"),
            P("seq", "head"),
            P("seq", "head"),
            P("head", None, None),
            P(("head", "seq"), None),
            P("seq", None),
        ),
        out_specs=(
            P("seq", "head"),
            P("seq", "head"),
            P("seq", "head"),
            P("seq", "head"),
            P("head", None, None),
        ),
        check_vma=False,
    )
```

profile of v0, /device:TPU:2, one launch (start us, length us, event | category | flops | bytes accessed | tf_op | source)
XLA Modules:
  0.0 502.1 jit_solution(3683059020974468242)
XLA Ops:
  7.2 1.5 copy.55
  8.7 1.4 copy.58
  12.3 1.1 select_convert_fusion.1
  13.4 1.7 copy-done
  15.1 2.3 fusion.7
  17.4 85.6 %all-gather.8.cloned.1.call-done = bf16[192,128,128]{2,1,0:T(8,128)(2,1)} async-done(((bf16[6,128,128]{2,1,0:T(8,128)(2,1)}), bf16[192,128,128]{2,1,0:T(8,128)(2,1)}) %all-gather.8.cloned.1.call-update) | async-done | bytes 6291472 | tf_op jit(solution)/shard_map/all_gather | solution.py:13
  103.1 103.0 %all-gather.6.cloned.1.call-done = bf16[768,6144]{1,0:T(8,128)(2,1)} async-done(((bf16[24,6144]{1,0:T(8,128)(2,1)}), bf16[768,6144]{1,0:T(8,128)(2,1)}) %all-gather.6.cloned.1.call-update) | async-done | bytes 9437200 | tf_op jit(solution)/shard_map/all_gather | solution.py:55
  206.1 9.6 %fusion.8 = f32[512,768]{0,1:T(8,128)S(1)} fusion(bf16[512,6144]{1,0:T(8,128)(2,1)} %param.15, bf16[768,6144]{1,0:T(8,128)(2,1)} %all-gather.6.cloned.1.call-done), kind=kOutput, calls=%fused_computation.27 | convolution fusion | flops 4831838208 | bytes 17301504 | tf_op jit(solution)/shard_map/dot_general | solution.py:57
  216.3 1.4 fusion
  220.5 10.8 %convolution_convert_fusion = bf16[512,6144]{1,0:T(8,128)(2,1)} fusion(bf16[512,768]{0,1:T(8,128)(2,1)} %bitcast.83, bf16[768,6144]{1,0:T(8,128)(2,1)} %all-gather.6.cloned.1.call-done), kind=kOutput, calls=%fused_computation.2 | convolution fusion | flops 4834983936 | bytes 16515072 | tf_op jit(solution)/shard_map/dot_general | solution.py:56
  231.3 2.0 select_convert_fusion
  233.3 1.1 fusion.9
  234.5 1.2 fusion.2
  235.7 2.3 copy.71
  238.0 3.8 fusion.10
  241.8 1.8 fusion.11
  243.6 119.4 %all-reduce.2.cloned.1.call-done = bf16[6,128,128]{1,2,0:T(8,128)(2,1)} async-done(((bf16[6,128,128]{1,2,0:T(8,128)(2,1)}), bf16[6,128,128]{1,2,0:T(8,128)(2,1)}) %all-reduce.2.cloned.1.call-update) | async-done | bytes 196624 | tf_op jit(solution)/shard_map/psum | solution.py:88
  362.9 1.8 copy.74
  364.8 87.8 %all-gather.10.cloned.1.call-done = bf16[192,128,128]{2,1,0:T(8,128)(2,1)} async-done(((bf16[6,128,128]{2,1,0:T(8,128)(2,1)}), bf16[192,128,128]{2,1,0:T(8,128)(2,1)}) %all-gather.10.cloned.1.call-update) | async-done | bytes 6291472 | tf_op jit(solution)/shard_map/all_gather | solution.py:13
  452.5 32.3 %while.23 = (s32[]{:T(128)}, f32[6,128,128]{2,1,0:T(8,128)S(1)}, s32[]{:T(128)}, bf16[32,6,128,128]{3,2,1,0:T(8,128)(2,1)}, s32[]{:T(128)}, /*index=5*/s32[]{:T(128)}, s32[]{:T(128)}, s32[]{:T(128)}) while((s32[]{:T(128)}, f32[6,128,128]{2,1,0:T(8,128)S(1)}, s32[]{:T(128)}, bf16[32,6,128,128]{3,2,1,0:T(8,128)(2,1)}, s32[]{:T(128)}, ...), condition=%wide.region_6.7_spmd, body=%wide.region_5.6_spmd.sunk | while | flops 196614 | bytes 983183 | solution.py:20
  484.8 2.9 add_convert_fusion
  487.7 2.3 copy.73
  490.4 1.2 copy.72
  491.5 4.1 reduce-scatter.2.cloned.1.call-done
  (70 shorter events, 37.5 us)
Async XLA Ops:
  7.2 4.8 copy-start.6
  7.2 95.8 %all-gather.8.cloned.1.call-start = ((), (), s32[]{:S(2)}) async-start(), calls=%async_computation.4 | async-start | bytes 6488064 | tf_op jit(solution)/shard_map/all_gather | solution.py:13
  11.2 194.9 %all-gather.6.cloned.1.call-start = ((), (), s32[]{:S(2)}) async-start(), calls=%async_computation.1 | async-start | bytes 9732096 | tf_op jit(solution)/shard_map/all_gather | solution.py:55
  12.3 1.1 copy-start.8
  13.4 1.7 copy-start
  17.4 85.7 %copy-start.7 = (f32[6,128,128]{2,1,0:T(8,128)S(1)}, f32[6,128,128]{2,1,0:T(8,128)}, u32[]{:S(2)}) copy-start(f32[6,128,128]{2,1,0:T(8,128)} %param.13) | copy-start | bytes 1179652
  206.1 9.6 %copy-start.4 = (f32[6,512,128]{1,2,0:T(8,128)S(1)}, f32[6,512,128]{1,2,0:T(8,128)}, u32[]{:S(2)}) copy-start(f32[6,512,128]{1,2,0:T(8,128)} %fusion.7) | copy-start | bytes 4718596
  218.1 0.8 copy-start.5
  218.9 144.0 %all-reduce.2.cloned.1.call-start = ((), (), s32[]{:S(2)}) async-start(), calls=%async_computation.3 | async-start | bytes 393216 | tf_op jit(solution)/shard_map/psum | solution.py:88
  219.6 232.9 %all-gather.10.cloned.1.call-start = ((), (), s32[]{:S(2)}) async-start(), calls=%async_computation.5 | async-start | bytes 6488064 | tf_op jit(solution)/shard_map/all_gather | solution.py:13
  220.2 275.4 %reduce-scatter.2.cloned.1.call-start = ((), (), s32[]{:S(2)}) async-start(), calls=%async_computation.2 | async-start | bytes 7077888 | tf_op jit(solution)/shard_map/reduce_scatter | solution.py:60
  233.3 2.4 copy-start.1
  238.0 3.8 copy-start.2
  484.8 5.2 %copy-start.3 = (f32[6,512,128]{1,2,0:T(8,128)S(1)}, f32[6,512,128]{1,2,0:T(8,128)}, u32[]{:S(2)}) copy-start(f32[6,512,128]{1,2,0:T(8,128)} %fusion.11) | copy-start | bytes 4718596
Sparse Core Ops, SparseCore 0:
  11.3 91.6 all-gather.7
  105.6 100.4 all-gather.5
  223.2 139.7 all-reduce.1
  366.3 86.1 all-gather.9
  455.7 39.8 reduce-scatter.1
where the time goes:
time: 506 us; the launch traced here: 502 us
  waiting for transfers between devices  402 us (79%)
  matrix products  38.9 us (8%)
  other arithmetic  33.1 us (7%)
  between operations  14 us (3%)
  local copies, waits for them, and re-layouts  13.3 us (3%)
    all_gather x2, waiting for transfers between devices, prefix(): gathered = lax.all_gather(value.astype(jnp.bfloat16), axis)  173 us
    psum x1, waiting for transfers between devices, shards(): lax.psum(own_adjoint.astype(jnp.bfloat16), 'seq').astype(jnp.float32)  119 us
    all_gather x1, waiting for transfers between devices, shards(): weight_rows = lax.all_gather(out_weight, 'seq', axis=0, tiled=True)  103 us
    add x31, other arithmetic, add_states(): return earlier + later  31.6 us
    unnamed x25, local copies, waits for them, and re-layouts  12.4 us
    dot_general x1, matrix products, shards(): projected = jnp.dot(normed, weight_rows, preferred_element_type=jnp.float32)  10.8 us
  transfers between devices with their start and end apart: 5, of which 5 were waited for; matrix products, arithmetic and copies ran while one was open for 13% of the time, Pallas kernels for 0%

commit v1 on v0

--- a/solution.py
+++ b/solution.py
@@ -6,26 +6,25 @@
 EPS = 1e-06
 
 
-def prefix(value, axis, join, neutral, backward):
+def butterfly(value, axis, backward):
     count = lax.axis_size(axis)
     place = lax.axis_index(axis)
-    ahead = count - 1 - place if backward else place
-    gathered = lax.all_gather(value.astype(jnp.bfloat16), axis)
-    state = jnp.zeros_like(value) + jnp.asarray(neutral, value.dtype)
-
-    def one(turn, state):
-        source = count - 1 - turn if backward else turn
-        return join(state, lax.dynamic_index_in_dim(gathered, source, 0, False).astype(value.dtype))
-
-    return lax.fori_loop(0, ahead, one, state)
+    total = value
+    partial = jnp.zeros_like(value)
+    step = 1
+    while step < count:
+        pairs = [(i, i ^ step) for i in range(count)]
+        other = lax.ppermute(total, axis, perm=pairs)
+        upper = (place & step) != 0
+        take = jnp.logical_not(upper) if backward else upper
+        partial = jnp.where(take, partial + other, partial)
+        total = total + other
+        step *= 2
+    return partial, total
 
 
 def normalize(attended):
     return attended * lax.rsqrt(jnp.mean(attended * attended, axis=-1, keepdims=True) + EPS)
-
-
-def add_states(earlier, later):
-    return earlier + later
 
 
 def shards(query, key, value, init_state, out_weight, out_grad):
@@ -37,8 +36,7 @@
     key_rows = key.reshape(tok_rows, heads_here, head_dim)
     val_rows = value.reshape(tok_rows, heads_here, head_dim)
     local_state = jnp.einsum("thi,thj->hij", key_rows, val_rows, preferred_element_type=jnp.float32)
-    zero_state = jnp.zeros_like(local_state)
-    earlier = prefix(local_state, "seq", add_states, zero_state, False)
+    earlier, _ = butterfly(local_state, "seq", False)
     state_half = (init_state + earlier).astype(jnp.bfloat16)
     row_index = lax.broadcasted_iota(jnp.int32, (tok_rows, tok_rows), 0)
     col_index = lax.broadcasted_iota(jnp.int32, (tok_rows, tok_rows), 1)
@@ -67,7 +65,7 @@
     grad_scores = jnp.einsum("thj,shj->hts", grad_att, val_rows, preferred_element_type=jnp.float32)
     grad_scores = jnp.where(causal, grad_scores, 0.0).astype(jnp.bfloat16)
     own_adjoint = jnp.einsum("thi,thj->hij", queries, grad_att, preferred_element_type=jnp.float32)
-    later = prefix(own_adjoint, "seq", add_states, zero_state, True)
+    later, adjoint_total = butterfly(own_adjoint, "seq", True)
     later_half = later.astype(jnp.bfloat16)
     grad_query = jnp.einsum(
         "hts,shi->thi", grad_scores, key_rows, preferred_element_type=jnp.float32
@@ -85,7 +83,7 @@
     grad_value = grad_value + jnp.einsum(
         "thi,hij->thj", key_rows, later_half, preferred_element_type=jnp.float32
     )
-    init_grad = lax.psum(own_adjoint.astype(jnp.bfloat16), "seq").astype(jnp.float32)
+    init_grad = adjoint_total
     return (
         mixed,
         grad_query.reshape(tok_rows, width).astype(jnp.bfloat16),

time: 506 us -> 248 us (0.49)
  waiting for transfers between devices: 402 us -> 141 us
  starting transfers between devices: 0.34 us -> 37.1 us
  other arithmetic: 33.1 us -> 7.95 us
    all_gather x2 -> x0, waiting for transfers between devices: 173 us -> none  [prefix(): gathered = lax.all_gather(value.astype(jnp.bfloat16), axis)]
    psum x1 -> x0, waiting for transfers between devices: 119 us -> none  [shards(): lax.psum(own_adjoint.astype(jnp.bfloat16), 'seq').astype(jnp.float32)]
    ppermute x0 -> x10, waiting for transfers between devices: none -> 112 us  [butterfly(): other = lax.ppermute(total, axis, perm=pairs)]
    all_gather x1, waiting for transfers between devices: 103 us -> 28.3 us  [shards(): weight_rows = lax.all_gather(out_weight, 'seq', axis=0, tiled=True)]
    ppermute x0 -> x10, starting transfers between devices: none -> 37 us  [butterfly(): other = lax.ppermute(total, axis, perm=pairs)]
    add x31 -> x9, other arithmetic: 31.6 us -> 5.28 us  [butterfly(): total = total + other]
    unnamed x25 -> x68, local copies, waits for them, and re-layouts: 12.4 us -> 11.4 us
  transfers between devices with their start and end apart: 5 -> 12, of which waited for: 5 -> 11; matrix products, arithmetic and copies ran while one was open for 13% -> 13% of each run, Pallas kernels for 0% -> 0%
where the time goes in v1:
time: 248 us
  waiting for transfers between devices  141 us (57%)
  starting transfers between devices  37.1 us (15%)
  matrix products  35.9 us (14%)
  between operations  14.4 us (6%)
  local copies, waits for them, and re-layouts  11.4 us (5%)
  other arithmetic  7.95 us (3%)
    ppermute x10, waiting for transfers between devices, butterfly(): other = lax.ppermute(total, axis, perm=pairs)  112 us
    ppermute x10, starting transfers between devices, butterfly(): other = lax.ppermute(total, axis, perm=pairs)  37 us
    all_gather x1, waiting for transfers between devices, shards(): weight_rows = lax.all_gather(out_weight, 'seq', axis=0, tiled=True)  28.3 us
    unnamed x68, local copies, waits for them, and re-layouts  11.4 us
    dot_general x1, matrix products, shards(): lax.dot_general(out_grad, weight_rows, (((1,), (1,)), ((), ())), preferre...  9.65 us
    dot_general x1, matrix products, shards(): projected = jnp.dot(normed, weight_rows, preferred_element_type=jnp.float32)  7.21 us
    add x9, other arithmetic, butterfly(): total = total + other  5.28 us
  transfers between devices with their start and end apart: 12, of which 11 were waited for; matrix products, arithmetic and copies ran while one was open for 13% of the time, Pallas kernels for 0%

profile of v1, /device:TPU:2, one launch (start us, length us, event | category | flops | bytes accessed | tf_op | source)
XLA Modules:
  0.0 247.8 jit_solution(7579798683494000018)
XLA Ops:
  11.8 9.3 %collective-permute-done = f32[6,128,128]{2,1,0:T(8,128)S(1)} collective-permute-done((f32[6,128,128]{2,1,0:T(8,128)S(1)}, f32[6,128,128]{2,1,0:T(8,128)S(1)}, u32[]{:S(2)}, u32[]{:S(2)}) %collective-permute-start) | collective-permute-done | bytes 393248 | tf_op jit(solution)/shard_map/ppermute | solution.py:17
  21.2 3.3 %collective-permute-start.1 = (f32[6,128,128]{2,1,0:T(8,128)S(1)}, f32[6,128,128]{2,1,0:T(8,128)S(1)}, u32[]{:S(2)}, u32[]{:S(2)}) collective-permute-start(f32[6,128,128]{2,1,0:T(8,128)S(1)} %add.80), channel_id=1, source_target_pairs={{0,16},{8,24},{16,0},{24,8},{32,48},{40,56},{48,32},{56,40},{64,80... | collective-permute-start | bytes 1179656 | tf_op jit(solution)/shard_map/ppermute | solution.py:17
  24.5 10.7 %collective-permute-done.1 = f32[6,128,128]{2,1,0:T(8,128)S(1)} collective-permute-done((f32[6,128,128]{2,1,0:T(8,128)S(1)}, f32[6,128,128]{2,1,0:T(8,128)S(1)}, u32[]{:S(2)}, u32[]{:S(2)}) %collective-permute-start.1) | collective-permute-done | bytes 393248 | tf_op jit(solution)/shard_map/ppermute | solution.py:17
  35.9 2.6 %collective-permute-start.2 = (f32[6,128,128]{2,1,0:T(8,128)S(1)}, f32[6,128,128]{2,1,0:T(8,128)S(1)}, u32[]{:S(2)}, u32[]{:S(2)}) collective-permute-start(f32[6,128,128]{2,1,0:T(8,128)S(1)} %add.82), channel_id=1, source_target_pairs={{0,32},{8,40},{16,48},{24,56},{32,0},{40,8},{48,16},{56,24},{64,96... | collective-permute-start | bytes 1179656 | tf_op jit(solution)/shard_map/ppermute | solution.py:17
  38.5 11.1 %collective-permute-done.2 = f32[6,128,128]{2,1,0:T(8,128)S(1)} collective-permute-done((f32[6,128,128]{2,1,0:T(8,128)S(1)}, f32[6,128,128]{2,1,0:T(8,128)S(1)}, u32[]{:S(2)}, u32[]{:S(2)}) %collective-permute-start.2) | collective-permute-done | bytes 393248 | tf_op jit(solution)/shard_map/ppermute | solution.py:17
  50.4 7.6 %collective-permute-start.3 = (f32[6,128,128]{2,1,0:T(8,128)S(1)}, f32[6,128,128]{2,1,0:T(8,128)S(1)}, u32[]{:S(2)}, u32[]{:S(2)}) collective-permute-start(f32[6,128,128]{2,1,0:T(8,128)S(1)} %add.84), channel_id=1, source_target_pairs={{0,64},{8,72},{16,80},{24,88},{32,96},{40,104},{48,112},{56,120},{... | collective-permute-start | bytes 1179656 | tf_op jit(solution)/shard_map/ppermute | solution.py:17
  59.3 10.9 %collective-permute-done.3 = f32[6,128,128]{2,1,0:T(8,128)S(1)} collective-permute-done((f32[6,128,128]{2,1,0:T(8,128)S(1)}, f32[6,128,128]{2,1,0:T(8,128)S(1)}, u32[]{:S(2)}, u32[]{:S(2)}) %collective-permute-start.3) | collective-permute-done | bytes 393248 | tf_op jit(solution)/shard_map/ppermute | solution.py:17
  70.2 11.3 %collective-permute-start.4 = (f32[6,128,128]{2,1,0:T(8,128)S(1)}, f32[6,128,128]{2,1,0:T(8,128)}, u32[]{:S(2)}, u32[]{:S(2)}) collective-permute-start(f32[6,128,128]{2,1,0:T(8,128)S(1)} %add.86), channel_id=1, source_target_pairs={{0,128},{8,136},{16,144},{24,152},{32,160},{40,168},{48,176},{56,1... | collective-permute-start | bytes 1179656 | tf_op jit(solution)/shard_map/ppermute | solution.py:17
  81.5 2.5 select_convert_fusion.1
  84.1 3.6 %fusion.8 = f32[6,512,128]{1,2,0:T(8,128)} fusion(bf16[6,512,512]{2,1,0:T(8,128)(2,1)S(1)} %select_convert_fusion.1, bf16[512,6,128]{0,2,1:T(8,128)(2,1)} %bitcast.57), kind=kOutput, calls=%fused_computation.31 | convolution fusion | flops 402653184 | bytes 5505024 | tf_op jit(solution)/shard_map/hts,shj->thj/dot_general | solution.py:46
  87.7 18.9 %collective-permute-done.4 = f32[6,128,128]{2,1,0:T(8,128)} collective-permute-done((f32[6,128,128]{2,1,0:T(8,128)S(1)}, f32[6,128,128]{2,1,0:T(8,128)}, u32[]{:S(2)}, u32[]{:S(2)}) %collective-permute-start.4) | collective-permute-done | bytes 393248 | tf_op jit(solution)/shard_map/ppermute | solution.py:17
  107.7 28.3 %all-gather.2.cloned.1.call-done = bf16[768,6144]{1,0:T(8,128)(2,1)} async-done(((bf16[24,6144]{1,0:T(8,128)(2,1)}), bf16[768,6144]{1,0:T(8,128)(2,1)}) %all-gather.2.cloned.1.call-update) | async-done | bytes 9437200 | tf_op jit(solution)/shard_map/all_gather | solution.py:53
  136.0 9.6 %fusion.10 = f32[512,768]{0,1:T(8,128)S(1)} fusion(bf16[512,6144]{1,0:T(8,128)(2,1)} %param.11, bf16[768,6144]{1,0:T(8,128)(2,1)} %all-gather.2.cloned.1.call-done), kind=kOutput, calls=%fused_computation.33 | convolution fusion | flops 4831838208 | bytes 17301504 | tf_op jit(solution)/shard_map/dot_general | solution.py:55
  149.7 7.2 %convolution_convert_fusion = bf16[512,6144]{1,0:T(8,128)(2,1)} fusion(bf16[512,768]{0,1:T(8,128)(2,1)S(1)} %bitcast.73, bf16[768,6144]{1,0:T(8,128)(2,1)S(1)} %copy-done.30), kind=kOutput, calls=%fused_computation | convolution fusion | flops 4834983936 | bytes 16515072 | tf_op jit(solution)/shard_map/dot_general | solution.py:54
  159.2 10.2 %collective-permute-done.5 = f32[6,128,128]{2,1,0:T(8,128)S(1)} collective-permute-done((f32[6,128,128]{2,1,0:T(8,128)S(1)}, f32[6,128,128]{2,1,0:T(8,128)S(1)}, u32[]{:S(2)}, u32[]{:S(2)}) %collective-permute-start.5) | collective-permute-done | bytes 393248 | tf_op jit(solution)/shard_map/ppermute | solution.py:17
  169.5 3.6 %collective-permute-start.6 = (f32[6,128,128]{2,1,0:T(8,128)S(1)}, f32[6,128,128]{2,1,0:T(8,128)S(1)}, u32[]{:S(2)}, u32[]{:S(2)}) collective-permute-start(f32[6,128,128]{2,1,0:T(8,128)S(1)} %add.92), channel_id=1, source_target_pairs={{0,16},{8,24},{16,0},{24,8},{32,48},{40,56},{48,32},{56,40},{64,80... | collective-permute-start | bytes 1179656 | tf_op jit(solution)/shard_map/ppermute | solution.py:17
  173.1 8.2 %collective-permute-done.6 = f32[6,128,128]{2,1,0:T(8,128)S(1)} collective-permute-done((f32[6,128,128]{2,1,0:T(8,128)S(1)}, f32[6,128,128]{2,1,0:T(8,128)S(1)}, u32[]{:S(2)}, u32[]{:S(2)}) %collective-permute-start.6) | collective-permute-done | bytes 393248 | tf_op jit(solution)/shard_map/ppermute | solution.py:17
  182.2 3.0 %fusion.12 = f32[6,128,512]{2,1,0:T(8,128)} fusion(bf16[512,6,128]{0,2,1:T(8,128)(2,1)} %get-tuple-element.17, bf16[6,512,512]{2,1,0:T(8,128)(2,1)S(1)} %select_convert_fusion.1), kind=kOutput, calls=%fused_computation.35 | convolution fusion | flops 402653184 | bytes 5505024 | tf_op jit(solution)/shard_map/hts,thj->shj/dot_general | solution.py:80
  185.3 6.5 %collective-permute-done.7 = f32[6,128,128]{2,1,0:T(8,128)} collective-permute-done((f32[6,128,128]{2,1,0:T(8,128)}, f32[6,128,128]{2,1,0:T(8,128)}, u32[]{:S(2)}, u32[]{:S(2)}) %collective-permute-start.7) | collective-permute-done | bytes 393248 | tf_op jit(solution)/shard_map/ppermute | solution.py:17
  195.7 15.2 %collective-permute-done.8 = f32[6,128,128]{2,1,0:T(8,128)S(1)} collective-permute-done((f32[6,128,128]{2,1,0:T(8,128)S(1)}, f32[6,128,128]{2,1,0:T(8,128)S(1)}, u32[]{:S(2)}, u32[]{:S(2)}) %collective-permute-start.8) | collective-permute-done | bytes 393248 | tf_op jit(solution)/shard_map/ppermute | solution.py:17
  211.8 5.9 %collective-permute-start.9 = (f32[6,128,128]{2,1,0:T(8,128)}, f32[6,128,128]{2,1,0:T(8,128)}, u32[]{:S(2)}, u32[]{:S(2)}) collective-permute-start(f32[6,128,128]{2,1,0:T(8,128)} %add.98), channel_id=1, source_target_pairs={{0,128},{8,136},{16,144},{24,152},{32,160},{40,168},{48,176},{56,1... | collective-permute-start | bytes 1179656 | tf_op jit(solution)/shard_map/ppermute | solution.py:17
  219.0 2.3 copy.49
  221.3 3.0 %fusion.13 = f32[6,512,128]{1,2,0:T(8,128)} fusion(bf16[512,6,128]{0,2,1:T(8,128)(2,1)} %bitcast.66, bf16[6,512,512]{2,1,0:T(8,128)(2,1)S(1)} %select_convert_fusion), kind=kOutput, calls=%fused_computation.36 | convolution fusion | flops 402653184 | bytes 5505024 | tf_op jit(solution)/shard_map/hts,thi->shi/dot_general | solution.py:76
  224.3 11.3 %collective-permute-done.9 = f32[6,128,128]{2,1,0:T(8,128)} collective-permute-done((f32[6,128,128]{2,1,0:T(8,128)}, f32[6,128,128]{2,1,0:T(8,128)}, u32[]{:S(2)}, u32[]{:S(2)}) %collective-permute-start.9) | collective-permute-done | bytes 393248 | tf_op jit(solution)/shard_map/ppermute | solution.py:17
  (97 shorter events, 27.5 us)
Async XLA Ops:
  7.2 128.8 %all-gather.2.cloned.1.call-start = ((), (), s32[]{:S(2)}) async-start(), calls=%async_computation.1 | async-start | bytes 9732096 | tf_op jit(solution)/shard_map/all_gather | solution.py:53
  7.9 233.1 %reduce-scatter.2.cloned.1.call-start = ((), (), s32[]{:S(2)}) async-start(), calls=%async_computation.2 | async-start | bytes 7077888 | tf_op jit(solution)/shard_map/reduce_scatter | solution.py:58
  10.3 47.8 %copy-start.26 = (bf16[512,768]{1,0:T(8,128)(2,1)S(1)}, bf16[512,768]{1,0:T(8,128)(2,1)}, u32[]{:S(2)}) copy-start(bf16[512,768]{1,0:T(8,128)(2,1)} %param.6) | copy-start | bytes 2359300
  10.3 10.9 %collective-permute-start = (f32[6,128,128]{2,1,0:T(8,128)S(1)}, f32[6,128,128]{2,1,0:T(8,128)S(1)}, u32[]{:S(2)}, u32[]{:S(2)}) collective-permute-start(f32[6,128,128]{2,1,0:T(8,128)S(1)} %fusion.9), channel_id=1, source_target_pairs={{0,8},{8,0},{16,24},{24,16},{32,40},{40,32},{48,56},{56,48},{64,72... | collective-permute-start | bytes 1179656 | tf_op jit(solution)/shard_map/ppermute | solution.py:17
  21.1 29.3 %copy-start.11 = (f32[6,128,128]{2,1,0:T(8,128)}, f32[6,128,128]{2,1,0:T(8,128)S(1)}, u32[]{:S(2)}) copy-start(f32[6,128,128]{2,1,0:T(8,128)S(1)} %collective-permute-done) | copy-start | bytes 1179652
  21.2 13.9 %collective-permute-start.1 = (f32[6,128,128]{2,1,0:T(8,128)S(1)}, f32[6,128,128]{2,1,0:T(8,128)S(1)}, u32[]{:S(2)}, u32[]{:S(2)}) collective-permute-start(f32[6,128,128]{2,1,0:T(8,128)S(1)} %add.80), channel_id=1, source_target_pairs={{0,16},{8,24},{16,0},{24,8},{32,48},{40,56},{48,32},{56,40},{64,80... | collective-permute-start | bytes 1179656 | tf_op jit(solution)/shard_map/ppermute | solution.py:17
  35.9 13.7 %collective-permute-start.2 = (f32[6,128,128]{2,1,0:T(8,128)S(1)}, f32[6,128,128]{2,1,0:T(8,128)S(1)}, u32[]{:S(2)}, u32[]{:S(2)}) collective-permute-start(f32[6,128,128]{2,1,0:T(8,128)S(1)} %add.82), channel_id=1, source_target_pairs={{0,32},{8,40},{16,48},{24,56},{32,0},{40,8},{48,16},{56,24},{64,96... | collective-permute-start | bytes 1179656 | tf_op jit(solution)/shard_map/ppermute | solution.py:17
  50.4 19.8 %collective-permute-start.3 = (f32[6,128,128]{2,1,0:T(8,128)S(1)}, f32[6,128,128]{2,1,0:T(8,128)S(1)}, u32[]{:S(2)}, u32[]{:S(2)}) collective-permute-start(f32[6,128,128]{2,1,0:T(8,128)S(1)} %add.84), channel_id=1, source_target_pairs={{0,64},{8,72},{16,80},{24,88},{32,96},{40,104},{48,112},{56,120},{... | collective-permute-start | bytes 1179656 | tf_op jit(solution)/shard_map/ppermute | solution.py:17
  59.3 24.7 %copy-start.28 = (pred[512,512]{1,0:T(8,128)(4,1)}, pred[512,512]{1,0:T(8,128)(4,1)S(1)}, u32[]{:S(2)}) copy-start(pred[512,512]{1,0:T(8,128)(4,1)S(1)} %iota_compare_fusion) | copy-start | bytes 786436
  70.2 36.3 %collective-permute-start.4 = (f32[6,128,128]{2,1,0:T(8,128)S(1)}, f32[6,128,128]{2,1,0:T(8,128)}, u32[]{:S(2)}, u32[]{:S(2)}) collective-permute-start(f32[6,128,128]{2,1,0:T(8,128)S(1)} %add.86), channel_id=1, source_target_pairs={{0,128},{8,136},{16,144},{24,152},{32,160},{40,168},{48,176},{56,1... | collective-permute-start | bytes 1179656 | tf_op jit(solution)/shard_map/ppermute | solution.py:17
  84.0 22.5 %copy-start.12 = (f32[6,128,128]{2,1,0:T(8,128)S(1)}, f32[6,128,128]{2,1,0:T(8,128)}, u32[]{:S(2)}) copy-start(f32[6,128,128]{2,1,0:T(8,128)} %copy-done.11) | copy-start | bytes 1179652
  84.0 22.5 %copy-start.14 = (f32[6,128,128]{2,1,0:T(8,128)S(1)}, f32[6,128,128]{2,1,0:T(8,128)}, u32[]{:S(2)}) copy-start(f32[6,128,128]{2,1,0:T(8,128)} %copy-done.13) | copy-start | bytes 1179652
  84.1 22.5 %copy-start.16 = (f32[6,128,128]{2,1,0:T(8,128)S(1)}, f32[6,128,128]{2,1,0:T(8,128)}, u32[]{:S(2)}) copy-start(f32[6,128,128]{2,1,0:T(8,128)} %copy-done.15) | copy-start | bytes 1179652
  84.1 22.5 %copy-start.18 = (f32[6,128,128]{2,1,0:T(8,128)S(1)}, f32[6,128,128]{2,1,0:T(8,128)}, u32[]{:S(2)}) copy-start(f32[6,128,128]{2,1,0:T(8,128)} %copy-done.17) | copy-start | bytes 1179652
  84.1 22.4 %copy-start.27 = (f32[6,128,128]{2,1,0:T(8,128)S(1)}, f32[6,128,128]{2,1,0:T(8,128)}, u32[]{:S(2)}) copy-start(f32[6,128,128]{2,1,0:T(8,128)} %param.9) | copy-start | bytes 1179652
  158.6 10.8 %collective-permute-start.5 = (f32[6,128,128]{2,1,0:T(8,128)S(1)}, f32[6,128,128]{2,1,0:T(8,128)S(1)}, u32[]{:S(2)}, u32[]{:S(2)}) collective-permute-start(f32[6,128,128]{2,1,0:T(8,128)S(1)} %convolution_bitcast_fusion), channel_id=1, source_target_pairs={{0,8},{8,0},{16,24},{24,16},{32,40},{40,32},{48,56},{56,48},{64,72... | collective-permute-start | bytes 1179656 | tf_op jit(solution)/shard_map/ppermute | solution.py:17
  169.5 11.8 %collective-permute-start.6 = (f32[6,128,128]{2,1,0:T(8,128)S(1)}, f32[6,128,128]{2,1,0:T(8,128)S(1)}, u32[]{:S(2)}, u32[]{:S(2)}) collective-permute-start(f32[6,128,128]{2,1,0:T(8,128)S(1)} %add.92), channel_id=1, source_target_pairs={{0,16},{8,24},{16,0},{24,8},{32,48},{40,56},{48,32},{56,40},{64,80... | collective-permute-start | bytes 1179656 | tf_op jit(solution)/shard_map/ppermute | solution.py:17
  182.2 9.6 %collective-permute-start.7 = (f32[6,128,128]{2,1,0:T(8,128)}, f32[6,128,128]{2,1,0:T(8,128)}, u32[]{:S(2)}, u32[]{:S(2)}) collective-permute-start(f32[6,128,128]{2,1,0:T(8,128)} %add.94), channel_id=1, source_target_pairs={{0,32},{8,40},{16,48},{24,56},{32,0},{40,8},{48,16},{56,24},{64,96... | collective-permute-start | bytes 1179656 | tf_op jit(solution)/shard_map/ppermute | solution.py:17
  193.0 18.0 %collective-permute-start.8 = (f32[6,128,128]{2,1,0:T(8,128)S(1)}, f32[6,128,128]{2,1,0:T(8,128)S(1)}, u32[]{:S(2)}, u32[]{:S(2)}) collective-permute-start(f32[6,128,128]{2,1,0:T(8,128)S(1)} %add.96), channel_id=1, source_target_pairs={{0,64},{8,72},{16,80},{24,88},{32,96},{40,104},{48,112},{56,120},{... | collective-permute-start | bytes 1179656 | tf_op jit(solution)/shard_map/ppermute | solution.py:17
  211.8 23.8 %collective-permute-start.9 = (f32[6,128,128]{2,1,0:T(8,128)}, f32[6,128,128]{2,1,0:T(8,128)}, u32[]{:S(2)}, u32[]{:S(2)}) collective-permute-start(f32[6,128,128]{2,1,0:T(8,128)} %add.98), channel_id=1, source_target_pairs={{0,128},{8,136},{16,144},{24,152},{32,160},{40,168},{48,176},{56,1... | collective-permute-start | bytes 1179656 | tf_op jit(solution)/shard_map/ppermute | solution.py:17
  221.3 14.3 %copy-start.20 = (f32[6,128,128]{2,1,0:T(8,128)S(1)}, f32[6,128,128]{2,1,0:T(8,128)}, u32[]{:S(2)}) copy-start(f32[6,128,128]{2,1,0:T(8,128)} %copy-done.19) | copy-start | bytes 1179652
  221.3 14.3 %copy-start.22 = (f32[6,128,128]{2,1,0:T(8,128)S(1)}, f32[6,128,128]{2,1,0:T(8,128)}, u32[]{:S(2)}) copy-start(f32[6,128,128]{2,1,0:T(8,128)} %copy-done.21) | copy-start | bytes 1179652
  221.3 14.3 %copy-start.24 = (f32[6,128,128]{2,1,0:T(8,128)S(1)}, f32[6,128,128]{2,1,0:T(8,128)}, u32[]{:S(2)}) copy-start(f32[6,128,128]{2,1,0:T(8,128)} %copy-done.23) | copy-start | bytes 1179652
  224.3 13.4 %copy-start.8 = (f32[6,128,512]{2,1,0:T(8,128)S(1)}, f32[6,128,512]{2,1,0:T(8,128)}, u32[]{:S(2)}) copy-start(f32[6,128,512]{2,1,0:T(8,128)} %fusion.12) | copy-start | bytes 4718596
  (19 other events, 124.0 us)
Sparse Core Ops, SparseCore 0:
  10.6 125.3 all-gather.1
  157.0 42.3 reduce-scatter.1

commit v2 on v1

--- a/solution.py
+++ b/solution.py
@@ -1,26 +1,72 @@
+import functools
+
 import jax
 import jax.numpy as jnp
 from jax import lax
+from jax.experimental import pallas as pl
+from jax.experimental.pallas import tpu as pltpu
 from jax.sharding import PartitionSpec as P
 
 EPS = 1e-06
 
 
+MESH = pl.DeviceIdType.MESH
+
+
+def butterfly_kernel(count, backward, value_ref, partial_ref, total_ref, sendbuf, recvbuf, send_sem, recv_sem):
+    me = lax.axis_index("seq")
+    head = lax.axis_index("head")
+    rounds = count.bit_length() - 1
+    partners = []
+    for k in range(rounds):
+        step = 1 << k
+        bit = (me // step) % 2
+        partners.append((me + step - 2 * step * bit, bit))
+    barrier = pltpu.get_barrier_semaphore()
+    for partner, _ in partners:
+        pl.semaphore_signal(barrier, inc=1, device_id=(partner, head), device_id_type=MESH)
+    pl.semaphore_wait(barrier, rounds)
+    total = value_ref[...]
+    partial = jnp.zeros_like(total)
+    for k, (partner, bit) in enumerate(partners):
+        sendbuf[k] = total
+        copy = pltpu.make_async_remote_copy(
+            src_ref=sendbuf.at[k],
+            dst_ref=recvbuf.at[k],
+            send_sem=send_sem.at[k],
+            recv_sem=recv_sem.at[k],
+            device_id=(partner, head),
+            device_id_type=MESH,
+        )
+        copy.start()
+        copy.wait()
+        other = recvbuf[k]
+        take = (bit == 0) if backward else (bit == 1)
+        partial = jnp.where(take, partial + other, partial)
+        total = total + other
+    partial_ref[...] = partial
+    total_ref[...] = total
+
+
 def butterfly(value, axis, backward):
     count = lax.axis_size(axis)
-    place = lax.axis_index(axis)
-    total = value
-    partial = jnp.zeros_like(value)
-    step = 1
-    while step < count:
-        pairs = [(i, i ^ step) for i in range(count)]
-        other = lax.ppermute(total, axis, perm=pairs)
-        upper = (place & step) != 0
-        take = jnp.logical_not(upper) if backward else upper
-        partial = jnp.where(take, partial + other, partial)
-        total = total + other
-        step *= 2
-    return partial, total
+    rounds = count.bit_length() - 1
+    shape = jax.ShapeDtypeStruct(value.shape, jnp.float32)
+    return pl.pallas_call(
+        functools.partial(butterfly_kernel, count, backward),
+        out_shape=(shape, shape),
+        in_specs=[pl.BlockSpec(memory_space=pltpu.VMEM)],
+        out_specs=(pl.BlockSpec(memory_space=pltpu.VMEM), pl.BlockSpec(memory_space=pltpu.VMEM)),
+        scratch_shapes=[
+            pltpu.VMEM((rounds,) + value.shape, jnp.float32),
+            pltpu.VMEM((rounds,) + value.shape, jnp.float32),
+            pltpu.SemaphoreType.DMA((rounds,)),
+            pltpu.SemaphoreType.DMA((rounds,)),
+        ],
+        compiler_params=pltpu.CompilerParams(
+            collective_id=1 if backward else 0, has_side_effects=True
+        ),
+    )(value.astype(jnp.float32))
 
 
 def normalize(attended):

time: 248 us -> 257 us (1.036)
  Pallas kernels: 0 us -> 168 us
  waiting for transfers between devices: 141 us -> 24.7 us
  starting transfers between devices: 37.1 us -> 0.08 us
  other arithmetic: 7.95 us -> 2.62 us
    pallas_call x0 -> x2, Pallas kernels: none -> 168 us  [butterfly(): pl.pallas_call(functools.partial(butterfly_kernel, count, backward), out_...]
    ppermute x10 -> x0, waiting for transfers between devices: 112 us -> none  [butterfly(): other = lax.ppermute(total, axis, perm=pairs)]
    ppermute x10 -> x0, starting transfers between devices: 37 us -> none  [butterfly(): other = lax.ppermute(total, axis, perm=pairs)]
    add x9 -> x0, other arithmetic: 5.28 us -> none  [butterfly(): total = total + other]
    all_gather x1, waiting for transfers between devices: 28.3 us -> 24 us  [shards(): weight_rows = lax.all_gather(out_weight, 'seq', axis=0, tiled=True)]
    unnamed x68 -> x41, local copies, waits for them, and re-layouts: 11.4 us -> 10.9 us
  transfers between devices with their start and end apart: 12 -> 2, of which waited for: 11 -> 1; matrix products, arithmetic and copies ran while one was open for 13% -> 10% of each run, Pallas kernels for 0% -> 66%
where the time goes in v2:
time: 257 us; the launch traced here: 256 us
  Pallas kernels  168 us (65%)
  matrix products  35.3 us (14%)
  waiting for transfers between devices  24.7 us (10%)
  between operations  14.3 us (6%)
  local copies, waits for them, and re-layouts  10.9 us (4%)
  other arithmetic  2.62 us (1%)
    pallas_call x2, Pallas kernels, butterfly(): pl.pallas_call(functools.partial(butterfly_kernel, count, backward), out_...  168 us
    all_gather x1, waiting for transfers between devices, shards(): weight_rows = lax.all_gather(out_weight, 'seq', axis=0, tiled=True)  24 us
    unnamed x41, local copies, waits for them, and re-layouts  10.9 us
    dot_general x1, matrix products, shards(): lax.dot_general(out_grad, weight_rows, (((1,), (1,)), ((), ())), preferre...  9.65 us
    dot_general x1, matrix products, shards(): projected = jnp.dot(normed, weight_rows, preferred_element_type=jnp.float32)  7.22 us
  transfers between devices with their start and end apart: 2, of which 1 were waited for; matrix products, arithmetic and copies ran while one was open for 10% of the time, Pallas kernels for 66%

profile of v2, /device:TPU:2, one launch (start us, length us, event | category | flops | bytes accessed | tf_op | source)
XLA Modules:
  0.0 256.0 jit_solution(3271014106662040617)
XLA Ops:
  7.2 0.7 all-gather.2.cloned.1.call-update
  8.0 2.4 copy.32
  10.9 1.1 fusion.7.value_ref
  12.0 96.0 %shard_map.101 = (f32[6,128,128]{2,1,0:T(8,128)}, f32[6,128,128]{2,1,0:T(8,128)}) custom-call(f32[6,128,128]{2,1,0:T(8,128)} %fusion.7.value_ref), custom_call_target="tpu_custom_call" | custom-call | tf_op jit(solution)/shard_map/pallas_call | solution.py:55
  108.1 1.1 add_convert_fusion.1
  109.3 2.6 %select_convert_fusion.1 = bf16[6,512,512]{2,1,0:T(8,128)(2,1)S(1)} fusion(pred[512,512]{1,0:T(8,128)(4,1)S(1)} %iota_compare_fusion, bf16[512,6,128]{0,2,1:T(8,128)(2,1)} %bitcast.62, bf16[512,6,128]{0,2,1:T(8,128)(2,1)} %bitcast.55), kind=kOutput, calls=%fused_computation.2 | convolution fusion | flops 405798912 | bytes 4980736 | tf_op jit(solution)/shard_map/thi,shi->hts/dot_general | solution.py:90
  111.9 2.3 fusion.6
  114.2 24.0 %all-gather.2.cloned.1.call-done = bf16[768,6144]{1,0:T(8,128)(2,1)} async-done(((bf16[24,6144]{1,0:T(8,128)(2,1)}), bf16[768,6144]{1,0:T(8,128)(2,1)}) %all-gather.2.cloned.1.call-update) | async-done | bytes 9437200 | tf_op jit(solution)/shard_map/all_gather | solution.py:99
  138.2 9.6 %fusion.8 = f32[512,768]{0,1:T(8,128)S(1)} fusion(bf16[512,6144]{1,0:T(8,128)(2,1)} %param.11, bf16[768,6144]{1,0:T(8,128)(2,1)} %all-gather.2.cloned.1.call-done), kind=kOutput, calls=%fused_computation.24 | convolution fusion | flops 4831838208 | bytes 17301504 | tf_op jit(solution)/shard_map/dot_general | solution.py:101
  147.9 0.6 multiply_reduce_fusion
  148.5 1.4 fusion
  149.9 2.0 copy-done.16
  151.9 7.2 %convolution_convert_fusion = bf16[512,6144]{1,0:T(8,128)(2,1)} fusion(bf16[512,768]{0,1:T(8,128)(2,1)S(1)} %bitcast.71, bf16[768,6144]{1,0:T(8,128)(2,1)S(1)} %copy-done.16), kind=kOutput, calls=%fused_computation | convolution fusion | flops 4834983936 | bytes 16515072 | tf_op jit(solution)/shard_map/dot_general | solution.py:100
  159.1 2.5 convolution_bitcast_fusion.value_ref
  161.6 72.1 %shard_map.102 = (f32[6,128,128]{2,1,0:T(8,128)}, f32[6,128,128]{2,1,0:T(8,128)}) custom-call(f32[6,128,128]{2,1,0:T(8,128)} %convolution_bitcast_fusion.value_ref), custom_call_target="tpu_custom_call" | custom-call | tf_op jit(solution)/shard_map/pallas_call | solution.py:55
  233.7 1.8 fusion.10
  236.0 1.2 copy.51
  237.1 2.6 %select_convert_fusion = bf16[6,512,512]{2,1,0:T(8,128)(2,1)S(1)} fusion(pred[512,512]{1,0:T(8,128)(4,1)} %copy-done.15, bf16[512,6,128]{0,2,1:T(8,128)(2,1)} %get-tuple-element.23, bf16[512,6,128]{0,2,1:T(8,128)(2,1)} %bitcast.59), kind=kOutput, calls=%fused_computation.1 | convolution fusion | flops 405798912 | bytes 4980736 | tf_op jit(solution)/shard_map/thj,shj->hts/dot_general | solution.py:111
  239.7 0.6 fusion.11
  241.0 1.3 fusion.1
  242.2 2.3 copy.50
  244.5 2.3 fusion.9
  247.3 1.2 copy.49
  248.4 0.7 copy.67
  (43 shorter events, 2.2 us)
Async XLA Ops:
  7.2 3.2 %copy-start.11 = (bf16[512,768]{1,0:T(8,128)(2,1)S(1)}, bf16[512,768]{1,0:T(8,128)(2,1)}, u32[]{:S(2)}) copy-start(bf16[512,768]{1,0:T(8,128)(2,1)} %param.7) | copy-start | bytes 2359300
  7.2 131.0 %all-gather.2.cloned.1.call-start = ((), (), s32[]{:S(2)}) async-start(), calls=%async_computation.1 | async-start | bytes 9732096 | tf_op jit(solution)/shard_map/all_gather | solution.py:99
  7.9 2.7 %copy-start.12 = (bf16[512,768]{1,0:T(8,128)(2,1)S(1)}, bf16[512,768]{1,0:T(8,128)(2,1)}, u32[]{:S(2)}) copy-start(bf16[512,768]{1,0:T(8,128)(2,1)} %param.8) | copy-start | bytes 2359300
  7.9 240.5 %reduce-scatter.2.cloned.1.call-start = ((), (), s32[]{:S(2)}) async-start(), calls=%async_computation.2 | async-start | bytes 7077888 | tf_op jit(solution)/shard_map/reduce_scatter | solution.py:104
  10.6 1.4 copy-start
  10.9 98.4 %copy-start.2 = (bf16[512,768]{0,1:T(8,128)(2,1)}, bf16[512,768]{0,1:T(8,128)(2,1)S(1)}, u32[]{:S(2)}) copy-start(bf16[512,768]{0,1:T(8,128)(2,1)S(1)} %copy.36) | copy-start | bytes 2359300
  10.9 97.2 %copy-start.14 = (f32[6,128,128]{2,1,0:T(8,128)S(1)}, f32[6,128,128]{2,1,0:T(8,128)}, u32[]{:S(2)}) copy-start(f32[6,128,128]{2,1,0:T(8,128)} %param.9) | copy-start | bytes 1179652
  108.1 3.8 %copy-start.15 = (pred[512,512]{1,0:T(8,128)(4,1)}, pred[512,512]{1,0:T(8,128)(4,1)S(1)}, u32[]{:S(2)}) copy-start(pred[512,512]{1,0:T(8,128)(4,1)S(1)} %iota_compare_fusion) | copy-start | bytes 786436
  109.3 2.6 %copy-start.3 = (bf16[512,768]{0,1:T(8,128)(2,1)S(1)}, bf16[512,768]{0,1:T(8,128)(2,1)}, u32[]{:S(2)}) copy-start(bf16[512,768]{0,1:T(8,128)(2,1)} %copy-done.2) | copy-start | bytes 2359300
  138.2 9.7 %copy-start.6 = (bf16[512,768]{0,1:T(8,128)(2,1)S(1)}, bf16[512,768]{0,1:T(8,128)(2,1)}, u32[]{:S(2)}) copy-start(bf16[512,768]{0,1:T(8,128)(2,1)} %copy.32) | copy-start | bytes 2359300
  138.2 9.7 %copy-start.8 = (f32[6,512,128]{1,2,0:T(8,128)S(1)}, f32[6,512,128]{1,2,0:T(8,128)}, u32[]{:S(2)}) copy-start(f32[6,512,128]{1,2,0:T(8,128)} %fusion.6) | copy-start | bytes 4718596
  147.9 4.0 %copy-start.16 = (bf16[768,6144]{1,0:T(8,128)(2,1)S(1)}, bf16[768,6144]{1,0:T(8,128)(2,1)}, u32[]{:S(2)}) copy-start(bf16[768,6144]{1,0:T(8,128)(2,1)} %all-gather.2.cloned.1.call-done) | copy-start | bytes 28311556
  233.7 1.8 copy-start.1
  233.7 1.8 copy-start.9
  237.1 2.6 %copy-start.7 = (bf16[512,768]{0,1:T(8,128)(2,1)S(1)}, bf16[512,768]{0,1:T(8,128)(2,1)}, u32[]{:S(2)}) copy-start(bf16[512,768]{0,1:T(8,128)(2,1)} %copy.32) | copy-start | bytes 2359300
  239.7 1.1 copy-start.4
  239.7 1.2 copy-start.10
  244.5 2.4 copy-start.5
  247.3 1.2 copy-start.13
Sparse Core Ops, SparseCore 0:
  10.6 127.5 all-gather.1
  159.2 40.6 reduce-scatter.1

commit v3 on v2

--- a/solution.py
+++ b/solution.py
@@ -29,7 +29,8 @@
     total = value_ref[...]
     partial = jnp.zeros_like(total)
     for k, (partner, bit) in enumerate(partners):
-        sendbuf[k] = total
+        sent = total.astype(jnp.bfloat16)
+        sendbuf[k] = sent
         copy = pltpu.make_async_remote_copy(
             src_ref=sendbuf.at[k],
             dst_ref=recvbuf.at[k],
@@ -40,10 +41,10 @@
         )
         copy.start()
         copy.wait()
-        other = recvbuf[k]
+        other = recvbuf[k].astype(jnp.float32)
         take = (bit == 0) if backward else (bit == 1)
         partial = jnp.where(take, partial + other, partial)
-        total = total + other
+        total = sent.astype(jnp.float32) + other
     partial_ref[...] = partial
     total_ref[...] = total
 
@@ -58,8 +59,8 @@
         in_specs=[pl.BlockSpec(memory_space=pltpu.VMEM)],
         out_specs=(pl.BlockSpec(memory_space=pltpu.VMEM), pl.BlockSpec(memory_space=pltpu.VMEM)),
         scratch_shapes=[
-            pltpu.VMEM((rounds,) + value.shape, jnp.float32),
-            pltpu.VMEM((rounds,) + value.shape, jnp.float32),
+            pltpu.VMEM((rounds,) + value.shape, jnp.bfloat16),
+            pltpu.VMEM((rounds,) + value.shape, jnp.bfloat16),
             pltpu.SemaphoreType.DMA((rounds,)),
             pltpu.SemaphoreType.DMA((rounds,)),
         ],

time: 257 us -> 218 us (0.85)
  Pallas kernels: 168 us -> 90.9 us
  waiting for transfers between devices: 24.7 us -> 63 us
    pallas_call x2, Pallas kernels: 168 us -> 90.9 us  [butterfly(): pl.pallas_call(functools.partial(butterfly_kernel, count, backward), out_...]
    all_gather x1, waiting for transfers between devices: 24 us -> 62.3 us  [shards(): weight_rows = lax.all_gather(out_weight, 'seq', axis=0, tiled=True)]
  transfers between devices with their start and end apart: 2 -> 2, of which waited for: 1 -> 1; matrix products, arithmetic and copies ran while one was open for 10% -> 12% of each run, Pallas kernels for 66% -> 42%
where the time goes in v3:
time: 218 us; the launch traced here: 217 us
  Pallas kernels  90.9 us (42%)
  waiting for transfers between devices  63 us (29%)
  matrix products  35.2 us (16%)
  between operations  14.3 us (7%)
  local copies, waits for them, and re-layouts  10.9 us (5%)
  other arithmetic  2.6 us (1%)
    pallas_call x2, Pallas kernels, butterfly(): pl.pallas_call(functools.partial(butterfly_kernel, count, backward), out_...  90.9 us
    all_gather x1, waiting for transfers between devices, shards(): weight_rows = lax.all_gather(out_weight, 'seq', axis=0, tiled=True)  62.3 us
    unnamed x41, local copies, waits for them, and re-layouts  10.9 us
    dot_general x1, matrix products, shards(): lax.dot_general(out_grad, weight_rows, (((1,), (1,)), ((), ())), preferre...  9.65 us
    dot_general x1, matrix products, shards(): projected = jnp.dot(normed, weight_rows, preferred_element_type=jnp.float32)  7.22 us
  transfers between devices with their start and end apart: 2, of which 1 were waited for; matrix products, arithmetic and copies ran while one was open for 12% of the time, Pallas kernels for 42%

profile of v3, /device:TPU:2, one launch (start us, length us, event | category | flops | bytes accessed | tf_op | source)
XLA Modules:
  0.0 217.0 jit_solution(18279738618633768261)
XLA Ops:
  7.2 0.7 all-gather.2.cloned.1.call-update
  8.0 2.4 %copy.32 = bf16[512,768]{0,1:T(8,128)(2,1)} copy(bf16[512,768]{1,0:T(8,128)(2,1)} %param.6) | data formatting | bytes 1572864 | tf_op args[0]
  10.9 1.1 fusion.7.value_ref
  12.0 49.9 %shard_map.101 = (f32[6,128,128]{2,1,0:T(8,128)}, f32[6,128,128]{2,1,0:T(8,128)}) custom-call(f32[6,128,128]{2,1,0:T(8,128)} %fusion.7.value_ref), custom_call_target="tpu_custom_call" | custom-call | tf_op jit(solution)/shard_map/pallas_call | solution.py:56
  62.1 1.1 add_convert_fusion.1
  63.3 2.5 %select_convert_fusion.1 = bf16[6,512,512]{2,1,0:T(8,128)(2,1)S(1)} fusion(pred[512,512]{1,0:T(8,128)(4,1)S(1)} %iota_compare_fusion, bf16[512,6,128]{0,2,1:T(8,128)(2,1)} %bitcast.62, bf16[512,6,128]{0,2,1:T(8,128)(2,1)} %bitcast.55), kind=kOutput, calls=%fused_computation.2 | convolution fusion | flops 405798912 | bytes 4980736 | tf_op jit(solution)/shard_map/thi,shi->hts/dot_general | solution.py:91
  65.8 2.3 %fusion.6 = f32[6,512,128]{1,2,0:T(8,128)} fusion(bf16[6,512,512]{2,1,0:T(8,128)(2,1)S(1)} %select_convert_fusion.1, bf16[512,6,128]{0,2,1:T(8,128)(2,1)S(1)} %bitcast.60), kind=kOutput, calls=%fused_computation.22 | convolution fusion | flops 402653184 | bytes 5505024 | tf_op jit(solution)/shard_map/hts,shj->thj/dot_general | solution.py:93
  68.1 62.3 %all-gather.2.cloned.1.call-done = bf16[768,6144]{1,0:T(8,128)(2,1)} async-done(((bf16[24,6144]{1,0:T(8,128)(2,1)}), bf16[768,6144]{1,0:T(8,128)(2,1)}) %all-gather.2.cloned.1.call-update) | async-done | bytes 9437200 | tf_op jit(solution)/shard_map/all_gather | solution.py:100
  130.4 9.7 %fusion.8 = f32[512,768]{0,1:T(8,128)S(1)} fusion(bf16[512,6144]{1,0:T(8,128)(2,1)} %param.11, bf16[768,6144]{1,0:T(8,128)(2,1)} %all-gather.2.cloned.1.call-done), kind=kOutput, calls=%fused_computation.24 | convolution fusion | flops 4831838208 | bytes 17301504 | tf_op jit(solution)/shard_map/dot_general | solution.py:102
  140.1 0.6 multiply_reduce_fusion
  140.7 1.4 fusion
  142.1 2.0 copy-done.16
  144.1 7.2 %convolution_convert_fusion = bf16[512,6144]{1,0:T(8,128)(2,1)} fusion(bf16[512,768]{0,1:T(8,128)(2,1)S(1)} %bitcast.71, bf16[768,6144]{1,0:T(8,128)(2,1)S(1)} %copy-done.16), kind=kOutput, calls=%fused_computation | convolution fusion | flops 4834983936 | bytes 16515072 | tf_op jit(solution)/shard_map/dot_general | solution.py:101
  151.3 2.5 %convolution_bitcast_fusion.value_ref = f32[6,128,128]{2,1,0:T(8,128)} fusion(bf16[512,6,128]{0,2,1:T(8,128)(2,1)} %get-tuple-element.23, bf16[512,6,128]{0,2,1:T(8,128)(2,1)} %bitcast.63), kind=kOutput, calls=%fused_computation.14 | convolution fusion | flops 100663296 | bytes 1966080 | tf_op jit(solution)/shard_map/thi,thj->hij/dot_general | solution.py:114
  153.8 40.9 %shard_map.102 = (f32[6,128,128]{2,1,0:T(8,128)}, f32[6,128,128]{2,1,0:T(8,128)}) custom-call(f32[6,128,128]{2,1,0:T(8,128)} %convolution_bitcast_fusion.value_ref), custom_call_target="tpu_custom_call" | custom-call | tf_op jit(solution)/shard_map/pallas_call | solution.py:56
  194.7 1.8 fusion.10
  197.0 1.2 copy.51
  198.2 2.6 %select_convert_fusion = bf16[6,512,512]{2,1,0:T(8,128)(2,1)S(1)} fusion(pred[512,512]{1,0:T(8,128)(4,1)} %copy-done.15, bf16[512,6,128]{0,2,1:T(8,128)(2,1)} %get-tuple-element.23, bf16[512,6,128]{0,2,1:T(8,128)(2,1)} %bitcast.59), kind=kOutput, calls=%fused_computation.1 | convolution fusion | flops 405798912 | bytes 4980736 | tf_op jit(solution)/shard_map/thj,shj->hts/dot_general | solution.py:112
  200.8 0.6 fusion.11
  202.0 1.3 fusion.1
  203.3 2.3 %copy.50 = bf16[512,768]{1,0:T(8,128)(2,1)} copy(bf16[512,768]{0,1:T(8,128)(2,1)} %bitcast.68) | data formatting | bytes 1572864
  205.6 2.3 %fusion.9 = f32[6,512,128]{1,2,0:T(8,128)S(1)} fusion(bf16[6,512,512]{2,1,0:T(8,128)(2,1)S(1)} %select_convert_fusion, bf16[512,6,128]{0,2,1:T(8,128)(2,1)} %bitcast.56), kind=kOutput, calls=%fused_computation.25 | convolution fusion | flops 402653184 | bytes 5505024 | tf_op jit(solution)/shard_map/hts,shi->thi/dot_general | solution.py:117
  208.3 1.2 copy.49
  209.4 0.7 copy.67
  (43 shorter events, 2.2 us)
Async XLA Ops:
  7.2 3.2 %copy-start.11 = (bf16[512,768]{1,0:T(8,128)(2,1)S(1)}, bf16[512,768]{1,0:T(8,128)(2,1)}, u32[]{:S(2)}) copy-start(bf16[512,768]{1,0:T(8,128)(2,1)} %param.7) | copy-start | bytes 2359300
  7.2 123.3 %all-gather.2.cloned.1.call-start = ((), (), s32[]{:S(2)}) async-start(), calls=%async_computation.1 | async-start | bytes 9732096 | tf_op jit(solution)/shard_map/all_gather | solution.py:100
  7.9 2.7 %copy-start.12 = (bf16[512,768]{1,0:T(8,128)(2,1)S(1)}, bf16[512,768]{1,0:T(8,128)(2,1)}, u32[]{:S(2)}) copy-start(bf16[512,768]{1,0:T(8,128)(2,1)} %param.8) | copy-start | bytes 2359300
  7.9 201.5 %reduce-scatter.2.cloned.1.call-start = ((), (), s32[]{:S(2)}) async-start(), calls=%async_computation.2 | async-start | bytes 7077888 | tf_op jit(solution)/shard_map/reduce_scatter | solution.py:105
  10.6 1.4 copy-start
  10.9 52.3 %copy-start.2 = (bf16[512,768]{0,1:T(8,128)(2,1)}, bf16[512,768]{0,1:T(8,128)(2,1)S(1)}, u32[]{:S(2)}) copy-start(bf16[512,768]{0,1:T(8,128)(2,1)S(1)} %copy.36) | copy-start | bytes 2359300
  10.9 51.2 %copy-start.14 = (f32[6,128,128]{2,1,0:T(8,128)S(1)}, f32[6,128,128]{2,1,0:T(8,128)}, u32[]{:S(2)}) copy-start(f32[6,128,128]{2,1,0:T(8,128)} %param.9) | copy-start | bytes 1179652
  62.1 3.7 %copy-start.15 = (pred[512,512]{1,0:T(8,128)(4,1)}, pred[512,512]{1,0:T(8,128)(4,1)S(1)}, u32[]{:S(2)}) copy-start(pred[512,512]{1,0:T(8,128)(4,1)S(1)} %iota_compare_fusion) | copy-start | bytes 786436
  63.3 2.6 %copy-start.3 = (bf16[512,768]{0,1:T(8,128)(2,1)S(1)}, bf16[512,768]{0,1:T(8,128)(2,1)}, u32[]{:S(2)}) copy-start(bf16[512,768]{0,1:T(8,128)(2,1)} %copy-done.2) | copy-start | bytes 2359300
  130.4 9.7 %copy-start.6 = (bf16[512,768]{0,1:T(8,128)(2,1)S(1)}, bf16[512,768]{0,1:T(8,128)(2,1)}, u32[]{:S(2)}) copy-start(bf16[512,768]{0,1:T(8,128)(2,1)} %copy.32) | copy-start | bytes 2359300
  130.4 9.7 %copy-start.8 = (f32[6,512,128]{1,2,0:T(8,128)S(1)}, f32[6,512,128]{1,2,0:T(8,128)}, u32[]{:S(2)}) copy-start(f32[6,512,128]{1,2,0:T(8,128)} %fusion.6) | copy-start | bytes 4718596
  140.1 4.0 %copy-start.16 = (bf16[768,6144]{1,0:T(8,128)(2,1)S(1)}, bf16[768,6144]{1,0:T(8,128)(2,1)}, u32[]{:S(2)}) copy-start(bf16[768,6144]{1,0:T(8,128)(2,1)} %all-gather.2.cloned.1.call-done) | copy-start | bytes 28311556
  194.7 1.8 copy-start.1
  194.7 1.8 copy-start.9
  198.1 2.6 %copy-start.7 = (bf16[512,768]{0,1:T(8,128)(2,1)S(1)}, bf16[512,768]{0,1:T(8,128)(2,1)}, u32[]{:S(2)}) copy-start(bf16[512,768]{0,1:T(8,128)(2,1)} %copy.32) | copy-start | bytes 2359300
  200.8 1.1 copy-start.4
  200.8 1.2 copy-start.10
  205.6 2.3 %copy-start.5 = (bf16[512,6,128]{0,2,1:T(8,128)(2,1)S(1)}, bf16[512,6,128]{0,2,1:T(8,128)(2,1)}, u32[]{:S(2)}) copy-start(bf16[512,6,128]{0,2,1:T(8,128)(2,1)} %get-tuple-element.23) | copy-start | bytes 2359300
  208.3 1.2 copy-start.13
Sparse Core Ops, SparseCore 0:
  10.6 119.8 all-gather.1
  151.4 39.9 reduce-scatter.1

commit v4 on v3

--- a/solution.py
+++ b/solution.py
@@ -70,6 +70,128 @@
     )(value.astype(jnp.float32))
 
 
+def gather_kernel(ny, ca, value_ref, w_ref, rows_ref, partial_ref, sendbuf, recvbuf, send_sem, recv_sem, bf_send, bf_recv, local_sem):
+    me = lax.axis_index("seq")
+    head = lax.axis_index("head")
+    count = lax.axis_size("seq")
+    nz = count // ny
+    y = me % ny
+    z = me // ny
+    piece, cols = w_ref.shape
+    A = pl.ds(0, ca)
+    B = pl.ds(ca, cols - ca)
+    hy, hz = ny // 2, nz // 2
+    hb = (cols - ca) // 2
+    B1 = pl.ds(ca, hb)
+    B2 = pl.ds(ca + hb, cols - ca - hb)
+
+    def zz(k):
+        return (z + nz + k) % nz
+
+    def yy(k):
+        return (y + ny + k) % ny
+
+    def dev(zi, yi):
+        return (zi * ny + yi, head)
+
+    rounds = count.bit_length() - 1
+    partners = []
+    for k in range(rounds):
+        step = 1 << k
+        bit = (me // step) % 2
+        partners.append((me + step - 2 * step * bit, bit))
+    ring = [dev(z, yy(1)), dev(z, yy(-1)), dev(zz(1), y), dev(zz(-1), y)]
+    barrier = pltpu.get_barrier_semaphore()
+    for target in ring:
+        pl.semaphore_signal(barrier, inc=1, device_id=target, device_id_type=MESH)
+    for partner, _ in partners:
+        pl.semaphore_signal(barrier, inc=1, device_id=(partner, head), device_id_type=MESH)
+    pl.semaphore_wait(barrier, len(ring) + rounds)
+
+    local = pltpu.make_async_copy(w_ref, rows_ref.at[z, y], local_sem)
+    local.start()
+    R = rows_ref
+    yr, yl, zr, zl = dev(z, yy(1)), dev(z, yy(-1)), dev(zz(1), y), dev(zz(-1), y)
+    ticks = [
+        [(w_ref.at[:, A], R.at[z, y, :, A], yr), (w_ref.at[:, A], R.at[z, y, :, A], yl),
+         (w_ref.at[:, B], R.at[z, y, :, B], zr), (w_ref.at[:, B], R.at[z, y, :, B], zl)],
+        [(R.at[z, yy(-1), :, A], R.at[z, yy(-1), :, A], yr),
+         (R.at[zz(-1), y, :, B], R.at[zz(-1), y, :, B], zr), (R.at[zz(1), y, :, B], R.at[zz(1), y, :, B], zl)],
+        [(R.at[z, :, :, A], R.at[z, :, :, A], zr), (R.at[z, :, :, A], R.at[z, :, :, A], zl),
+         (R.at[zz(-2), y, :, B], R.at[zz(-2), y, :, B], zr), (R.at[zz(2), y, :, B], R.at[zz(2), y, :, B], zl)],
+        [(R.at[zz(-1), :, :, A], R.at[zz(-1), :, :, A], zr), (R.at[zz(1), :, :, A], R.at[zz(1), :, :, A], zl),
+         (R.at[zz(-3), y, :, B1], R.at[zz(-3), y, :, B1], zr),
+         (R.at[zz(3), y, :, B2], R.at[zz(3), y, :, B2], zl)],
+        [(R.at[zz(-2), :, :, A], R.at[zz(-2), :, :, A], zr), (R.at[zz(2), :, :, A], R.at[zz(2), :, :, A], zl),
+         (R.at[:, y, :, B], R.at[:, y, :, B], yr), (R.at[:, y, :, B], R.at[:, y, :, B], yl)],
+        [(R.at[zz(-3), pl.ds(0, hy), :, A], R.at[zz(-3), pl.ds(0, hy), :, A], zr),
+         (R.at[zz(3), pl.ds(hy, ny - hy), :, A], R.at[zz(3), pl.ds(hy, ny - hy), :, A], zl),
+         (R.at[pl.ds(0, hz), yy(-1), :, B], R.at[pl.ds(0, hz), yy(-1), :, B], yr),
+         (R.at[pl.ds(hz, nz - hz), yy(1), :, B], R.at[pl.ds(hz, nz - hz), yy(1), :, B], yl)],
+    ]
+    total = value_ref[...]
+    partial = jnp.zeros_like(total)
+    n = 0
+    for t, moves in enumerate(ticks):
+        if t == 2:
+            local.wait()
+        started = []
+        for src, dst, target in moves:
+            copy = pltpu.make_async_remote_copy(
+                src_ref=src, dst_ref=dst, send_sem=send_sem.at[n], recv_sem=recv_sem.at[n],
+                device_id=target, device_id_type=MESH,
+            )
+            copy.start()
+            started.append(copy)
+            n += 1
+        scan = None
+        if t < rounds:
+            partner, bit = partners[t]
+            sent = total.astype(jnp.bfloat16)
+            sendbuf[t] = sent
+            scan = pltpu.make_async_remote_copy(
+                src_ref=sendbuf.at[t], dst_ref=recvbuf.at[t], send_sem=bf_send.at[t],
+                recv_sem=bf_recv.at[t], device_id=(partner, head), device_id_type=MESH,
+            )
+            scan.start()
+        for copy in started:
+            copy.wait()
+        if scan is not None:
+            scan.wait()
+            other = recvbuf[t].astype(jnp.float32)
+            partial = jnp.where(bit == 1, partial + other, partial)
+            total = sent.astype(jnp.float32) + other
+    partial_ref[...] = partial
+
+
+def gather_and_scan(value, weight):
+    count = lax.axis_size("seq")
+    ny = 4
+    piece, cols = weight.shape
+    rounds = count.bit_length() - 1
+    ca = (cols * 2 // 3) // 128 * 128
+    n_copies = 23
+    return pl.pallas_call(
+        functools.partial(gather_kernel, ny, ca),
+        out_shape=(
+            jax.ShapeDtypeStruct((count // ny, ny, piece, cols), weight.dtype),
+            jax.ShapeDtypeStruct(value.shape, jnp.float32),
+        ),
+        in_specs=[pl.BlockSpec(memory_space=pltpu.VMEM), pl.BlockSpec(memory_space=pl.ANY)],
+        out_specs=(pl.BlockSpec(memory_space=pl.ANY), pl.BlockSpec(memory_space=pltpu.VMEM)),
+        scratch_shapes=[
+            pltpu.VMEM((rounds,) + value.shape, jnp.bfloat16),
+            pltpu.VMEM((rounds,) + value.shape, jnp.bfloat16),
+            pltpu.SemaphoreType.DMA((n_copies,)),
+            pltpu.SemaphoreType.DMA((n_copies,)),
+            pltpu.SemaphoreType.DMA((rounds,)),
+            pltpu.SemaphoreType.DMA((rounds,)),
+            pltpu.SemaphoreType.DMA(()),
+        ],
+        compiler_params=pltpu.CompilerParams(collective_id=2, has_side_effects=True),
+    )(value.astype(jnp.float32), weight)
+
+
 def normalize(attended):
     return attended * lax.rsqrt(jnp.mean(attended * attended, axis=-1, keepdims=True) + EPS)
 
@@ -83,7 +205,7 @@
     key_rows = key.reshape(tok_rows, heads_here, head_dim)
     val_rows = value.reshape(tok_rows, heads_here, head_dim)
     local_state = jnp.einsum("thi,thj->hij", key_rows, val_rows, preferred_element_type=jnp.float32)
-    earlier, _ = butterfly(local_state, "seq", False)
+    gathered, earlier = gather_and_scan(local_state, out_weight)
     state_half = (init_state + earlier).astype(jnp.bfloat16)
     row_index = lax.broadcasted_iota(jnp.int32, (tok_rows, tok_rows), 0)
     col_index = lax.broadcasted_iota(jnp.int32, (tok_rows, tok_rows), 1)
@@ -97,7 +219,7 @@
         "thi,hij->thj", queries, state_half, preferred_element_type=jnp.float32
     )
     normed = normalize(attended).astype(jnp.bfloat16).reshape(tok_rows, width)
-    weight_rows = lax.all_gather(out_weight, "seq", axis=0, tiled=True)
+    weight_rows = gathered.reshape(-1, out_weight.shape[1])
     projected = jnp.dot(normed, weight_rows, preferred_element_type=jnp.float32)
     grad_normed = lax.dot_general(
         out_grad, weight_rows, (((1,), (1,)), ((), ())), preferred_element_type=jnp.float32

time: 218 us -> 220 us (level)
  Pallas kernels: 90.9 us -> 157 us
  waiting for transfers between devices: 63 us -> 0.02 us
    pallas_call x0 -> x1, Pallas kernels: none -> 120 us  [gather_and_scan(): pl.pallas_call(functools.partial(gather_kernel, ny, ca), out_shape=(jax.S...]
    all_gather x1 -> x0, waiting for transfers between devices: 62.3 us -> none  [shards(): weight_rows = lax.all_gather(out_weight, 'seq', axis=0, tiled=True)]
    pallas_call x2 -> x1, Pallas kernels: 90.9 us -> 36.5 us  [butterfly(): pl.pallas_call(functools.partial(butterfly_kernel, count, backward), out_...]
    unnamed x41 -> x45, local copies, waits for them, and re-layouts: 10.9 us -> 11.5 us
  transfers between devices with their start and end apart: 2 -> 1, of which waited for: 1 -> 0; matrix products, arithmetic and copies ran while one was open for 12% -> 7% of each run, Pallas kernels for 42% -> 17%
where the time goes in v4:
time: 220 us; the launch traced here: 219 us
  Pallas kernels  157 us (71%)
  matrix products  35.2 us (16%)
  between operations  14.4 us (7%)
  local copies, waits for them, and re-layouts  11.5 us (5%)
    pallas_call x1, Pallas kernels, gather_and_scan(): pl.pallas_call(functools.partial(gather_kernel, ny, ca), out_shape=(jax.S...  120 us
    pallas_call x1, Pallas kernels, butterfly(): pl.pallas_call(functools.partial(butterfly_kernel, count, backward), out_...  36.5 us
    unnamed x45, local copies, waits for them, and re-layouts  11.5 us
    dot_general x1, matrix products, shards(): lax.dot_general(out_grad, weight_rows, (((1,), (1,)), ((), ())), preferre...  9.83 us
    dot_general x1, matrix products, shards(): projected = jnp.dot(normed, weight_rows, preferred_element_type=jnp.float32)  7.26 us
  transfers between devices with their start and end apart: 1, of which 0 were waited for; matrix products, arithmetic and copies ran while one was open for 7% of the time, Pallas kernels for 17%

profile of v4, /device:TPU:2, one launch (start us, length us, event | category | flops | bytes accessed | tf_op | source)
XLA Modules:
  0.0 219.2 jit_solution(9309947030592049634)
XLA Ops:
  7.3 2.5 %copy.31 = bf16[512,768]{0,1:T(8,128)(2,1)} copy(bf16[512,768]{1,0:T(8,128)(2,1)} %param.6) | data formatting | bytes 1572864 | tf_op args[0]
  10.4 1.1 fusion.7.value_ref
  11.5 0.4 copy-done.6
  12.0 2.3 %select_convert_fusion.1 = bf16[6,512,512]{2,1,0:T(8,128)(2,1)S(1)} fusion(pred[512,512]{1,0:T(8,128)(4,1)S(1)} %iota_compare_fusion, bf16[512,6,128]{0,2,1:T(8,128)(2,1)S(1)} %bitcast.66, bf16[512,6,128]{0,2,1:T(8,128)(2,1)} %bitcast.58), kind=kOutput, calls=%fused_computation.2 | convolution fusion | flops 405798912 | bytes 4980736 | tf_op jit(solution)/shard_map/thi,shi->hts/dot_general | solution.py:213
  14.3 2.3 %fusion.6 = f32[6,512,128]{1,2,0:T(8,128)} fusion(bf16[6,512,512]{2,1,0:T(8,128)(2,1)S(1)} %select_convert_fusion.1, bf16[512,6,128]{0,2,1:T(8,128)(2,1)S(1)} %bitcast.63), kind=kOutput, calls=%fused_computation.22 | convolution fusion | flops 402653184 | bytes 5505024 | tf_op jit(solution)/shard_map/hts,shj->thj/dot_general | solution.py:215
  16.6 120.0 %shard_map.101 = (bf16[8,4,24,6144]{3,2,1,0:T(8,128)(2,1)}, f32[6,128,128]{2,1,0:T(8,128)}) custom-call(f32[6,128,128]{2,1,0:T(8,128)} %fusion.7.value_ref, bf16[24,6144]{1,0:T(8,128)(2,1)} %w_ref.1), custom_call_target="tpu_custom_call" | custom-call | tf_op jit(solution)/shard_map/pallas_call | solution.py:174
  136.7 9.8 %fusion.8 = f32[768,512]{1,0:T(8,128)S(1)} fusion(bf16[768,6144]{1,0:T(8,128)(2,1)} %bitcast.75, bf16[512,6144]{1,0:T(8,128)(2,1)} %param.11), kind=kOutput, calls=%fused_computation.24 | convolution fusion | flops 4831838208 | bytes 17301504 | tf_op jit(solution)/shard_map/dot_general | solution.py:224
  146.6 0.6 multiply_reduce_fusion
  147.2 1.4 fusion
  148.6 2.0 copy-done.18
  150.6 7.3 %convolution_convert_fusion = bf16[512,6144]{1,0:T(8,128)(2,1)} fusion(bf16[512,768]{0,1:T(8,128)(2,1)S(1)} %bitcast.74, bf16[768,6144]{1,0:T(8,128)(2,1)S(1)} %bitcast.76), kind=kOutput, calls=%fused_computation | convolution fusion | flops 4834983936 | bytes 16515072 | tf_op jit(solution)/shard_map/dot_general | solution.py:223
  157.9 2.5 %convolution_bitcast_fusion.value_ref = f32[6,128,128]{2,1,0:T(8,128)} fusion(bf16[512,6,128]{0,2,1:T(8,128)(2,1)} %get-tuple-element.25, bf16[512,6,128]{0,2,1:T(8,128)(2,1)} %bitcast.65), kind=kOutput, calls=%fused_computation.14 | convolution fusion | flops 100663296 | bytes 1966080 | tf_op jit(solution)/shard_map/thi,thj->hij/dot_general | solution.py:236
  160.3 36.5 %shard_map.102 = (f32[6,128,128]{2,1,0:T(8,128)}, f32[6,128,128]{2,1,0:T(8,128)}) custom-call(f32[6,128,128]{2,1,0:T(8,128)} %convolution_bitcast_fusion.value_ref), custom_call_target="tpu_custom_call" | custom-call | tf_op jit(solution)/shard_map/pallas_call | solution.py:56
  196.9 1.8 fusion.10
  198.7 0.4 add_convert_fusion
  199.2 1.2 copy.49
  200.3 2.6 %select_convert_fusion = bf16[6,512,512]{2,1,0:T(8,128)(2,1)S(1)} fusion(pred[512,512]{1,0:T(8,128)(4,1)} %copy-done.17, bf16[512,6,128]{0,2,1:T(8,128)(2,1)} %get-tuple-element.25, bf16[512,6,128]{0,2,1:T(8,128)(2,1)} %bitcast.62), kind=kOutput, calls=%fused_computation.1 | convolution fusion | flops 405798912 | bytes 4980736 | tf_op jit(solution)/shard_map/thj,shj->hts/dot_general | solution.py:234
  202.9 0.6 fusion.11
  203.5 0.5 copy-done.4
  204.2 1.3 fusion.1
  205.4 2.3 %copy.48 = bf16[512,768]{1,0:T(8,128)(2,1)} copy(bf16[512,768]{0,1:T(8,128)(2,1)} %bitcast.71) | data formatting | bytes 1572864
  207.7 2.4 %fusion.9 = f32[6,512,128]{1,2,0:T(8,128)S(1)} fusion(bf16[6,512,512]{2,1,0:T(8,128)(2,1)S(1)} %select_convert_fusion, bf16[512,6,128]{0,2,1:T(8,128)(2,1)} %bitcast.59), kind=kOutput, calls=%fused_computation.25 | convolution fusion | flops 402653184 | bytes 5505024 | tf_op jit(solution)/shard_map/hts,shi->thi/dot_general | solution.py:239
  210.5 1.2 copy.47
  211.6 0.7 copy.64
  (44 shorter events, 1.3 us)
Async XLA Ops:
  7.2 2.6 %copy-start.12 = (bf16[512,768]{1,0:T(8,128)(2,1)S(1)}, bf16[512,768]{1,0:T(8,128)(2,1)}, u32[]{:S(2)}) copy-start(bf16[512,768]{1,0:T(8,128)(2,1)} %param.7) | copy-start | bytes 2359300
  7.2 204.4 %reduce-scatter.2.cloned.1.call-start = ((), (), s32[]{:S(2)}) async-start(), calls=%async_computation.1 | async-start | bytes 7077888 | tf_op jit(solution)/shard_map/reduce_scatter | solution.py:227
  7.3 4.2 %copy-start.17 = (pred[512,512]{1,0:T(8,128)(4,1)}, pred[512,512]{1,0:T(8,128)(4,1)S(1)}, u32[]{:S(2)}) copy-start(pred[512,512]{1,0:T(8,128)(4,1)S(1)} %iota_compare_fusion) | copy-start | bytes 786436
  7.3 2.8 %copy-start.13 = (bf16[512,768]{1,0:T(8,128)(2,1)S(1)}, bf16[512,768]{1,0:T(8,128)(2,1)}, u32[]{:S(2)}) copy-start(bf16[512,768]{1,0:T(8,128)(2,1)} %param.8) | copy-start | bytes 2359300
  10.1 1.4 copy-start
  10.4 1.1 copy-start.2
  10.4 1.6 copy-start.6
  12.0 2.3 %copy-start.3 = (bf16[512,768]{0,1:T(8,128)(2,1)S(1)}, bf16[512,768]{0,1:T(8,128)(2,1)}, u32[]{:S(2)}) copy-start(bf16[512,768]{0,1:T(8,128)(2,1)} %copy-done.2) | copy-start | bytes 2359300
  136.6 9.9 %copy-start.15 = (f32[6,128,128]{2,1,0:T(8,128)S(1)}, f32[6,128,128]{2,1,0:T(8,128)}, u32[]{:S(2)}) copy-start(f32[6,128,128]{2,1,0:T(8,128)} %param.9) | copy-start | bytes 1179652
  136.7 9.9 %copy-start.16 = (f32[6,128,128]{2,1,0:T(8,128)S(1)}, f32[6,128,128]{2,1,0:T(8,128)}, u32[]{:S(2)}) copy-start(f32[6,128,128]{2,1,0:T(8,128)} %get-tuple-element.9) | copy-start | bytes 1179652
  136.7 9.9 %copy-start.7 = (bf16[512,768]{0,1:T(8,128)(2,1)S(1)}, bf16[512,768]{0,1:T(8,128)(2,1)}, u32[]{:S(2)}) copy-start(bf16[512,768]{0,1:T(8,128)(2,1)} %copy.31) | copy-start | bytes 2359300
  136.7 9.9 %copy-start.9 = (f32[6,512,128]{1,2,0:T(8,128)S(1)}, f32[6,512,128]{1,2,0:T(8,128)}, u32[]{:S(2)}) copy-start(f32[6,512,128]{1,2,0:T(8,128)} %fusion.6) | copy-start | bytes 4718596
  146.6 4.0 %copy-start.18 = (bf16[8,4,24,6144]{3,2,1,0:T(8,128)(2,1)S(1)}, bf16[8,4,24,6144]{3,2,1,0:T(8,128)(2,1)}, u32[]{:S(2)}) copy-start(bf16[8,4,24,6144]{3,2,1,0:T(8,128)(2,1)} %get-tuple-element.10) | copy-start | bytes 28311556
  196.9 1.8 copy-start.1
  196.9 1.8 copy-start.10
  200.3 2.6 %copy-start.8 = (bf16[512,768]{0,1:T(8,128)(2,1)S(1)}, bf16[512,768]{0,1:T(8,128)(2,1)}, u32[]{:S(2)}) copy-start(bf16[512,768]{0,1:T(8,128)(2,1)} %copy.31) | copy-start | bytes 2359300
  202.9 1.1 copy-start.4
  202.9 1.2 copy-start.11
  207.7 2.4 %copy-start.5 = (bf16[512,6,128]{0,2,1:T(8,128)(2,1)S(1)}, bf16[512,6,128]{0,2,1:T(8,128)(2,1)}, u32[]{:S(2)}) copy-start(bf16[512,6,128]{0,2,1:T(8,128)(2,1)} %get-tuple-element.25) | copy-start | bytes 2359300
  210.5 1.2 copy-start.14
Sparse Core Ops, SparseCore 0:
  158.0 40.0 reduce-scatter.1

commit v5 on v4

--- a/solution.py
+++ b/solution.py
@@ -205,7 +205,9 @@
     key_rows = key.reshape(tok_rows, heads_here, head_dim)
     val_rows = value.reshape(tok_rows, heads_here, head_dim)
     local_state = jnp.einsum("thi,thj->hij", key_rows, val_rows, preferred_element_type=jnp.float32)
-    gathered, earlier = gather_and_scan(local_state, out_weight)
+    half = out_weight.shape[1] // 2
+    gathered, earlier = gather_and_scan(local_state, out_weight[:, :half])
+    other_half = lax.all_gather(out_weight[:, half:], "seq", axis=0, tiled=True)
     state_half = (init_state + earlier).astype(jnp.bfloat16)
     row_index = lax.broadcasted_iota(jnp.int32, (tok_rows, tok_rows), 0)
     col_index = lax.broadcasted_iota(jnp.int32, (tok_rows, tok_rows), 1)
@@ -219,7 +221,7 @@
         "thi,hij->thj", queries, state_half, preferred_element_type=jnp.float32
     )
     normed = normalize(attended).astype(jnp.bfloat16).reshape(tok_rows, width)
-    weight_rows = gathered.reshape(-1, out_weight.shape[1])
+    weight_rows = jnp.concatenate([gathered.reshape(-1, half), other_half], axis=1)
     projected = jnp.dot(normed, weight_rows, preferred_element_type=jnp.float32)
     grad_normed = lax.dot_general(
         out_grad, weight_rows, (((1,), (1,)), ((), ())), preferred_element_type=jnp.float32

time: 220 us -> 218 us (level); the launches traced: 219 us -> 214 us
  Pallas kernels: 157 us -> 146 us
  matrix products: 35.2 us -> 38.3 us
    pallas_call x1, Pallas kernels: 120 us -> 107 us  [gather_and_scan(): pl.pallas_call(functools.partial(gather_kernel, ny, ca), out_shape=(jax.S...]
    dot_general x1, matrix products: 7.26 us -> 10.1 us  [shards(): projected = jnp.dot(normed, weight_rows, preferred_element_type=jnp.float32)]
    unnamed x45 -> x41, local copies, waits for them, and re-layouts: 11.5 us -> 10.8 us
  transfers between devices with their start and end apart: 1 -> 2, of which waited for: 0 -> 0; matrix products, arithmetic and copies ran while one was open for 7% -> 13% of each run, Pallas kernels for 17% -> 68%
where the time goes in v5:
time: 218 us; the launch traced here: 214 us
  Pallas kernels  146 us (67%)
  matrix products  38.3 us (18%)
  between operations  14.3 us (7%)
  local copies, waits for them, and re-layouts  12.6 us (6%)
  other arithmetic  2.65 us (1%)
    pallas_call x1, Pallas kernels, gather_and_scan(): pl.pallas_call(functools.partial(gather_kernel, ny, ca), out_shape=(jax.S...  107 us
    pallas_call x1, Pallas kernels, butterfly(): pl.pallas_call(functools.partial(butterfly_kernel, count, backward), out_...  38.3 us
    unnamed x41, local copies, waits for them, and re-layouts  10.8 us
    dot_general x1, matrix products, shards(): projected = jnp.dot(normed, weight_rows, preferred_element_type=jnp.float32)  10.1 us
    dot_general x1, matrix products, shards(): lax.dot_general(out_grad, weight_rows, (((1,), (1,)), ((), ())), preferre...  9.83 us
  transfers between devices with their start and end apart: 2, of which 0 were waited for; matrix products, arithmetic and copies ran while one was open for 13% of the time, Pallas kernels for 68%

profile of v5, /device:TPU:2, one launch (start us, length us, event | category | flops | bytes accessed | tf_op | source)
XLA Modules:
  0.0 213.7 jit_solution(10543624257109868323)
XLA Ops:
  7.2 1.8 fusion.9
  9.1 1.4 copy.32
  10.5 1.7 copy.35
  12.2 1.2 copy.31
  13.4 1.1 fusion.11.value_ref
  14.5 107.4 %shard_map.101 = (bf16[8,4,24,3072]{3,2,1,0:T(8,128)(2,1)}, f32[6,128,128]{2,1,0:T(8,128)}) custom-call(f32[6,128,128]{2,1,0:T(8,128)} %fusion.11.value_ref, bf16[24,3072]{1,0:T(8,128)(2,1)} %get-tuple-element.28.w_ref), custom_call_target="tpu_custom_call" | custom-call | tf_op jit(solution)/shard_map/pallas_call | solution.py:174
  122.0 1.1 add_convert_fusion.1
  123.2 2.5 %select_convert_fusion.1 = bf16[6,512,512]{2,1,0:T(8,128)(2,1)S(1)} fusion(pred[512,512]{1,0:T(8,128)(4,1)S(1)} %iota_compare_fusion, bf16[512,6,128]{0,2,1:T(8,128)(2,1)} %bitcast.63, bf16[512,6,128]{0,2,1:T(8,128)(2,1)} %bitcast.56), kind=kOutput, calls=%fused_computation.3 | convolution fusion | flops 405798912 | bytes 4980736 | tf_op jit(solution)/shard_map/thi,shi->hts/dot_general | solution.py:215
  125.8 2.4 %fusion.10 = f32[6,512,128]{1,2,0:T(8,128)} fusion(bf16[6,512,512]{2,1,0:T(8,128)(2,1)S(1)} %select_convert_fusion.1, bf16[512,6,128]{0,2,1:T(8,128)(2,1)S(1)} %bitcast.61), kind=kOutput, calls=%fused_computation.27 | convolution fusion | flops 402653184 | bytes 5505024 | tf_op jit(solution)/shard_map/hts,shj->thj/dot_general | solution.py:217
  128.1 9.8 %fusion = f32[768,512]{1,0:T(8,128)S(1)} fusion(bf16[512,6144]{1,0:T(8,128)(2,1)} %param.11, bf16[768,3072]{1,0:T(8,128)(2,1)} %all-gather.2.cloned.1.call-done, bf16[768,3072]{1,0:T(8,128)(2,1)} %bitcast.75), kind=kOutput, calls=%fused_computation.4 | convolution fusion | flops 4850712576 | bytes 17301504 | tf_op jit(solution)/shard_map/dot_general | solution.py:226
  138.0 0.6 multiply_reduce_fusion
  138.6 1.4 fusion.1
  140.6 10.1 %convolution_convert_fusion = bf16[512,6144]{1,0:T(8,128)(2,1)} fusion(bf16[512,768]{0,1:T(8,128)(2,1)S(1)} %bitcast.72, bf16[768,3072]{1,0:T(8,128)(2,1)S(1)} %bitcast.74, bf16[768,3072]{1,0:T(8,128)(2,1)} %bitcast.76), kind=kOutput, calls=%fused_computation.1 | convolution fusion | flops 4853858304 | bytes 16515072 | tf_op jit(solution)/shard_map/dot_general | solution.py:225
  150.7 2.5 %convolution_bitcast_fusion.value_ref = f32[6,128,128]{2,1,0:T(8,128)} fusion(bf16[512,6,128]{0,2,1:T(8,128)(2,1)} %get-tuple-element.25, bf16[512,6,128]{0,2,1:T(8,128)(2,1)} %bitcast.64), kind=kOutput, calls=%fused_computation.16 | convolution fusion | flops 100663296 | bytes 1966080 | tf_op jit(solution)/shard_map/thi,thj->hij/dot_general | solution.py:238
  153.2 38.3 %shard_map.102 = (f32[6,128,128]{2,1,0:T(8,128)}, f32[6,128,128]{2,1,0:T(8,128)}) custom-call(f32[6,128,128]{2,1,0:T(8,128)} %convolution_bitcast_fusion.value_ref), custom_call_target="tpu_custom_call" | custom-call | tf_op jit(solution)/shard_map/pallas_call | solution.py:56
  191.5 1.8 fusion.13
  193.7 1.2 copy.49
  194.9 2.6 %select_convert_fusion = bf16[6,512,512]{2,1,0:T(8,128)(2,1)S(1)} fusion(pred[512,512]{1,0:T(8,128)(4,1)} %copy-done.14, bf16[512,6,128]{0,2,1:T(8,128)(2,1)} %get-tuple-element.25, bf16[512,6,128]{0,2,1:T(8,128)(2,1)} %bitcast.60), kind=kOutput, calls=%fused_computation.2 | convolution fusion | flops 405798912 | bytes 4980736 | tf_op jit(solution)/shard_map/thj,shj->hts/dot_general | solution.py:236
  197.5 0.6 fusion.14
  198.7 1.3 fusion.2
  200.0 2.3 %copy.48 = bf16[512,768]{1,0:T(8,128)(2,1)} copy(bf16[512,768]{0,1:T(8,128)(2,1)} %bitcast.69) | data formatting | bytes 1572864
  202.2 2.3 %fusion.12 = f32[6,512,128]{1,2,0:T(8,128)S(1)} fusion(bf16[6,512,512]{2,1,0:T(8,128)(2,1)S(1)} %select_convert_fusion, bf16[512,6,128]{0,2,1:T(8,128)(2,1)} %bitcast.57), kind=kOutput, calls=%fused_computation.29 | convolution fusion | flops 402653184 | bytes 5505024 | tf_op jit(solution)/shard_map/hts,shi->thi/dot_general | solution.py:241
  205.0 1.2 copy.47
  206.1 0.7 copy.64
  (45 shorter events, 2.2 us)
Async XLA Ops:
  7.2 5.1 %copy-start.11 = (bf16[512,768]{1,0:T(8,128)(2,1)S(1)}, bf16[512,768]{1,0:T(8,128)(2,1)}, u32[]{:S(2)}) copy-start(bf16[512,768]{1,0:T(8,128)(2,1)} %param.6) | copy-start | bytes 2359300
  7.2 120.9 %all-gather.2.cloned.1.call-start = ((), (), s32[]{:S(2)}) async-start(), calls=%async_computation.1 | async-start | bytes 4866048 | tf_op jit(solution)/shard_map/all_gather | solution.py:210
  9.0 197.1 %reduce-scatter.2.cloned.1.call-start = ((), (), s32[]{:S(2)}) async-start(), calls=%async_computation.2 | async-start | bytes 7077888 | tf_op jit(solution)/shard_map/reduce_scatter | solution.py:229
  10.5 112.7 %copy-start = (bf16[512,768]{0,1:T(8,128)(2,1)}, bf16[512,768]{0,1:T(8,128)(2,1)S(1)}, u32[]{:S(2)}) copy-start(bf16[512,768]{0,1:T(8,128)(2,1)S(1)} %copy.32) | copy-start | bytes 2359300
  10.5 111.5 %copy-start.13 = (f32[6,128,128]{2,1,0:T(8,128)S(1)}, f32[6,128,128]{2,1,0:T(8,128)}, u32[]{:S(2)}) copy-start(f32[6,128,128]{2,1,0:T(8,128)} %param.9) | copy-start | bytes 1179652
  12.2 111.0 %copy-start.2 = (bf16[512,768]{0,1:T(8,128)(2,1)}, bf16[512,768]{0,1:T(8,128)(2,1)S(1)}, u32[]{:S(2)}) copy-start(bf16[512,768]{0,1:T(8,128)(2,1)S(1)} %copy.35) | copy-start | bytes 2359300
  122.0 1.2 copy-start.14
  123.2 2.6 %copy-start.3 = (bf16[512,768]{0,1:T(8,128)(2,1)S(1)}, bf16[512,768]{0,1:T(8,128)(2,1)}, u32[]{:S(2)}) copy-start(bf16[512,768]{0,1:T(8,128)(2,1)} %copy-done.2) | copy-start | bytes 2359300
  128.1 9.9 %copy-start.6 = (bf16[512,768]{0,1:T(8,128)(2,1)S(1)}, bf16[512,768]{0,1:T(8,128)(2,1)}, u32[]{:S(2)}) copy-start(bf16[512,768]{0,1:T(8,128)(2,1)} %copy.31) | copy-start | bytes 2359300
  128.1 9.9 %copy-start.8 = (f32[6,512,128]{1,2,0:T(8,128)S(1)}, f32[6,512,128]{1,2,0:T(8,128)}, u32[]{:S(2)}) copy-start(f32[6,512,128]{1,2,0:T(8,128)} %fusion.10) | copy-start | bytes 4718596
  138.0 2.4 %slice-start = ((s8[4718592]{0:T(1024)(128)(4,1)}), s8[4194304]{0:T(1024)(128)(4,1)S(1)}, s32[]{:S(2)}) async-start(s8[4718592]{0:T(1024)(128)(4,1)} %bitcast.73), calls=%async_computation.3 | async-start | bytes 8388608
  138.0 2.6 %slice-start.1 = ((s8[4718592]{0:T(1024)(128)(4,1)}), s8[524288]{0:T(1024)(128)(4,1)S(1)}, s32[]{:S(2)}) async-start(s8[4718592]{0:T(1024)(128)(4,1)} %bitcast.73), calls=%async_computation.4 | async-start | bytes 1048576
  191.4 1.8 copy-start.1
  191.4 1.8 copy-start.9
  194.9 2.6 %copy-start.7 = (bf16[512,768]{0,1:T(8,128)(2,1)S(1)}, bf16[512,768]{0,1:T(8,128)(2,1)}, u32[]{:S(2)}) copy-start(bf16[512,768]{0,1:T(8,128)(2,1)} %copy.31) | copy-start | bytes 2359300
  197.5 1.1 copy-start.4
  197.5 1.2 copy-start.10
  202.2 2.3 %copy-start.5 = (bf16[512,6,128]{0,2,1:T(8,128)(2,1)S(1)}, bf16[512,6,128]{0,2,1:T(8,128)(2,1)}, u32[]{:S(2)}) copy-start(bf16[512,6,128]{0,2,1:T(8,128)(2,1)} %get-tuple-element.25) | copy-start | bytes 2359300
  204.6 1.5 copy-start.12
Sparse Core Ops, SparseCore 0:
  11.2 106.6 all-gather.1
  150.8 39.4 reduce-scatter.1

commit v6 on v5

--- a/solution.py
+++ b/solution.py
@@ -68,6 +68,92 @@
             collective_id=1 if backward else 0, has_side_effects=True
         ),
     )(value.astype(jnp.float32))
+
+
+def backward_kernel(adj_ref, q_ref, k_ref, v_ref, ga_ref, sh_ref, gq_ref, gk_ref, gv_ref, total_ref,
+                    sendbuf, recvbuf, send_sem, recv_sem, gk_acc, gv_acc):
+    me = lax.axis_index("seq")
+    head = lax.axis_index("head")
+    count = lax.axis_size("seq")
+    rounds = count.bit_length() - 1
+    heads = sh_ref.shape[0]
+    dim = sh_ref.shape[2]
+    rows = q_ref.shape[0]
+    partners = []
+    for k in range(rounds):
+        step = 1 << k
+        bit = (me // step) % 2
+        partners.append((me + step - 2 * step * bit, bit))
+    barrier = pltpu.get_barrier_semaphore()
+    for partner, _ in partners:
+        pl.semaphore_signal(barrier, inc=1, device_id=(partner, head), device_id_type=MESH)
+    pl.semaphore_wait(barrier, rounds)
+    causal = lax.broadcasted_iota(jnp.int32, (rows, rows), 1) <= lax.broadcasted_iota(jnp.int32, (rows, rows), 0)
+    nt = (((1,), (1,)), ((), ()))
+    tn = (((0,), (0,)), ((), ()))
+
+    def head_work(h):
+        cols = pl.ds(h * dim, dim)
+        qh, kh, vh, gah = q_ref[:, cols], k_ref[:, cols], v_ref[:, cols], ga_ref[:, cols]
+        gs = lax.dot_general(gah, vh, nt, preferred_element_type=jnp.float32)
+        gs = jnp.where(causal, gs, 0.0).astype(jnp.bfloat16)
+        aw = lax.dot_general(qh, kh, nt, preferred_element_type=jnp.float32)
+        aw = jnp.where(causal, aw, 0.0).astype(jnp.bfloat16)
+        gq = jnp.dot(gs, kh, preferred_element_type=jnp.float32)
+        gq = gq + lax.dot_general(gah, sh_ref[h], nt, preferred_element_type=jnp.float32)
+        gq_ref[:, cols] = gq.astype(gq_ref.dtype)
+        gk_acc[:, cols] = lax.dot_general(gs, qh, tn, preferred_element_type=jnp.float32)
+        gv_acc[:, cols] = lax.dot_general(aw, gah, tn, preferred_element_type=jnp.float32)
+
+    order = [[] for _ in range(rounds)]
+    for h in range(heads):
+        order[min(h, rounds - 1)].append(h)
+    total = adj_ref[...]
+    partial = jnp.zeros_like(total)
+    for t, (partner, bit) in enumerate(partners):
+        sent = total.astype(jnp.bfloat16)
+        sendbuf[t] = sent
+        copy = pltpu.make_async_remote_copy(
+            src_ref=sendbuf.at[t], dst_ref=recvbuf.at[t], send_sem=send_sem.at[t],
+            recv_sem=recv_sem.at[t], device_id=(partner, head), device_id_type=MESH,
+        )
+        copy.start()
+        for h in order[t]:
+            head_work(h)
+        copy.wait()
+        other = recvbuf[t].astype(jnp.float32)
+        partial = jnp.where(bit == 0, partial + other, partial)
+        total = sent.astype(jnp.float32) + other
+    total_ref[...] = total
+    later = partial.astype(jnp.bfloat16)
+    for h in range(heads):
+        cols = pl.ds(h * dim, dim)
+        gk = gk_acc[:, cols] + lax.dot_general(v_ref[:, cols], later[h], nt, preferred_element_type=jnp.float32)
+        gk_ref[:, cols] = gk.astype(gk_ref.dtype)
+        gv = gv_acc[:, cols] + jnp.dot(k_ref[:, cols], later[h], preferred_element_type=jnp.float32)
+        gv_ref[:, cols] = gv.astype(gv_ref.dtype)
+
+
+def backward_pass(own_adjoint, query, key, value, grad_att, state_half):
+    count = lax.axis_size("seq")
+    rounds = count.bit_length() - 1
+    tokens = jax.ShapeDtypeStruct(query.shape, jnp.bfloat16)
+    vmem = pl.BlockSpec(memory_space=pltpu.VMEM)
+    return pl.pallas_call(
+        backward_kernel,
+        out_shape=(tokens, tokens, tokens, jax.ShapeDtypeStruct(own_adjoint.shape, jnp.float32)),
+        in_specs=[vmem] * 6,
+        out_specs=(vmem, vmem, vmem, vmem),
+        scratch_shapes=[
+            pltpu.VMEM((rounds,) + own_adjoint.shape, jnp.bfloat16),
+            pltpu.VMEM((rounds,) + own_adjoint.shape, jnp.bfloat16),
+            pltpu.SemaphoreType.DMA((rounds,)),
+            pltpu.SemaphoreType.DMA((rounds,)),
+            pltpu.VMEM(query.shape, jnp.float32),
+            pltpu.VMEM(query.shape, jnp.float32),
+        ],
+        compiler_params=pltpu.CompilerParams(collective_id=1, has_side_effects=True),
+    )(own_adjoint, query, key, value, grad_att, state_half)
 
 
 def gather_kernel(ny, ca, value_ref, w_ref, rows_ref, partial_ref, sendbuf, recvbuf, send_sem, recv_sem, bf_send, bf_recv, local_sem):
@@ -233,35 +319,11 @@
     grad_att = norm_back(grad_normed.reshape(tok_rows, heads_here, head_dim))[0].astype(
         jnp.bfloat16
     )
-    grad_scores = jnp.einsum("thj,shj->hts", grad_att, val_rows, preferred_element_type=jnp.float32)
-    grad_scores = jnp.where(causal, grad_scores, 0.0).astype(jnp.bfloat16)
     own_adjoint = jnp.einsum("thi,thj->hij", queries, grad_att, preferred_element_type=jnp.float32)
-    later, adjoint_total = butterfly(own_adjoint, "seq", True)
-    later_half = later.astype(jnp.bfloat16)
-    grad_query = jnp.einsum(
-        "hts,shi->thi", grad_scores, key_rows, preferred_element_type=jnp.float32
-    )
-    grad_query = grad_query + jnp.einsum(
-        "thj,hij->thi", grad_att, state_half, preferred_element_type=jnp.float32
-    )
-    grad_key = jnp.einsum("hts,thi->shi", grad_scores, queries, preferred_element_type=jnp.float32)
-    grad_key = grad_key + jnp.einsum(
-        "thj,hij->thi", val_rows, later_half, preferred_element_type=jnp.float32
-    )
-    grad_value = jnp.einsum(
-        "hts,thj->shj", attn_weights, grad_att, preferred_element_type=jnp.float32
-    )
-    grad_value = grad_value + jnp.einsum(
-        "thi,hij->thj", key_rows, later_half, preferred_element_type=jnp.float32
-    )
-    init_grad = adjoint_total
-    return (
-        mixed,
-        grad_query.reshape(tok_rows, width).astype(jnp.bfloat16),
-        grad_key.reshape(tok_rows, width).astype(jnp.bfloat16),
-        grad_value.reshape(tok_rows, width).astype(jnp.bfloat16),
-        init_grad,
-    )
+    grad_query, grad_key, grad_value, init_grad = backward_pass(
+        own_adjoint, query, key, value, grad_att.reshape(tok_rows, width), state_half
+    )
+    return (mixed, grad_query, grad_key, grad_value, init_grad)
 
 
 def solution(mesh):

time: 218 us -> 212 us (0.972); the launches traced: 214 us -> 211 us
  matrix products: 38.3 us -> 30.8 us
    dot_general x8 -> x0, matrix products: 11.9 us -> none  [the longest x1 2.58 us: shards(): jnp.einsum('thj,shj->hts', grad_att, val_rows, preferred_element_type=jnp...]
    dot_general x1, matrix products: 2.35 us -> 5.11 us  [shards(): jnp.einsum('hts,shj->thj', attn_weights, val_rows, preferred_element_type...]
    pallas_call x1, Pallas kernels: 38.3 us -> 40.5 us  [backward_pass(): pl.pallas_call(backward_kernel, out_shape=(tokens, tokens, tokens, jax.Sh...]
    unnamed x41 -> x13, local copies, waits for them, and re-layouts: 10.8 us -> 11.2 us
  transfers between devices with their start and end apart: 2 -> 2, of which waited for: 0 -> 0; matrix products, arithmetic and copies ran while one was open for 13% -> 5% of each run, Pallas kernels for 68% -> 70%
where the time goes in v6:
time: 212 us; the launch traced here: 211 us
  Pallas kernels  148 us (70%)
  matrix products  30.8 us (15%)
  local copies, waits for them, and re-layouts  14.1 us (7%)
  between operations  14.1 us (7%)
  other arithmetic  3.49 us (2%)
    pallas_call x1, Pallas kernels, gather_and_scan(): pl.pallas_call(functools.partial(gather_kernel, ny, ca), out_shape=(jax.S...  107 us
    pallas_call x1, Pallas kernels, backward_pass(): pl.pallas_call(backward_kernel, out_shape=(tokens, tokens, tokens, jax.Sh...  40.5 us
    dot_general x1, matrix products, shards(): projected = jnp.dot(normed, weight_rows, preferred_element_type=jnp.float32)  11.6 us
    unnamed x13, local copies, waits for them, and re-layouts  11.2 us
    dot_general x1, matrix products, shards(): lax.dot_general(out_grad, weight_rows, (((1,), (1,)), ((), ())), preferre...  10.4 us
    dot_general x1, matrix products, shards(): jnp.einsum('hts,shj->thj', attn_weights, val_rows, preferred_element_type...  5.11 us
  transfers between devices with their start and end apart: 2, of which 0 were waited for; matrix products, arithmetic and copies ran while one was open for 5% of the time, Pallas kernels for 70%

profile of v6, /device:TPU:2, one launch (start us, length us, event | category | flops | bytes accessed | tf_op | source)
XLA Modules:
  0.0 210.7 jit_solution(4207323264808439574)
XLA Ops:
  7.2 0.0 all-gather.2.cloned.1.call-start
  7.2 1.8 fusion.11
  9.0 0.0 all-gather.2.cloned.1.call-update
  9.0 0.0 reduce-scatter.2.cloned.1.call-start
  9.0 1.4 copy.19
  10.5 1.4 copy.20
  11.9 1.4 copy.21
  13.3 1.1 fusion.12.value_ref
  14.4 107.4 %shard_map.101 = (bf16[8,4,24,3072]{3,2,1,0:T(8,128)(2,1)}, f32[6,128,128]{2,1,0:T(8,128)}) custom-call(f32[6,128,128]{2,1,0:T(8,128)} %fusion.12.value_ref, bf16[24,3072]{1,0:T(8,128)(2,1)} %get-tuple-element.22.w_ref), custom_call_target="tpu_custom_call" | custom-call | tf_op jit(solution)/shard_map/pallas_call | solution.py:260
  121.9 0.1 iota_compare_fusion
  122.0 1.0 add_convert_fusion.sh_ref
  123.0 1.6 fusion.13
  124.6 10.4 %fusion = f32[768,512]{1,0:T(8,128)} fusion(bf16[512,6144]{1,0:T(8,128)(2,1)} %param.11, bf16[768,3072]{1,0:T(8,128)(2,1)} %all-gather.2.cloned.1.call-done, bf16[768,3072]{1,0:T(8,128)(2,1)} %bitcast.37), kind=kOutput, calls=%fused_computation.3 | convolution fusion | flops 4850712576 | bytes 17301504 | tf_op jit(solution)/shard_map/dot_general | solution.py:312
  135.0 5.1 %multiply_reduce_fusion = (f32[512,6]{0,1:T(8,128)S(1)}, f32[512,6]{0,1:T(8,128)S(1)}, f32[512,6,128]{0,2,1:T(8,128)}) fusion(f32[512,6,128]{0,2,1:T(8,128)} %bitcast.34, f32[6,128,512]{2,1,0:T(8,128)} %fusion.13, bf16[512,6,128]{0,2,1:T(8,128)(2,1)S(1)} %bitcast.33, pred[512,512]{1,0:T(8,128)(4,1)S(1)} %iota_compare_fusion, ...), kind=kOutput, calls=%fused_computation.11 | convolution fusion | flops 810412032 | bytes 7364608 | tf_op jit(solution)/shard_map/hts,shj->thj/dot_general | solution.py:303
  140.1 2.4 %fusion.6 = (bf16[512,6,128]{0,2,1:T(8,128)(2,1)S(1)}, bf16[512,6,128]{0,2,1:T(8,128)(2,1)S(1)}) fusion(f32[512,6,128]{0,2,1:T(8,128)} %get-tuple-element.25, f32[512,6,128]{0,2,1:T(8,128)} %bitcast.35, f32[512,6]{0,1:T(8,128)S(1)} %get-tuple-element.23, f32[512,6]{0,1:T(8,128)S(1)} %get-tuple-element.24), kind=kLoop, calls=%fused_computation.9 | loop fusion | flops 2752512 | bytes 4743168 | tf_op jit(solution)/shard_map/convert_element_type | solution.py:319
  142.5 11.6 %convolution_convert_fusion = bf16[512,6144]{1,0:T(8,128)(2,1)} fusion(bf16[512,768]{0,1:T(8,128)(2,1)S(1)} %bitcast.36, bf16[768,3072]{1,0:T(8,128)(2,1)} %all-gather.2.cloned.1.call-done, bf16[768,3072]{1,0:T(8,128)(2,1)} %bitcast.38), kind=kOutput, calls=%fused_computation.1 | convolution fusion | flops 4853858304 | bytes 16515072 | tf_op jit(solution)/shard_map/dot_general | solution.py:311
  154.0 1.2 copy.27.ga_ref
  155.2 1.1 convolution_bitcast_fusion.adj_ref
  156.3 40.5 %shard_map.102 = (bf16[512,768]{1,0:T(8,128)(2,1)}, bf16[512,768]{1,0:T(8,128)(2,1)}, bf16[512,768]{1,0:T(8,128)(2,1)}, f32[6,128,128]{2,1,0:T(8,128)}) custom-call(f32[6,128,128]{2,1,0:T(8,128)} %convolution_bitcast_fusion.adj_ref, bf16[512,768]{1,0:T(8,128)(2,1)} %q_ref.1, bf16[512,768]{1,0:T(8,128)(2,1)} %k_ref.1, bf16[512,768]{1,0:T(8,128)(2,1)} %v_ref.1, ...), custom_call_target="tpu_custom_call" | custom-call | tf_op jit(solution)/shard_map/pallas_call | solution.py:142
  196.8 0.0 reduce-scatter.2.cloned.1.call-done
  196.9 2.1 %copy.37 = bf16[512,768]{1,0:T(8,128)(2,1)} copy(bf16[512,768]{1,0:T(8,128)(2,1)} %get-tuple-element.32) | data formatting | bytes 1572864
  199.0 2.1 copy.38
  201.0 2.1 copy.39
  203.1 0.7 copy.40
  (9 shorter events, 0.0 us)
Async XLA Ops:
  7.2 114.8 %copy-start.2 = (f32[6,128,128]{2,1,0:T(8,128)S(1)}, f32[6,128,128]{2,1,0:T(8,128)}, u32[]{:S(2)}) copy-start(f32[6,128,128]{2,1,0:T(8,128)} %param.9) | copy-start | bytes 1179652
  7.2 117.4 %all-gather.2.cloned.1.call-start = ((), (), s32[]{:S(2)}) async-start(), calls=%async_computation.1 | async-start | bytes 4866048 | tf_op jit(solution)/shard_map/all_gather | solution.py:296
  9.0 187.9 %reduce-scatter.2.cloned.1.call-start = ((), (), s32[]{:S(2)}) async-start(), calls=%async_computation.2 | async-start | bytes 7077888 | tf_op jit(solution)/shard_map/reduce_scatter | solution.py:315
  123.0 12.0 %copy-start = (bf16[6,128,128]{2,1,0:T(8,128)(2,1)}, bf16[6,128,128]{2,1,0:T(8,128)(2,1)S(1)}, u32[]{:S(2)}) copy-start(bf16[6,128,128]{2,1,0:T(8,128)(2,1)S(1)} %add_convert_fusion.sh_ref) | copy-start | bytes 589828
  196.8 6.3 %copy-start.1 = (f32[6,128,128]{2,1,0:T(8,128)S(1)}, f32[6,128,128]{2,1,0:T(8,128)}, u32[]{:S(2)}) copy-start(f32[6,128,128]{2,1,0:T(8,128)} %get-tuple-element.35) | copy-start | bytes 1179652
Sparse Core Ops, SparseCore 0:
  11.2 105.8 all-gather.1
  154.2 39.6 reduce-scatter.1

commit v7 on v6

--- a/solution.py
+++ b/solution.py
@@ -70,8 +70,8 @@
     )(value.astype(jnp.float32))
 
 
-def backward_kernel(adj_ref, q_ref, k_ref, v_ref, ga_ref, sh_ref, gq_ref, gk_ref, gv_ref, total_ref,
-                    sendbuf, recvbuf, send_sem, recv_sem, gk_acc, gv_acc):
+def backward_kernel(adj_ref, q_ref, k_ref, v_ref, ga_ref, sh_ref, gq_ref, gk_acc, gv_acc, later_ref, total_ref,
+                    sendbuf, recvbuf, send_sem, recv_sem):
     me = lax.axis_index("seq")
     head = lax.axis_index("head")
     count = lax.axis_size("seq")
@@ -125,12 +125,19 @@
         partial = jnp.where(bit == 0, partial + other, partial)
         total = sent.astype(jnp.float32) + other
     total_ref[...] = total
-    later = partial.astype(jnp.bfloat16)
+    later_ref[...] = partial.astype(later_ref.dtype)
+
+
+def finish_kernel(gq_in, gk_acc, gv_acc, v_ref, k_ref, later_ref, gq_ref, gk_ref, gv_ref):
+    heads, dim = later_ref.shape[0], later_ref.shape[2]
+    nt = (((1,), (1,)), ((), ()))
+    gq_ref[...] = gq_in[...]
     for h in range(heads):
         cols = pl.ds(h * dim, dim)
-        gk = gk_acc[:, cols] + lax.dot_general(v_ref[:, cols], later[h], nt, preferred_element_type=jnp.float32)
+        later = later_ref[h]
+        gk = gk_acc[:, cols] + lax.dot_general(v_ref[:, cols], later, nt, preferred_element_type=jnp.float32)
         gk_ref[:, cols] = gk.astype(gk_ref.dtype)
-        gv = gv_acc[:, cols] + jnp.dot(k_ref[:, cols], later[h], preferred_element_type=jnp.float32)
+        gv = gv_acc[:, cols] + jnp.dot(k_ref[:, cols], later, preferred_element_type=jnp.float32)
         gv_ref[:, cols] = gv.astype(gv_ref.dtype)
 
 
@@ -139,21 +146,28 @@
     rounds = count.bit_length() - 1
     tokens = jax.ShapeDtypeStruct(query.shape, jnp.bfloat16)
     vmem = pl.BlockSpec(memory_space=pltpu.VMEM)
-    return pl.pallas_call(
+    accs = jax.ShapeDtypeStruct(query.shape, jnp.float32)
+    gq, gk_acc, gv_acc, later, total = pl.pallas_call(
         backward_kernel,
-        out_shape=(tokens, tokens, tokens, jax.ShapeDtypeStruct(own_adjoint.shape, jnp.float32)),
+        out_shape=(tokens, accs, accs, jax.ShapeDtypeStruct(own_adjoint.shape, jnp.bfloat16),
+                   jax.ShapeDtypeStruct(own_adjoint.shape, jnp.float32)),
         in_specs=[vmem] * 6,
-        out_specs=(vmem, vmem, vmem, vmem),
+        out_specs=(vmem,) * 5,
         scratch_shapes=[
             pltpu.VMEM((rounds,) + own_adjoint.shape, jnp.bfloat16),
             pltpu.VMEM((rounds,) + own_adjoint.shape, jnp.bfloat16),
             pltpu.SemaphoreType.DMA((rounds,)),
             pltpu.SemaphoreType.DMA((rounds,)),
-            pltpu.VMEM(query.shape, jnp.float32),
-            pltpu.VMEM(query.shape, jnp.float32),
         ],
         compiler_params=pltpu.CompilerParams(collective_id=1, has_side_effects=True),
     )(own_adjoint, query, key, value, grad_att, state_half)
+    gq, gk, gv = pl.pallas_call(
+        finish_kernel,
+        out_shape=(tokens, tokens, tokens),
+        in_specs=[vmem] * 6,
+        out_specs=(vmem,) * 3,
+    )(gq, gk_acc, gv_acc, value, key, later)
+    return gq, gk, gv, total
 
 
 def gather_kernel(ny, ca, value_ref, w_ref, rows_ref, partial_ref, sendbuf, recvbuf, send_sem, recv_sem, bf_send, bf_recv, local_sem):
@@ -308,12 +322,13 @@
     )
     normed = normalize(attended).astype(jnp.bfloat16).reshape(tok_rows, width)
     weight_rows = jnp.concatenate([gathered.reshape(-1, half), other_half], axis=1)
-    projected = jnp.dot(normed, weight_rows, preferred_element_type=jnp.float32)
+    projected = jnp.dot(normed, weight_rows, preferred_element_type=jnp.float32).astype(jnp.bfloat16)
+    projected, weight_rows = lax.optimization_barrier((projected, weight_rows))
     grad_normed = lax.dot_general(
         out_grad, weight_rows, (((1,), (1,)), ((), ())), preferred_element_type=jnp.float32
     )
     mixed = lax.psum_scatter(
-        projected.astype(jnp.bfloat16), "head", scatter_dimension=1, tiled=True
+        projected, "head", scatter_dimension=1, tiled=True
     )
     _, norm_back = jax.vjp(normalize, attended)
     grad_att = norm_back(grad_normed.reshape(tok_rows, heads_here, head_dim))[0].astype(

time: 212 us -> 215 us (1.014)
  other arithmetic: 3.49 us -> 12.2 us
  local copies, waits for them, and re-layouts: 14.1 us -> 7.92 us
  Pallas kernels: 148 us -> 153 us
  matrix products: 30.8 us -> 27.4 us
    concatenate x0 -> x1, other arithmetic: none -> 9.36 us  [shards(): jnp.concatenate([gathered.reshape(-1, half), other_half], axis=1)]
    unnamed x13 -> x14, local copies, waits for them, and re-layouts: 11.2 us -> 5.01 us
    pallas_call x1 -> x2, Pallas kernels: 40.5 us -> 45.2 us  [the longest x1 40.6 us: backward_pass(): pl.pallas_call(backward_kernel, out_shape=(tokens, accs, accs, jax.ShapeD...]
  transfers between devices with their start and end apart: 2 -> 2, of which waited for: 0 -> 0; matrix products, arithmetic and copies ran while one was open for 5% -> 12% of each run, Pallas kernels for 70% -> 71%
where the time goes in v7:
time: 215 us
  Pallas kernels  153 us (71%)
  matrix products  27.4 us (13%)
  between operations  14.2 us (7%)
  other arithmetic  12.2 us (6%)
  local copies, waits for them, and re-layouts  7.92 us (4%)
    pallas_call x1, Pallas kernels, gather_and_scan(): pl.pallas_call(functools.partial(gather_kernel, ny, ca), out_shape=(jax.S...  108 us
    pallas_call x1, Pallas kernels, backward_pass(): pl.pallas_call(backward_kernel, out_shape=(tokens, accs, accs, jax.ShapeD...  40.6 us
    dot_general x1, matrix products, shards(): jnp.dot(normed, weight_rows, preferred_element_type=jnp.float32)  10.1 us
    dot_general x1, matrix products, shards(): lax.dot_general(out_grad, weight_rows, (((1,), (1,)), ((), ())), preferre...  9.69 us
    concatenate x1, other arithmetic, shards(): jnp.concatenate([gathered.reshape(-1, half), other_half], axis=1)  9.36 us
    unnamed x14, local copies, waits for them, and re-layouts  5.01 us
    pallas_call x1, Pallas kernels, backward_pass(): pl.pallas_call(finish_kernel, out_shape=(tokens, tokens, tokens), in_spec...  4.58 us
  transfers between devices with their start and end apart: 2, of which 0 were waited for; matrix products, arithmetic and copies ran while one was open for 12% of the time, Pallas kernels for 71%

profile of v7, /device:TPU:2, one launch (start us, length us, event | category | flops | bytes accessed | tf_op | source)
XLA Modules:
  0.0 214.6 jit_solution(11325219787188467025)
XLA Ops:
  7.2 0.0 all-gather.2.cloned.1.call-start
  7.2 1.8 fusion.8
  9.0 0.0 reduce-scatter.2.cloned.1.call-start
  9.0 1.4 copy.19
  10.5 1.4 copy.20
  11.9 1.4 copy.21
  13.3 1.1 fusion.9.value_ref
  14.4 107.5 %shard_map.101 = (bf16[8,4,24,3072]{3,2,1,0:T(8,128)(2,1)}, f32[6,128,128]{2,1,0:T(8,128)}) custom-call(f32[6,128,128]{2,1,0:T(8,128)} %fusion.9.value_ref, bf16[24,3072]{1,0:T(8,128)(2,1)} %get-tuple-element.30.w_ref), custom_call_target="tpu_custom_call" | custom-call | tf_op jit(solution)/shard_map/pallas_call | solution.py:274
  122.0 0.8 iota_compare_fusion
  122.7 1.0 add_convert_fusion.sh_ref
  123.8 1.6 fusion.10
  125.4 3.8 %multiply_reduce_fusion.1 = (f32[512,6]{0,1:T(8,128)S(1)}, f32[512,6,128]{0,2,1:T(8,128)S(1)}) fusion(f32[6,128,512]{2,1,0:T(8,128)} %fusion.10, bf16[512,6,128]{0,2,1:T(8,128)(2,1)} %bitcast.38, pred[512,512]{1,0:T(8,128)(4,1)} %iota_compare_fusion, bf16[512,6,128]{0,2,1:T(8,128)(2,1)S(1)} %bitcast.28, bf16[512,6,128]{0,2,1:T(8,128)(2,1)S(1)} %bitcast.36), kind=kOutput, calls=%fused_computation.12 | convolution fusion | flops 809628672 | bytes 5779456 | tf_op jit(solution)/shard_map/hts,shj->thj/dot_general | solution.py:317
  129.2 0.2 multiply_convert_fusion
  129.4 0.0 all-gather.2.cloned.1.call-done
  129.4 9.4 %pad_maximum_fusion = bf16[768,6144]{1,0:T(8,128)(2,1)} fusion(bf16[768,3072]{1,0:T(8,128)(2,1)} %all-gather.2.cloned.1.call-done, bf16[768,3072]{1,0:T(8,128)(2,1)} %bitcast.33), kind=kLoop, calls=%fused_computation | loop fusion | flops 18874368 | bytes 18874368 | tf_op jit(solution)/shard_map/concatenate | solution.py:324
  138.8 10.1 %convolution_convert_fusion = bf16[512,6144]{1,0:T(8,128)(2,1)} fusion(bf16[512,768]{0,1:T(8,128)(2,1)S(1)} %bitcast.39, bf16[768,3072]{1,0:T(8,128)(2,1)S(1)} %copy-done, bf16[768,3072]{1,0:T(8,128)(2,1)} %bitcast.34), kind=kOutput, calls=%fused_computation.1 | convolution fusion | flops 4853858304 | bytes 16515072 | tf_op jit(solution)/shard_map/dot_general | solution.py:325
  148.9 9.7 %fusion.11 = f32[768,512]{1,0:T(8,128)S(1)} fusion(bf16[768,6144]{1,0:T(8,128)(2,1)} %pad_maximum_fusion, bf16[512,6144]{1,0:T(8,128)(2,1)} %param.11), kind=kOutput, calls=%fused_computation.23 | convolution fusion | flops 4831838208 | bytes 17301504 | tf_op jit(solution)/shard_map/dot_general | solution.py:327
  158.7 0.4 multiply_reduce_fusion
  159.1 0.4 fusion.5
  159.5 1.2 copy.27.ga_ref
  160.7 1.1 convolution_bitcast_fusion.adj_ref
  161.8 40.6 %shard_map.102 = (bf16[512,768]{1,0:T(8,128)(2,1)}, f32[512,768]{1,0:T(8,128)}, f32[512,768]{1,0:T(8,128)}, bf16[6,128,128]{2,1,0:T(8,128)(2,1)}, f32[6,128,128]{2,1,0:T(8,128)}) custom-call(f32[6,128,128]{2,1,0:T(8,128)} %convolution_bitcast_fusion.adj_ref, bf16[512,768]{1,0:T(8,128)(2,1)} %q_ref.1, bf16[512,768]{1,0:T(8,128)(2,1)} %k_ref.3, ...), custom_call_target="tpu_custom_call" | custom-call | tf_op jit(solution)/shard_map/pallas_call | solution.py:150
  202.4 4.6 %shard_map.103 = (bf16[512,768]{1,0:T(8,128)(2,1)}, bf16[512,768]{1,0:T(8,128)(2,1)}, bf16[512,768]{1,0:T(8,128)(2,1)}) custom-call(bf16[512,768]{1,0:T(8,128)(2,1)} %get-tuple-element.21.gq_in, f32[512,768]{1,0:T(8,128)} %get-tuple-element.22.gk_acc, f32[512,768]{1,0:T(8,128)} %get-tuple-element.23.gv_acc, bf16[512,768]{1,0:T(8,128)(2,1)} %v_ref.3, ...), custom_call_target="tpu_custom_call" | custom-call | tf_op jit(solution)/shard_map/pallas_call | solution.py:164
  207.0 0.7 copy.34
  (15 shorter events, 0.1 us)
Async XLA Ops:
  7.2 115.6 %copy-start.4 = (f32[6,128,128]{2,1,0:T(8,128)S(1)}, f32[6,128,128]{2,1,0:T(8,128)}, u32[]{:S(2)}) copy-start(f32[6,128,128]{2,1,0:T(8,128)} %param.9) | copy-start | bytes 1179652
  7.2 122.2 %all-gather.2.cloned.1.call-start = ((), (), s32[]{:S(2)}) async-start(), calls=%async_computation.1 | async-start | bytes 4866048 | tf_op jit(solution)/shard_map/all_gather | solution.py:310
  9.0 198.0 %reduce-scatter.2.cloned.1.call-start = ((), (), s32[]{:S(2)}) async-start(), calls=%async_computation.2 | async-start | bytes 7077888 | tf_op jit(solution)/shard_map/reduce_scatter | solution.py:330
  13.3 110.5 %copy-start.1 = (bf16[512,768]{0,1:T(8,128)(2,1)}, bf16[512,768]{0,1:T(8,128)(2,1)S(1)}, u32[]{:S(2)}) copy-start(bf16[512,768]{0,1:T(8,128)(2,1)S(1)} %copy.21) | copy-start | bytes 2359300
  123.8 5.4 %copy-start.2 = (bf16[6,128,128]{2,1,0:T(8,128)(2,1)}, bf16[6,128,128]{2,1,0:T(8,128)(2,1)S(1)}, u32[]{:S(2)}) copy-start(bf16[6,128,128]{2,1,0:T(8,128)(2,1)S(1)} %add_convert_fusion.sh_ref) | copy-start | bytes 589828
  129.4 9.4 %copy-start = (bf16[768,3072]{1,0:T(8,128)(2,1)S(1)}, bf16[768,3072]{1,0:T(8,128)(2,1)}, u32[]{:S(2)}) copy-start(bf16[768,3072]{1,0:T(8,128)(2,1)} %all-gather.2.cloned.1.call-done) | copy-start | bytes 14155780
  202.4 4.6 %copy-start.3 = (f32[6,128,128]{2,1,0:T(8,128)S(1)}, f32[6,128,128]{2,1,0:T(8,128)}, u32[]{:S(2)}) copy-start(f32[6,128,128]{2,1,0:T(8,128)} %get-tuple-element.42) | copy-start | bytes 1179652
Sparse Core Ops, SparseCore 0:
  11.2 105.8 all-gather.1
  149.1 39.4 reduce-scatter.1

commit v8 on v7

--- a/solution.py
+++ b/solution.py
@@ -321,12 +321,14 @@
         "thi,hij->thj", queries, state_half, preferred_element_type=jnp.float32
     )
     normed = normalize(attended).astype(jnp.bfloat16).reshape(tok_rows, width)
-    weight_rows = jnp.concatenate([gathered.reshape(-1, half), other_half], axis=1)
+    first_rows = gathered.reshape(-1, half)
+    weight_rows = jnp.concatenate([first_rows, other_half], axis=1)
     projected = jnp.dot(normed, weight_rows, preferred_element_type=jnp.float32).astype(jnp.bfloat16)
-    projected, weight_rows = lax.optimization_barrier((projected, weight_rows))
+    projected, first_rows, other_half = lax.optimization_barrier((projected, first_rows, other_half))
+    contract = (((1,), (1,)), ((), ()))
     grad_normed = lax.dot_general(
-        out_grad, weight_rows, (((1,), (1,)), ((), ())), preferred_element_type=jnp.float32
-    )
+        out_grad[:, :half], first_rows, contract, preferred_element_type=jnp.float32
+    ) + lax.dot_general(out_grad[:, half:], other_half, contract, preferred_element_type=jnp.float32)
     mixed = lax.psum_scatter(
         projected, "head", scatter_dimension=1, tiled=True
     )

time: 215 us -> 207 us (0.963)
  other arithmetic: 12.2 us -> 2.98 us
  matrix products: 27.4 us -> 30.2 us
    concatenate x1 -> x0, other arithmetic: 9.36 us -> none  [shards(): jnp.concatenate([gathered.reshape(-1, half), other_half], axis=1)]
    dot_general x1 -> x2, matrix products: 9.69 us -> 11.1 us  [the longest x1 5.65 us: shards(): lax.dot_general(out_grad[:, half:], other_half, contract, preferred_eleme...]
    unnamed x14 -> x12, local copies, waits for them, and re-layouts: 5.01 us -> 3.88 us
  transfers between devices with their start and end apart: 2 -> 2, of which waited for: 0 -> 0; matrix products, arithmetic and copies ran while one was open for 12% -> 13% of each run, Pallas kernels for 71% -> 73%
where the time goes in v8:
time: 207 us; the launch traced here: 205 us
  Pallas kernels  151 us (73%)
  matrix products  30.2 us (15%)
  between operations  14.2 us (7%)
  local copies, waits for them, and re-layouts  6.81 us (3%)
  other arithmetic  2.98 us (1%)
    pallas_call x1, Pallas kernels, gather_and_scan(): pl.pallas_call(functools.partial(gather_kernel, ny, ca), out_shape=(jax.S...  107 us
    pallas_call x1, Pallas kernels, backward_pass(): pl.pallas_call(backward_kernel, out_shape=(tokens, accs, accs, jax.ShapeD...  38.7 us
    dot_general x1, matrix products, shards(): jnp.dot(normed, weight_rows, preferred_element_type=jnp.float32)  11.6 us
    dot_general x1, matrix products, shards(): lax.dot_general(out_grad[:, half:], other_half, contract, preferred_eleme...  5.65 us
    dot_general x1, matrix products, shards(): lax.dot_general(out_grad[:, :half], first_rows, contract, preferred_eleme...  5.48 us
    pallas_call x1, Pallas kernels, backward_pass(): pl.pallas_call(finish_kernel, out_shape=(tokens, tokens, tokens), in_spec...  4.58 us
  transfers between devices with their start and end apart: 2, of which 0 were waited for; matrix products, arithmetic and copies ran while one was open for 13% of the time, Pallas kernels for 73%

profile of v8, /device:TPU:2, one launch (start us, length us, event | category | flops | bytes accessed | tf_op | source)
XLA Modules:
  0.0 204.9 jit_solution(16538800463793097648)
XLA Ops:
  7.2 0.0 all-gather.2.cloned.1.call-start
  7.2 1.8 fusion.23
  9.0 0.0 reduce-scatter.2.cloned.1.call-start
  9.1 1.4 copy.19
  10.5 1.4 copy.20
  11.9 0.3 copy.21
  12.2 1.1 fusion.24.value_ref
  13.3 107.3 %shard_map.101 = (bf16[8,4,24,3072]{3,2,1,0:T(8,128)(2,1)}, f32[6,128,128]{2,1,0:T(8,128)}) custom-call(f32[6,128,128]{2,1,0:T(8,128)} %fusion.24.value_ref, bf16[24,3072]{1,0:T(8,128)(2,1)} %get-tuple-element.32.w_ref), custom_call_target="tpu_custom_call" | custom-call | tf_op jit(solution)/shard_map/pallas_call | solution.py:274
  120.6 0.8 iota_compare_fusion
  121.4 1.2 add_convert_fusion.sh_ref
  122.6 1.6 fusion.25
  124.2 3.8 %multiply_reduce_fusion.1 = (f32[512,6]{0,1:T(8,128)S(1)}, f32[512,6,128]{0,2,1:T(8,128)S(1)}) fusion(f32[6,128,512]{2,1,0:T(8,128)} %fusion.25, bf16[512,6,128]{0,2,1:T(8,128)(2,1)} %bitcast.36, pred[512,512]{1,0:T(8,128)(4,1)} %iota_compare_fusion, bf16[512,6,128]{0,2,1:T(8,128)(2,1)S(1)} %bitcast.28, bf16[512,6,128]{0,2,1:T(8,128)(2,1)S(1)} %bitcast.34), kind=kOutput, calls=%fused_computation.19 | convolution fusion | flops 809628672 | bytes 5779456 | tf_op jit(solution)/shard_map/hts,shj->thj/dot_general | solution.py:317
  128.0 0.2 multiply_convert_fusion
  128.2 0.0 all-gather.2.cloned.1.call-done
  128.2 11.6 %fusion.4 = bf16[512,6144]{1,0:T(8,128)(2,1)} fusion(bf16[512,768]{0,1:T(8,128)(2,1)S(1)} %bitcast.37, bf16[768,3072]{1,0:T(8,128)(2,1)} %all-gather.2.cloned.1.call-done, bf16[768,3072]{1,0:T(8,128)(2,1)} %bitcast.38), kind=kOutput, calls=%fused_computation.4 | convolution fusion | flops 4853858304 | bytes 16515072 | tf_op jit(solution)/shard_map/dot_general | solution.py:326
  139.8 5.7 %fusion.8 = f32[768,512]{1,0:T(8,128)S(1)} fusion(bf16[768,3072]{1,0:T(8,128)(2,1)} %all-gather.2.cloned.1.call-done, bf16[512,6144]{1,0:T(8,128)(2,1)} %param.11), kind=kOutput, calls=%fused_computation.7 | convolution fusion | flops 2415919104 | bytes 9437184 | tf_op jit(solution)/shard_map/dot_general | solution.py:331
  145.5 5.5 %fusion.17 = f32[768,512]{1,0:T(8,128)S(1)} fusion(f32[768,512]{1,0:T(8,128)S(1)} %fusion.8, bf16[768,3072]{1,0:T(8,128)(2,1)} %bitcast.39, bf16[512,6144]{1,0:T(8,128)(2,1)} %param.11), kind=kOutput, calls=%fused_computation.20 | convolution fusion | flops 2416312320 | bytes 11010048 | tf_op jit(solution)/shard_map/dot_general | solution.py:329
  150.9 0.4 multiply_reduce_fusion
  151.3 0.4 fusion.16
  151.8 1.2 copy.27.ga_ref
  152.9 1.1 convolution_bitcast_fusion.adj_ref
  154.0 38.7 %shard_map.102 = (bf16[512,768]{1,0:T(8,128)(2,1)}, f32[512,768]{1,0:T(8,128)}, f32[512,768]{1,0:T(8,128)}, bf16[6,128,128]{2,1,0:T(8,128)(2,1)}, f32[6,128,128]{2,1,0:T(8,128)}) custom-call(f32[6,128,128]{2,1,0:T(8,128)} %convolution_bitcast_fusion.adj_ref, bf16[512,768]{1,0:T(8,128)(2,1)} %q_ref.1, bf16[512,768]{1,0:T(8,128)(2,1)} %k_ref.3, ...), custom_call_target="tpu_custom_call" | custom-call | tf_op jit(solution)/shard_map/pallas_call | solution.py:150
  192.7 4.6 %shard_map.103 = (bf16[512,768]{1,0:T(8,128)(2,1)}, bf16[512,768]{1,0:T(8,128)(2,1)}, bf16[512,768]{1,0:T(8,128)(2,1)}) custom-call(bf16[512,768]{1,0:T(8,128)(2,1)} %get-tuple-element.23.gq_in, f32[512,768]{1,0:T(8,128)} %get-tuple-element.24.gk_acc, f32[512,768]{1,0:T(8,128)} %get-tuple-element.25.gv_acc, bf16[512,768]{1,0:T(8,128)(2,1)} %v_ref.3, ...), custom_call_target="tpu_custom_call" | custom-call | tf_op jit(solution)/shard_map/pallas_call | solution.py:164
  197.3 0.7 copy.34
  (13 shorter events, 0.1 us)
Async XLA Ops:
  7.2 4.7 %copy-start = (bf16[512,768]{1,0:T(8,128)(2,1)S(1)}, bf16[512,768]{1,0:T(8,128)(2,1)}, u32[]{:S(2)}) copy-start(bf16[512,768]{1,0:T(8,128)(2,1)} %v_ref.3) | copy-start | bytes 2359300
  7.2 121.0 %all-gather.2.cloned.1.call-start = ((), (), s32[]{:S(2)}) async-start(), calls=%async_computation.1 | async-start | bytes 4866048 | tf_op jit(solution)/shard_map/all_gather | solution.py:310
  9.0 188.3 %reduce-scatter.2.cloned.1.call-start = ((), (), s32[]{:S(2)}) async-start(), calls=%async_computation.2 | async-start | bytes 7077888 | tf_op jit(solution)/shard_map/reduce_scatter | solution.py:332
  12.2 110.4 %copy-start.1 = (bf16[512,768]{0,1:T(8,128)(2,1)}, bf16[512,768]{0,1:T(8,128)(2,1)S(1)}, u32[]{:S(2)}) copy-start(bf16[512,768]{0,1:T(8,128)(2,1)S(1)} %copy.21) | copy-start | bytes 2359300
  122.6 5.4 %copy-start.2 = (bf16[6,128,128]{2,1,0:T(8,128)(2,1)}, bf16[6,128,128]{2,1,0:T(8,128)(2,1)S(1)}, u32[]{:S(2)}) copy-start(bf16[6,128,128]{2,1,0:T(8,128)(2,1)S(1)} %add_convert_fusion.sh_ref) | copy-start | bytes 589828
  192.7 4.6 %copy-start.3 = (f32[6,128,128]{2,1,0:T(8,128)S(1)}, f32[6,128,128]{2,1,0:T(8,128)}, u32[]{:S(2)}) copy-start(f32[6,128,128]{2,1,0:T(8,128)} %get-tuple-element.44) | copy-start | bytes 1179652
Sparse Core Ops, SparseCore 0:
  11.2 107.5 all-gather.1
  139.9 41.0 reduce-scatter.1

commit v9 on v8

--- a/solution.py
+++ b/solution.py
@@ -170,7 +170,8 @@
     return gq, gk, gv, total
 
 
-def gather_kernel(ny, ca, value_ref, w_ref, rows_ref, partial_ref, sendbuf, recvbuf, send_sem, recv_sem, bf_send, bf_recv, local_sem):
+def gather_kernel(ny, ca, value_ref, init_ref, q_ref, k_ref, v_ref, w_ref, rows_ref, normed_ref, att_ref, sh_ref,
+                  sendbuf, recvbuf, send_sem, recv_sem, bf_send, bf_recv, local_sem):
     me = lax.axis_index("seq")
     head = lax.axis_index("head")
     count = lax.axis_size("seq")
@@ -229,6 +230,28 @@
          (R.at[pl.ds(0, hz), yy(-1), :, B], R.at[pl.ds(0, hz), yy(-1), :, B], yr),
          (R.at[pl.ds(hz, nz - hz), yy(1), :, B], R.at[pl.ds(hz, nz - hz), yy(1), :, B], yl)],
     ]
+    heads, dim = sh_ref.shape[0], sh_ref.shape[2]
+    tokens = q_ref.shape[0]
+    causal = lax.broadcasted_iota(jnp.int32, (tokens, tokens), 1) <= lax.broadcasted_iota(jnp.int32, (tokens, tokens), 0)
+    nt = (((1,), (1,)), ((), ()))
+
+    def intra(h):
+        cols = pl.ds(h * dim, dim)
+        qh, kh = q_ref[:, cols], k_ref[:, cols]
+        aw = lax.dot_general(qh, kh, nt, preferred_element_type=jnp.float32)
+        aw = jnp.where(causal, aw, 0.0).astype(jnp.bfloat16)
+        att_ref[:, cols] = jnp.dot(aw, v_ref[:, cols], preferred_element_type=jnp.float32)
+
+    def finish(h):
+        cols = pl.ds(h * dim, dim)
+        a = att_ref[:, cols] + jnp.dot(q_ref[:, cols], sh_ref[h], preferred_element_type=jnp.float32)
+        att_ref[:, cols] = a
+        scale = lax.rsqrt(jnp.mean(a * a, axis=-1, keepdims=True) + EPS)
+        normed_ref[:, cols] = (a * scale).astype(normed_ref.dtype)
+
+    work = [[] for _ in ticks]
+    for h in range(heads):
+        work[min(h, 3)].append(h)
     total = value_ref[...]
     partial = jnp.zeros_like(total)
     n = 0
@@ -254,6 +277,12 @@
                 recv_sem=bf_recv.at[t], device_id=(partner, head), device_id_type=MESH,
             )
             scan.start()
+        for h in work[t]:
+            intra(h)
+        if t == rounds:
+            sh_ref[...] = (init_ref[...] + partial).astype(sh_ref.dtype)
+            for h in range(heads):
+                finish(h)
         for copy in started:
             copy.wait()
         if scan is not None:
@@ -261,24 +290,26 @@
             other = recvbuf[t].astype(jnp.float32)
             partial = jnp.where(bit == 1, partial + other, partial)
             total = sent.astype(jnp.float32) + other
-    partial_ref[...] = partial
-
-
-def gather_and_scan(value, weight):
+
+
+def gather_and_scan(value, init_state, query, key, val, weight):
     count = lax.axis_size("seq")
     ny = 4
     piece, cols = weight.shape
     rounds = count.bit_length() - 1
     ca = (cols * 2 // 3) // 128 * 128
     n_copies = 23
+    vmem = pl.BlockSpec(memory_space=pltpu.VMEM)
     return pl.pallas_call(
         functools.partial(gather_kernel, ny, ca),
         out_shape=(
             jax.ShapeDtypeStruct((count // ny, ny, piece, cols), weight.dtype),
-            jax.ShapeDtypeStruct(value.shape, jnp.float32),
+            jax.ShapeDtypeStruct(query.shape, jnp.bfloat16),
+            jax.ShapeDtypeStruct(query.shape, jnp.float32),
+            jax.ShapeDtypeStruct(value.shape, jnp.bfloat16),
         ),
-        in_specs=[pl.BlockSpec(memory_space=pltpu.VMEM), pl.BlockSpec(memory_space=pl.ANY)],
-        out_specs=(pl.BlockSpec(memory_space=pl.ANY), pl.BlockSpec(memory_space=pltpu.VMEM)),
+        in_specs=[vmem] * 5 + [pl.BlockSpec(memory_space=pl.ANY)],
+        out_specs=(pl.BlockSpec(memory_space=pl.ANY), vmem, vmem, vmem),
         scratch_shapes=[
             pltpu.VMEM((rounds,) + value.shape, jnp.bfloat16),
             pltpu.VMEM((rounds,) + value.shape, jnp.bfloat16),
@@ -289,7 +320,7 @@
             pltpu.SemaphoreType.DMA(()),
         ],
         compiler_params=pltpu.CompilerParams(collective_id=2, has_side_effects=True),
-    )(value.astype(jnp.float32), weight)
+    )(value.astype(jnp.float32), init_state, query, key, val, weight)
 
 
 def normalize(attended):
@@ -306,21 +337,11 @@
     val_rows = value.reshape(tok_rows, heads_here, head_dim)
     local_state = jnp.einsum("thi,thj->hij", key_rows, val_rows, preferred_element_type=jnp.float32)
     half = out_weight.shape[1] // 2
-    gathered, earlier = gather_and_scan(local_state, out_weight[:, :half])
+    gathered, normed, attended, state_half = gather_and_scan(
+        local_state, init_state, query, key, value, out_weight[:, :half]
+    )
     other_half = lax.all_gather(out_weight[:, half:], "seq", axis=0, tiled=True)
-    state_half = (init_state + earlier).astype(jnp.bfloat16)
-    row_index = lax.broadcasted_iota(jnp.int32, (tok_rows, tok_rows), 0)
-    col_index = lax.broadcasted_iota(jnp.int32, (tok_rows, tok_rows), 1)
-    causal = col_index <= row_index
-    scores = jnp.einsum("thi,shi->hts", queries, key_rows, preferred_element_type=jnp.float32)
-    attn_weights = jnp.where(causal, scores, 0.0).astype(jnp.bfloat16)
-    attended = jnp.einsum(
-        "hts,shj->thj", attn_weights, val_rows, preferred_element_type=jnp.float32
-    )
-    attended = attended + jnp.einsum(
-        "thi,hij->thj", queries, state_half, preferred_element_type=jnp.float32
-    )
-    normed = normalize(attended).astype(jnp.bfloat16).reshape(tok_rows, width)
+    attended = attended.reshape(tok_rows, heads_here, head_dim)
     first_rows = gathered.reshape(-1, half)
     weight_rows = jnp.concatenate([first_rows, other_half], axis=1)
     projected = jnp.dot(normed, weight_rows, preferred_element_type=jnp.float32).astype(jnp.bfloat16)

time: 207 us -> 223 us (1.077)
  local copies, waits for them, and re-layouts: 6.81 us -> 18.3 us
  Pallas kernels: 151 us -> 156 us
    dot_general x2 -> x0, matrix products: 5.33 us -> none  [the longest x1 3.76 us: shards(): jnp.einsum('hts,shj->thj', attn_weights, val_rows, preferred_element_type...]
    broadcast_in_dim x0 -> x2, local copies, waits for them, and re-layouts: none -> 4.5 us  [normalize(): jnp.mean(attended * attended, axis=-1, keepdims=True) + EPS]
    mul x0 -> x2, local copies, waits for them, and re-layouts: none -> 4.44 us  [normalize(): attended * lax.rsqrt(jnp.mean(attended * attended, axis=-1, keepdims=True...]
    pallas_call x1, Pallas kernels: 38.7 us -> 41.7 us  [backward_pass(): pl.pallas_call(backward_kernel, out_shape=(tokens, accs, accs, jax.ShapeD...]
    convert_element_type x1, other arithmetic: 0.43 us -> 3.25 us  [shards(): norm_back(grad_normed.reshape(tok_rows, heads_here, head_dim))[0]]
    pallas_call x1, Pallas kernels: 107 us -> 110 us  [gather_and_scan(): pl.pallas_call(functools.partial(gather_kernel, ny, ca), out_shape=(jax.S...]
    unnamed x12 -> x16, local copies, waits for them, and re-layouts: 3.88 us -> 5.26 us
  transfers between devices with their start and end apart: 2 -> 2, of which waited for: 0 -> 0; matrix products, arithmetic and copies ran while one was open for 13% -> 16% of each run, Pallas kernels for 73% -> 71%
where the time goes in v9:
time: 223 us; the launch traced here: 222 us
  Pallas kernels  156 us (70%)
  matrix products  29 us (13%)
  local copies, waits for them, and re-layouts  18.3 us (8%)
  between operations  14.1 us (6%)
  other arithmetic  3.7 us (2%)
    pallas_call x1, Pallas kernels, gather_and_scan(): pl.pallas_call(functools.partial(gather_kernel, ny, ca), out_shape=(jax.S...  110 us
    pallas_call x1, Pallas kernels, backward_pass(): pl.pallas_call(backward_kernel, out_shape=(tokens, accs, accs, jax.ShapeD...  41.7 us
    dot_general x1, matrix products, shards(): jnp.dot(normed, weight_rows, preferred_element_type=jnp.float32)  11.7 us
    dot_general x1, matrix products, shards(): lax.dot_general(out_grad[:, :half], first_rows, contract, preferred_eleme...  7.66 us
    dot_general x1, matrix products, shards(): lax.dot_general(out_grad[:, half:], other_half, contract, preferred_eleme...  5.97 us
    unnamed x16, local copies, waits for them, and re-layouts  5.26 us
    pallas_call x1, Pallas kernels, backward_pass(): pl.pallas_call(finish_kernel, out_shape=(tokens, tokens, tokens), in_spec...  4.58 us
    broadcast_in_dim x2, local copies, waits for them, and re-layouts, normalize(): jnp.mean(attended * attended, axis=-1, keepdims=True) + EPS  4.5 us
  transfers between devices with their start and end apart: 2, of which 0 were waited for; matrix products, arithmetic and copies ran while one was open for 16% of the time, Pallas kernels for 71%

profile of v9, /device:TPU:2, one launch (start us, length us, event | category | flops | bytes accessed | tf_op | source)
XLA Modules:
  0.0 221.5 jit_solution(15805068759286921446)
XLA Ops:
  7.2 1.8 fusion.20
  9.0 0.0 reduce-scatter.2.cloned.1.call-start
  9.1 1.4 copy.21
  10.5 0.3 copy.22
  10.8 1.1 fusion.21.value_ref
  11.9 110.0 %shard_map.101 = (bf16[8,4,24,3072]{3,2,1,0:T(8,128)(2,1)}, bf16[512,768]{1,0:T(8,128)(2,1)}, f32[512,768]{1,0:T(8,128)}, bf16[6,128,128]{2,1,0:T(8,128)(2,1)}) custom-call(f32[6,128,128]{2,1,0:T(8,128)} %fusion.21.value_ref, f32[6,128,128]{2,1,0:T(8,128)} %init_ref.1, bf16[512,768]{1,0:T(8,128)(2,1)} %q_ref.3, bf16[512,768]{1,0:T(8,128)(2,1)} %k_ref.5, ...), custom_call_target="tpu_custom_call" | custom-call | tf_op jit(solution)/shard_map/pallas_call | solution.py:303
  121.9 11.7 %fusion.4 = bf16[512,6144]{1,0:T(8,128)(2,1)} fusion(bf16[512,768]{1,0:T(8,128)(2,1)} %get-tuple-element.20, bf16[768,3072]{1,0:T(8,128)(2,1)} %all-gather.2.cloned.1.call-done, bf16[768,3072]{1,0:T(8,128)(2,1)} %bitcast.27), kind=kOutput, calls=%fused_computation.4 | convolution fusion | flops 4853858304 | bytes 16515072 | tf_op jit(solution)/shard_map/dot_general | solution.py:347
  133.7 1.1 copy-done.1
  134.8 1.2 copy.28
  135.9 0.5 copy-done.2
  136.5 0.5 copy.27
  136.9 6.0 %fusion.7 = f32[768,512]{0,1:T(8,128)S(1)} fusion(bf16[768,3072]{1,0:T(8,128)(2,1)} %all-gather.2.cloned.1.call-done, bf16[512,6144]{1,0:T(8,128)(2,1)} %param.11), kind=kOutput, calls=%fused_computation.5 | convolution fusion | flops 2415919104 | bytes 9437184 | tf_op jit(solution)/shard_map/dot_general | solution.py:352
  142.9 7.7 %add_bitcast_fusion = f32[512,768]{1,0:T(8,128)} fusion(f32[768,512]{0,1:T(8,128)S(1)} %fusion.7, bf16[768,3072]{1,0:T(8,128)(2,1)} %bitcast.28, bf16[512,6144]{1,0:T(8,128)(2,1)} %param.11), kind=kOutput, calls=%fused_computation.15 | convolution fusion | flops 2416312320 | bytes 11010048 | tf_op jit(solution)/shard_map/dot_general | solution.py:350
  150.6 1.9 copy.26
  152.5 0.4 multiply_reduce_fusion.1
  152.9 1.3 broadcast_in_dim.6
  154.3 3.2 %copy.32 = f32[512,768]{1,0:T(8,128)} copy(f32[512,768]{0,1:T(8,128)} %bitcast.22) | data formatting | bytes 3145728 | tf_op jit(solution)/shard_map/transpose(jvp())/broadcast_in_dim | solution.py:327
  157.4 1.4 mul.42
  158.8 3.1 %copy.31 = f32[512,768]{1,0:T(8,128)} copy(f32[512,768]{0,1:T(8,128)} %bitcast.23) | data formatting | bytes 3145728 | tf_op jit(solution)/shard_map/transpose(jvp())/mul | solution.py:327
  161.9 2.5 %convolution_bitcast_fusion.adj_ref = f32[6,128,128]{2,1,0:T(8,128)} fusion(bf16[512,6,128]{0,2,1:T(8,128)(2,1)} %bitcast.26, f32[512,6,128]{0,2,1:T(8,128)S(1)} %bitcast.19, f32[512,6,128]{0,2,1:T(8,128)S(1)} %bitcast.21, f32[512,6]{0,1:T(8,128)S(1)} %get-tuple-element.40, f32[512,6]{0,1:T(8,128)S(1)} %get-tuple-element.39), kind=kOutput, calls=%fused_computation.16 | convolution fusion | flops 102629376 | bytes 4349952 | tf_op jit(solution)/shard_map/thi,thj->hij/dot_general | solution.py:360
  164.4 3.3 %fusion.12.ga_ref = bf16[512,768]{1,0:T(8,128)(2,1)} fusion(f32[512,768]{1,0:T(8,128)S(1)} %copy-done.3, f32[512,768]{1,0:T(8,128)} %copy.32, f32[512,768]{1,0:T(8,128)S(1)} %copy-done.4, f32[512,768]{1,0:T(8,128)} %copy.31), kind=kLoop, calls=%fused_computation.12 | loop fusion | flops 1966080 | bytes 7077888 | tf_op jit(solution)/shard_map/convert_element_type | solution.py:357
  167.7 41.7 %shard_map.102 = (bf16[512,768]{1,0:T(8,128)(2,1)}, f32[512,768]{1,0:T(8,128)}, f32[512,768]{1,0:T(8,128)}, bf16[6,128,128]{2,1,0:T(8,128)(2,1)}, f32[6,128,128]{2,1,0:T(8,128)}) custom-call(f32[6,128,128]{2,1,0:T(8,128)} %convolution_bitcast_fusion.adj_ref, bf16[512,768]{1,0:T(8,128)(2,1)} %q_ref.3, bf16[512,768]{1,0:T(8,128)(2,1)} %k_ref.5, ...), custom_call_target="tpu_custom_call" | custom-call | tf_op jit(solution)/shard_map/pallas_call | solution.py:150
  209.4 4.6 %shard_map.103 = (bf16[512,768]{1,0:T(8,128)(2,1)}, bf16[512,768]{1,0:T(8,128)(2,1)}, bf16[512,768]{1,0:T(8,128)(2,1)}) custom-call(bf16[512,768]{1,0:T(8,128)(2,1)} %get-tuple-element.27.gq_in, f32[512,768]{1,0:T(8,128)} %get-tuple-element.28.gk_acc, f32[512,768]{1,0:T(8,128)} %get-tuple-element.29.gv_acc, bf16[512,768]{1,0:T(8,128)(2,1)} %v_ref.5, ...), custom_call_target="tpu_custom_call" | custom-call | tf_op jit(solution)/shard_map/pallas_call | solution.py:164
  214.0 0.7 copy.39
  (16 shorter events, 0.1 us)
Async XLA Ops:
  7.2 3.3 %copy-start = (bf16[512,768]{1,0:T(8,128)(2,1)S(1)}, bf16[512,768]{1,0:T(8,128)(2,1)}, u32[]{:S(2)}) copy-start(bf16[512,768]{1,0:T(8,128)(2,1)} %v_ref.5) | copy-start | bytes 2359300
  7.2 114.7 %all-gather.2.cloned.1.call-start = ((), (), s32[]{:S(2)}) async-start(), calls=%async_computation.1 | async-start | bytes 4866048 | tf_op jit(solution)/shard_map/all_gather | solution.py:343
  9.0 204.9 %reduce-scatter.2.cloned.1.call-start = ((), (), s32[]{:S(2)}) async-start(), calls=%async_computation.2 | async-start | bytes 7077888 | tf_op jit(solution)/shard_map/reduce_scatter | solution.py:353
  133.6 1.1 copy-start.1
  134.8 1.7 copy-start.2
  161.9 2.5 %copy-start.3 = (f32[512,768]{1,0:T(8,128)S(1)}, f32[512,768]{1,0:T(8,128)}, u32[]{:S(2)}) copy-start(f32[512,768]{1,0:T(8,128)} %get-tuple-element.25) | copy-start | bytes 4718596
  161.9 2.5 %copy-start.4 = (f32[512,768]{1,0:T(8,128)S(1)}, f32[512,768]{1,0:T(8,128)}, u32[]{:S(2)}) copy-start(f32[512,768]{1,0:T(8,128)} %add_bitcast_fusion) | copy-start | bytes 4718596
  209.4 4.6 %copy-start.5 = (f32[6,128,128]{2,1,0:T(8,128)S(1)}, f32[6,128,128]{2,1,0:T(8,128)}, u32[]{:S(2)}) copy-start(f32[6,128,128]{2,1,0:T(8,128)} %get-tuple-element.50) | copy-start | bytes 1179652
Sparse Core Ops, SparseCore 0:
  11.2 108.7 all-gather.1
  133.8 41.2 reduce-scatter.1

commit v10 on v6

--- a/solution.py
+++ b/solution.py
@@ -307,13 +307,16 @@
         "thi,hij->thj", queries, state_half, preferred_element_type=jnp.float32
     )
     normed = normalize(attended).astype(jnp.bfloat16).reshape(tok_rows, width)
-    weight_rows = jnp.concatenate([gathered.reshape(-1, half), other_half], axis=1)
-    projected = jnp.dot(normed, weight_rows, preferred_element_type=jnp.float32)
+    first_rows = gathered.reshape(-1, half)
+    weight_rows = jnp.concatenate([first_rows, other_half], axis=1)
+    projected = jnp.dot(normed, weight_rows, preferred_element_type=jnp.float32).astype(jnp.bfloat16)
+    projected, first_rows, other_half = lax.optimization_barrier((projected, first_rows, other_half))
+    contract = (((1,), (1,)), ((), ()))
     grad_normed = lax.dot_general(
-        out_grad, weight_rows, (((1,), (1,)), ((), ())), preferred_element_type=jnp.float32
-    )
+        out_grad[:, :half], first_rows, contract, preferred_element_type=jnp.float32
+    ) + lax.dot_general(out_grad[:, half:], other_half, contract, preferred_element_type=jnp.float32)
     mixed = lax.psum_scatter(
-        projected.astype(jnp.bfloat16), "head", scatter_dimension=1, tiled=True
+        projected, "head", scatter_dimension=1, tiled=True
     )
     _, norm_back = jax.vjp(normalize, attended)
     grad_att = norm_back(grad_normed.reshape(tok_rows, heads_here, head_dim))[0].astype(

time: 212 us -> 208 us (0.981)
  local copies, waits for them, and re-layouts: 14.1 us -> 11.9 us
    unnamed x13 -> x17, local copies, waits for them, and re-layouts: 11.2 us -> 8.97 us
    pallas_call x1, Pallas kernels: 40.5 us -> 38.3 us  [backward_pass(): pl.pallas_call(backward_kernel, out_shape=(tokens, tokens, tokens, jax.Sh...]
    dot_general x2 -> x3, matrix products: 21.9 us -> 22.7 us  [the longest x1 11.6 us: shards(): jnp.dot(normed, weight_rows, preferred_element_type=jnp.float32)]
  transfers between devices with their start and end apart: 2 -> 2, of which waited for: 0 -> 0; matrix products, arithmetic and copies ran while one was open for 5% -> 13% of each run, Pallas kernels for 70% -> 71%
where the time goes in v10:
time: 208 us; the launch traced here: 205 us
  Pallas kernels  146 us (70%)
  matrix products  30.2 us (15%)
  between operations  14.2 us (7%)
  local copies, waits for them, and re-layouts  11.9 us (6%)
  other arithmetic  2.98 us (1%)
    pallas_call x1, Pallas kernels, gather_and_scan(): pl.pallas_call(functools.partial(gather_kernel, ny, ca), out_shape=(jax.S...  107 us
    pallas_call x1, Pallas kernels, backward_pass(): pl.pallas_call(backward_kernel, out_shape=(tokens, tokens, tokens, jax.Sh...  38.3 us
    dot_general x1, matrix products, shards(): jnp.dot(normed, weight_rows, preferred_element_type=jnp.float32)  11.6 us
    unnamed x17, local copies, waits for them, and re-layouts  8.97 us
    dot_general x1, matrix products, shards(): lax.dot_general(out_grad[:, half:], other_half, contract, preferred_eleme...  5.65 us
    dot_general x1, matrix products, shards(): lax.dot_general(out_grad[:, :half], first_rows, contract, preferred_eleme...  5.48 us
  transfers between devices with their start and end apart: 2, of which 0 were waited for; matrix products, arithmetic and copies ran while one was open for 13% of the time, Pallas kernels for 71%

profile of v10, /device:TPU:2, one launch (start us, length us, event | category | flops | bytes accessed | tf_op | source)
XLA Modules:
  0.0 205.0 jit_solution(3822639577588655850)
XLA Ops:
  7.2 1.8 fusion.23
  9.0 0.0 reduce-scatter.2.cloned.1.call-start
  9.1 1.4 copy.19
  10.5 1.4 copy.20
  11.9 0.3 copy.21
  12.2 1.1 fusion.24.value_ref
  13.3 107.2 %shard_map.101 = (bf16[8,4,24,3072]{3,2,1,0:T(8,128)(2,1)}, f32[6,128,128]{2,1,0:T(8,128)}) custom-call(f32[6,128,128]{2,1,0:T(8,128)} %fusion.24.value_ref, bf16[24,3072]{1,0:T(8,128)(2,1)} %get-tuple-element.24.w_ref), custom_call_target="tpu_custom_call" | custom-call | tf_op jit(solution)/shard_map/pallas_call | solution.py:260
  120.6 0.8 iota_compare_fusion
  121.3 1.2 add_convert_fusion.sh_ref
  122.5 1.6 fusion.25
  124.1 3.8 %multiply_reduce_fusion.1 = (f32[512,6]{0,1:T(8,128)S(1)}, f32[512,6,128]{0,2,1:T(8,128)S(1)}) fusion(f32[6,128,512]{2,1,0:T(8,128)} %fusion.25, bf16[512,6,128]{0,2,1:T(8,128)(2,1)} %bitcast.36, pred[512,512]{1,0:T(8,128)(4,1)} %iota_compare_fusion, bf16[512,6,128]{0,2,1:T(8,128)(2,1)S(1)} %bitcast.28, bf16[512,6,128]{0,2,1:T(8,128)(2,1)S(1)} %bitcast.34), kind=kOutput, calls=%fused_computation.19 | convolution fusion | flops 809628672 | bytes 5779456 | tf_op jit(solution)/shard_map/hts,shj->thj/dot_general | solution.py:303
  127.9 0.2 multiply_convert_fusion
  128.1 11.6 %fusion.4 = bf16[512,6144]{1,0:T(8,128)(2,1)} fusion(bf16[512,768]{0,1:T(8,128)(2,1)S(1)} %bitcast.37, bf16[768,3072]{1,0:T(8,128)(2,1)} %all-gather.2.cloned.1.call-done, bf16[768,3072]{1,0:T(8,128)(2,1)} %bitcast.38), kind=kOutput, calls=%fused_computation.4 | convolution fusion | flops 4853858304 | bytes 16515072 | tf_op jit(solution)/shard_map/dot_general | solution.py:312
  139.7 5.7 %fusion.8 = f32[768,512]{1,0:T(8,128)S(1)} fusion(bf16[768,3072]{1,0:T(8,128)(2,1)} %all-gather.2.cloned.1.call-done, bf16[512,6144]{1,0:T(8,128)(2,1)} %param.11), kind=kOutput, calls=%fused_computation.7 | convolution fusion | flops 2415919104 | bytes 9437184 | tf_op jit(solution)/shard_map/dot_general | solution.py:317
  145.4 5.5 %fusion.17 = f32[768,512]{1,0:T(8,128)S(1)} fusion(f32[768,512]{1,0:T(8,128)S(1)} %fusion.8, bf16[768,3072]{1,0:T(8,128)(2,1)} %bitcast.39, bf16[512,6144]{1,0:T(8,128)(2,1)} %param.11), kind=kOutput, calls=%fused_computation.20 | convolution fusion | flops 2416312320 | bytes 11010048 | tf_op jit(solution)/shard_map/dot_general | solution.py:315
  150.8 0.4 multiply_reduce_fusion
  151.3 0.4 fusion.16
  151.7 1.2 copy.27.ga_ref
  152.9 1.1 convolution_bitcast_fusion.adj_ref
  154.0 38.3 %shard_map.102 = (bf16[512,768]{1,0:T(8,128)(2,1)}, bf16[512,768]{1,0:T(8,128)(2,1)}, bf16[512,768]{1,0:T(8,128)(2,1)}, f32[6,128,128]{2,1,0:T(8,128)}) custom-call(f32[6,128,128]{2,1,0:T(8,128)} %convolution_bitcast_fusion.adj_ref, bf16[512,768]{1,0:T(8,128)(2,1)} %q_ref.1, bf16[512,768]{1,0:T(8,128)(2,1)} %k_ref.1, bf16[512,768]{1,0:T(8,128)(2,1)} %v_ref.1, ...), custom_call_target="tpu_custom_call" | custom-call | tf_op jit(solution)/shard_map/pallas_call | solution.py:142
  192.3 2.2 %copy.37 = bf16[512,768]{1,0:T(8,128)(2,1)} copy(bf16[512,768]{1,0:T(8,128)(2,1)} %get-tuple-element.33) | data formatting | bytes 1572864
  194.5 2.1 %copy.38 = bf16[512,768]{1,0:T(8,128)(2,1)} copy(bf16[512,768]{1,0:T(8,128)(2,1)} %get-tuple-element.34) | data formatting | bytes 1572864
  196.5 0.9 copy.39
  197.4 0.7 copy.40
  (17 shorter events, 0.2 us)
Async XLA Ops:
  7.2 4.7 %copy-start = (bf16[512,768]{1,0:T(8,128)(2,1)S(1)}, bf16[512,768]{1,0:T(8,128)(2,1)}, u32[]{:S(2)}) copy-start(bf16[512,768]{1,0:T(8,128)(2,1)} %v_ref.1) | copy-start | bytes 2359300
  7.2 120.9 %all-gather.2.cloned.1.call-start = ((), (), s32[]{:S(2)}) async-start(), calls=%async_computation.1 | async-start | bytes 4866048 | tf_op jit(solution)/shard_map/all_gather | solution.py:296
  9.0 183.3 %reduce-scatter.2.cloned.1.call-start = ((), (), s32[]{:S(2)}) async-start(), calls=%async_computation.2 | async-start | bytes 7077888 | tf_op jit(solution)/shard_map/reduce_scatter | solution.py:318
  12.2 110.3 %copy-start.1 = (bf16[512,768]{0,1:T(8,128)(2,1)}, bf16[512,768]{0,1:T(8,128)(2,1)S(1)}, u32[]{:S(2)}) copy-start(bf16[512,768]{0,1:T(8,128)(2,1)S(1)} %copy.21) | copy-start | bytes 2359300
  122.5 5.4 %copy-start.2 = (bf16[6,128,128]{2,1,0:T(8,128)(2,1)}, bf16[6,128,128]{2,1,0:T(8,128)(2,1)S(1)}, u32[]{:S(2)}) copy-start(bf16[6,128,128]{2,1,0:T(8,128)(2,1)S(1)} %add_convert_fusion.sh_ref) | copy-start | bytes 589828
  192.3 4.3 %copy-start.3 = (bf16[512,768]{1,0:T(8,128)(2,1)S(1)}, bf16[512,768]{1,0:T(8,128)(2,1)}, u32[]{:S(2)}) copy-start(bf16[512,768]{1,0:T(8,128)(2,1)} %get-tuple-element.35) | copy-start | bytes 2359300
  192.3 5.1 %copy-start.4 = (f32[6,128,128]{2,1,0:T(8,128)S(1)}, f32[6,128,128]{2,1,0:T(8,128)}, u32[]{:S(2)}) copy-start(f32[6,128,128]{2,1,0:T(8,128)} %get-tuple-element.36) | copy-start | bytes 1179652
Sparse Core Ops, SparseCore 0:
  11.2 107.7 all-gather.1
  139.8 40.6 reduce-scatter.1

commit v11 on v8

--- a/solution.py
+++ b/solution.py
@@ -322,8 +322,10 @@
     )
     normed = normalize(attended).astype(jnp.bfloat16).reshape(tok_rows, width)
     first_rows = gathered.reshape(-1, half)
-    weight_rows = jnp.concatenate([first_rows, other_half], axis=1)
-    projected = jnp.dot(normed, weight_rows, preferred_element_type=jnp.float32).astype(jnp.bfloat16)
+    projected = jnp.concatenate([
+        jnp.dot(normed, first_rows, preferred_element_type=jnp.float32).astype(jnp.bfloat16),
+        jnp.dot(normed, other_half, preferred_element_type=jnp.float32).astype(jnp.bfloat16),
+    ], axis=1)
     projected, first_rows, other_half = lax.optimization_barrier((projected, first_rows, other_half))
     contract = (((1,), (1,)), ((), ()))
     grad_normed = lax.dot_general(

time: 207 us -> 210 us (1.014)
  other arithmetic: 2.98 us -> 6.2 us
    concatenate x0 -> x1, other arithmetic: none -> 3.22 us  [shards(): jnp.concatenate([jnp.dot(normed, first_rows, preferred_element_type=jnp.f...]
    dot_general x1 -> x2, matrix products: 11.6 us -> 11.7 us  [the longest x1 6.38 us: shards(): jnp.dot(normed, first_rows, preferred_element_type=jnp.float32)]
  transfers between devices with their start and end apart: 2 -> 2, of which waited for: 0 -> 0; matrix products, arithmetic and copies ran while one was open for 13% -> 15% of each run, Pallas kernels for 73% -> 72%
where the time goes in v11:
time: 210 us; the launch traced here: 208 us
  Pallas kernels  151 us (72%)
  matrix products  30.4 us (14%)
  between operations  14.2 us (7%)
  local copies, waits for them, and re-layouts  6.81 us (3%)
  other arithmetic  6.2 us (3%)
    pallas_call x1, Pallas kernels, gather_and_scan(): pl.pallas_call(functools.partial(gather_kernel, ny, ca), out_shape=(jax.S...  107 us
    pallas_call x1, Pallas kernels, backward_pass(): pl.pallas_call(backward_kernel, out_shape=(tokens, accs, accs, jax.ShapeD...  38.7 us
    dot_general x1, matrix products, shards(): jnp.dot(normed, first_rows, preferred_element_type=jnp.float32)  6.38 us
    dot_general x1, matrix products, shards(): lax.dot_general(out_grad[:, :half], first_rows, contract, preferred_eleme...  5.66 us
    dot_general x1, matrix products, shards(): lax.dot_general(out_grad[:, half:], other_half, contract, preferred_eleme...  5.47 us
    dot_general x1, matrix products, shards(): jnp.dot(normed, other_half, preferred_element_type=jnp.float32)  5.36 us
    pallas_call x1, Pallas kernels, backward_pass(): pl.pallas_call(finish_kernel, out_shape=(tokens, tokens, tokens), in_spec...  4.58 us
  transfers between devices with their start and end apart: 2, of which 0 were waited for; matrix products, arithmetic and copies ran while one was open for 15% of the time, Pallas kernels for 72%

profile of v11, /device:TPU:2, one launch (start us, length us, event | category | flops | bytes accessed | tf_op | source)
XLA Modules:
  0.0 208.3 jit_solution(16861165630515975007)
XLA Ops:
  7.2 1.8 fusion.15
  9.0 0.0 reduce-scatter.2.cloned.1.call-start
  9.1 1.4 copy.19
  10.5 1.4 copy.20
  11.9 0.3 copy.21
  12.2 1.1 fusion.16.value_ref
  13.3 107.3 %shard_map.101 = (bf16[8,4,24,3072]{3,2,1,0:T(8,128)(2,1)}, f32[6,128,128]{2,1,0:T(8,128)}) custom-call(f32[6,128,128]{2,1,0:T(8,128)} %fusion.16.value_ref, bf16[24,3072]{1,0:T(8,128)(2,1)} %get-tuple-element.32.w_ref), custom_call_target="tpu_custom_call" | custom-call | tf_op jit(solution)/shard_map/pallas_call | solution.py:274
  120.6 0.8 iota_compare_fusion
  121.4 1.2 add_convert_fusion.sh_ref
  122.6 1.6 fusion.17
  124.2 3.8 %multiply_reduce_fusion.1 = (f32[512,6]{0,1:T(8,128)S(1)}, f32[512,6,128]{0,2,1:T(8,128)S(1)}) fusion(f32[6,128,512]{2,1,0:T(8,128)} %fusion.17, bf16[512,6,128]{0,2,1:T(8,128)(2,1)} %bitcast.39, pred[512,512]{1,0:T(8,128)(4,1)} %iota_compare_fusion, bf16[512,6,128]{0,2,1:T(8,128)(2,1)S(1)} %bitcast.31, bf16[512,6,128]{0,2,1:T(8,128)(2,1)S(1)} %bitcast.37), kind=kOutput, calls=%fused_computation.17 | convolution fusion | flops 809628672 | bytes 5779456 | tf_op jit(solution)/shard_map/hts,shj->thj/dot_general | solution.py:317
  128.0 0.2 multiply_convert_fusion
  128.2 6.4 %convolution_convert_fusion.1 = bf16[512,3072]{1,0:T(8,128)(2,1)} fusion(bf16[512,768]{0,1:T(8,128)(2,1)S(1)} %bitcast.40, bf16[768,3072]{1,0:T(8,128)(2,1)} %bitcast.42), kind=kOutput, calls=%fused_computation.3 | convolution fusion | flops 2417491968 | bytes 8650752 | tf_op jit(solution)/shard_map/dot_general | solution.py:326
  134.5 5.4 %convolution_convert_fusion = bf16[512,3072]{1,0:T(8,128)(2,1)S(1)} fusion(bf16[512,768]{0,1:T(8,128)(2,1)S(1)} %bitcast.41, bf16[768,3072]{1,0:T(8,128)(2,1)} %all-gather.2.cloned.1.call-done), kind=kOutput, calls=%fused_computation.2 | convolution fusion | flops 2417491968 | bytes 8650752 | tf_op jit(solution)/shard_map/dot_general | solution.py:327
  139.9 3.2 %pad_maximum_fusion = bf16[512,6144]{1,0:T(8,128)(2,1)} fusion(bf16[512,3072]{1,0:T(8,128)(2,1)S(1)} %convolution_convert_fusion, bf16[512,3072]{1,0:T(8,128)(2,1)S(1)} %copy-done.2), kind=kLoop, calls=%fused_computation | loop fusion | flops 12582912 | bytes 12582912 | tf_op jit(solution)/shard_map/concatenate | solution.py:325
  143.2 5.5 %fusion.1 = f32[768,512]{1,0:T(8,128)S(1)} fusion(bf16[768,3072]{1,0:T(8,128)(2,1)} %all-gather.2.cloned.1.call-done, bf16[512,6144]{1,0:T(8,128)(2,1)} %param.11), kind=kOutput, calls=%fused_computation.5 | convolution fusion | flops 2415919104 | bytes 9437184 | tf_op jit(solution)/shard_map/dot_general | solution.py:333
  148.6 5.7 %fusion.10 = f32[768,512]{1,0:T(8,128)S(1)} fusion(f32[768,512]{1,0:T(8,128)S(1)} %fusion.1, bf16[768,3072]{1,0:T(8,128)(2,1)} %bitcast.43, bf16[512,6144]{1,0:T(8,128)(2,1)} %param.11), kind=kOutput, calls=%fused_computation.18 | convolution fusion | flops 2416312320 | bytes 11010048 | tf_op jit(solution)/shard_map/dot_general | solution.py:331
  154.3 0.4 multiply_reduce_fusion
  154.7 0.4 fusion.9
  155.2 1.2 copy.27.ga_ref
  156.3 1.1 convolution_bitcast_fusion.adj_ref
  157.4 38.7 %shard_map.102 = (bf16[512,768]{1,0:T(8,128)(2,1)}, f32[512,768]{1,0:T(8,128)}, f32[512,768]{1,0:T(8,128)}, bf16[6,128,128]{2,1,0:T(8,128)(2,1)}, f32[6,128,128]{2,1,0:T(8,128)}) custom-call(f32[6,128,128]{2,1,0:T(8,128)} %convolution_bitcast_fusion.adj_ref, bf16[512,768]{1,0:T(8,128)(2,1)} %q_ref.1, bf16[512,768]{1,0:T(8,128)(2,1)} %k_ref.3, ...), custom_call_target="tpu_custom_call" | custom-call | tf_op jit(solution)/shard_map/pallas_call | solution.py:150
  196.1 4.6 %shard_map.103 = (bf16[512,768]{1,0:T(8,128)(2,1)}, bf16[512,768]{1,0:T(8,128)(2,1)}, bf16[512,768]{1,0:T(8,128)(2,1)}) custom-call(bf16[512,768]{1,0:T(8,128)(2,1)} %get-tuple-element.23.gq_in, f32[512,768]{1,0:T(8,128)} %get-tuple-element.24.gk_acc, f32[512,768]{1,0:T(8,128)} %get-tuple-element.25.gv_acc, bf16[512,768]{1,0:T(8,128)(2,1)} %v_ref.3, ...), custom_call_target="tpu_custom_call" | custom-call | tf_op jit(solution)/shard_map/pallas_call | solution.py:164
  200.7 0.7 copy.34
  (17 shorter events, 0.1 us)
Async XLA Ops:
  7.2 4.7 %copy-start = (bf16[512,768]{1,0:T(8,128)(2,1)S(1)}, bf16[512,768]{1,0:T(8,128)(2,1)}, u32[]{:S(2)}) copy-start(bf16[512,768]{1,0:T(8,128)(2,1)} %v_ref.3) | copy-start | bytes 2359300
  7.2 127.4 %all-gather.2.cloned.1.call-start = ((), (), s32[]{:S(2)}) async-start(), calls=%async_computation.1 | async-start | bytes 4866048 | tf_op jit(solution)/shard_map/all_gather | solution.py:310
  9.0 191.7 %reduce-scatter.2.cloned.1.call-start = ((), (), s32[]{:S(2)}) async-start(), calls=%async_computation.2 | async-start | bytes 7077888 | tf_op jit(solution)/shard_map/reduce_scatter | solution.py:334
  12.2 110.4 %copy-start.1 = (bf16[512,768]{0,1:T(8,128)(2,1)}, bf16[512,768]{0,1:T(8,128)(2,1)S(1)}, u32[]{:S(2)}) copy-start(bf16[512,768]{0,1:T(8,128)(2,1)S(1)} %copy.21) | copy-start | bytes 2359300
  122.6 5.4 %copy-start.3 = (bf16[6,128,128]{2,1,0:T(8,128)(2,1)}, bf16[6,128,128]{2,1,0:T(8,128)(2,1)S(1)}, u32[]{:S(2)}) copy-start(bf16[6,128,128]{2,1,0:T(8,128)(2,1)S(1)} %add_convert_fusion.sh_ref) | copy-start | bytes 589828
  134.5 5.4 %copy-start.2 = (bf16[512,3072]{1,0:T(8,128)(2,1)S(1)}, bf16[512,3072]{1,0:T(8,128)(2,1)}, u32[]{:S(2)}) copy-start(bf16[512,3072]{1,0:T(8,128)(2,1)} %convolution_convert_fusion.1) | copy-start | bytes 9437188
  196.1 4.6 %copy-start.4 = (f32[6,128,128]{2,1,0:T(8,128)S(1)}, f32[6,128,128]{2,1,0:T(8,128)}, u32[]{:S(2)}) copy-start(f32[6,128,128]{2,1,0:T(8,128)} %get-tuple-element.44) | copy-start | bytes 1179652
Sparse Core Ops, SparseCore 0:
  11.2 107.5 all-gather.1
  143.3 41.0 reduce-scatter.1

commit v12 on v8

--- a/solution.py
+++ b/solution.py
@@ -70,8 +70,12 @@
     )(value.astype(jnp.float32))
 
 
-def backward_kernel(adj_ref, q_ref, k_ref, v_ref, ga_ref, sh_ref, gq_ref, gk_acc, gv_acc, later_ref, total_ref,
-                    sendbuf, recvbuf, send_sem, recv_sem):
+def backward_kernel(adj_ref, q_hbm, k_hbm, v_hbm, ga_hbm, sh_ref, gq_ref, gk_acc, gv_acc, later_ref, total_ref,
+                    sendbuf, recvbuf, send_sem, recv_sem, q_ref, k_ref, v_ref, ga_ref, load_sem):
+    loads = [pltpu.make_async_copy(src, dst, load_sem.at[i])
+             for i, (src, dst) in enumerate([(q_hbm, q_ref), (k_hbm, k_ref), (v_hbm, v_ref), (ga_hbm, ga_ref)])]
+    for load in loads:
+        load.start()
     me = lax.axis_index("seq")
     head = lax.axis_index("head")
     count = lax.axis_size("seq")
@@ -118,6 +122,9 @@
             recv_sem=recv_sem.at[t], device_id=(partner, head), device_id_type=MESH,
         )
         copy.start()
+        if t == 0:
+            for load in loads:
+                load.wait()
         for h in order[t]:
             head_work(h)
         copy.wait()
@@ -151,14 +158,14 @@
         backward_kernel,
         out_shape=(tokens, accs, accs, jax.ShapeDtypeStruct(own_adjoint.shape, jnp.bfloat16),
                    jax.ShapeDtypeStruct(own_adjoint.shape, jnp.float32)),
-        in_specs=[vmem] * 6,
+        in_specs=[vmem] + [pl.BlockSpec(memory_space=pl.ANY)] * 4 + [vmem],
         out_specs=(vmem,) * 5,
         scratch_shapes=[
             pltpu.VMEM((rounds,) + own_adjoint.shape, jnp.bfloat16),
             pltpu.VMEM((rounds,) + own_adjoint.shape, jnp.bfloat16),
             pltpu.SemaphoreType.DMA((rounds,)),
             pltpu.SemaphoreType.DMA((rounds,)),
-        ],
+        ] + [pltpu.VMEM(query.shape, jnp.bfloat16)] * 4 + [pltpu.SemaphoreType.DMA((4,))],
         compiler_params=pltpu.CompilerParams(collective_id=1, has_side_effects=True),
     )(own_adjoint, query, key, value, grad_att, state_half)
     gq, gk, gv = pl.pallas_call(

time: 207 us -> 206 us (level)
  no operation moved by 1% of the time
where the time goes in v12:
time: 206 us; the launch traced here: 204 us
  Pallas kernels  150 us (73%)
  matrix products  30.2 us (15%)
  between operations  14.2 us (7%)
  local copies, waits for them, and re-layouts  6.81 us (3%)
  other arithmetic  2.98 us (1%)
    pallas_call x1, Pallas kernels, gather_and_scan(): pl.pallas_call(functools.partial(gather_kernel, ny, ca), out_shape=(jax.S...  107 us
    pallas_call x1, Pallas kernels, backward_pass(): pl.pallas_call(backward_kernel, out_shape=(tokens, accs, accs, jax.ShapeD...  37.8 us
    dot_general x1, matrix products, shards(): jnp.dot(normed, weight_rows, preferred_element_type=jnp.float32)  11.6 us
    dot_general x1, matrix products, shards(): lax.dot_general(out_grad[:, half:], other_half, contract, preferred_eleme...  5.65 us
    dot_general x1, matrix products, shards(): lax.dot_general(out_grad[:, :half], first_rows, contract, preferred_eleme...  5.48 us
    pallas_call x1, Pallas kernels, backward_pass(): pl.pallas_call(finish_kernel, out_shape=(tokens, tokens, tokens), in_spec...  4.58 us
  transfers between devices with their start and end apart: 2, of which 0 were waited for; matrix products, arithmetic and copies ran while one was open for 13% of the time, Pallas kernels for 73%

profile of v12, /device:TPU:2, one launch (start us, length us, event | category | flops | bytes accessed | tf_op | source)
XLA Modules:
  0.0 204.1 jit_solution(2343323106267200049)
XLA Ops:
  7.2 0.0 all-gather.2.cloned.1.call-start
  7.2 1.8 fusion.23
  9.0 0.0 reduce-scatter.2.cloned.1.call-start
  9.1 1.4 copy.19
  10.5 1.4 copy.20
  11.9 0.3 copy.21
  12.2 1.1 fusion.24.value_ref
  13.3 107.3 %shard_map.101 = (bf16[8,4,24,3072]{3,2,1,0:T(8,128)(2,1)}, f32[6,128,128]{2,1,0:T(8,128)}) custom-call(f32[6,128,128]{2,1,0:T(8,128)} %fusion.24.value_ref, bf16[24,3072]{1,0:T(8,128)(2,1)} %get-tuple-element.32.w_ref), custom_call_target="tpu_custom_call" | custom-call | tf_op jit(solution)/shard_map/pallas_call | solution.py:281
  120.6 0.8 iota_compare_fusion
  121.4 1.2 add_convert_fusion.sh_ref
  122.6 1.6 fusion.25
  124.2 3.8 %multiply_reduce_fusion.1 = (f32[512,6]{0,1:T(8,128)S(1)}, f32[512,6,128]{0,2,1:T(8,128)S(1)}) fusion(f32[6,128,512]{2,1,0:T(8,128)} %fusion.25, bf16[512,6,128]{0,2,1:T(8,128)(2,1)} %bitcast.36, pred[512,512]{1,0:T(8,128)(4,1)} %iota_compare_fusion, bf16[512,6,128]{0,2,1:T(8,128)(2,1)S(1)} %bitcast.28, bf16[512,6,128]{0,2,1:T(8,128)(2,1)S(1)} %bitcast.34), kind=kOutput, calls=%fused_computation.19 | convolution fusion | flops 809628672 | bytes 5779456 | tf_op jit(solution)/shard_map/hts,shj->thj/dot_general | solution.py:324
  128.0 0.2 multiply_convert_fusion
  128.2 0.0 all-gather.2.cloned.1.call-done
  128.2 11.6 %fusion.4 = bf16[512,6144]{1,0:T(8,128)(2,1)} fusion(bf16[512,768]{0,1:T(8,128)(2,1)S(1)} %bitcast.37, bf16[768,3072]{1,0:T(8,128)(2,1)} %all-gather.2.cloned.1.call-done, bf16[768,3072]{1,0:T(8,128)(2,1)} %bitcast.38), kind=kOutput, calls=%fused_computation.4 | convolution fusion | flops 4853858304 | bytes 16515072 | tf_op jit(solution)/shard_map/dot_general | solution.py:333
  139.8 5.7 %fusion.8 = f32[768,512]{1,0:T(8,128)S(1)} fusion(bf16[768,3072]{1,0:T(8,128)(2,1)} %all-gather.2.cloned.1.call-done, bf16[512,6144]{1,0:T(8,128)(2,1)} %param.11), kind=kOutput, calls=%fused_computation.7 | convolution fusion | flops 2415919104 | bytes 9437184 | tf_op jit(solution)/shard_map/dot_general | solution.py:338
  145.5 5.5 %fusion.17 = f32[768,512]{1,0:T(8,128)S(1)} fusion(f32[768,512]{1,0:T(8,128)S(1)} %fusion.8, bf16[768,3072]{1,0:T(8,128)(2,1)} %bitcast.39, bf16[512,6144]{1,0:T(8,128)(2,1)} %param.11), kind=kOutput, calls=%fused_computation.20 | convolution fusion | flops 2416312320 | bytes 11010048 | tf_op jit(solution)/shard_map/dot_general | solution.py:336
  150.9 0.4 multiply_reduce_fusion
  151.3 0.4 fusion.16
  151.8 1.2 copy.27.ga_hbm
  152.9 1.1 convolution_bitcast_fusion.adj_ref
  154.0 37.8 %shard_map.102 = (bf16[512,768]{1,0:T(8,128)(2,1)}, f32[512,768]{1,0:T(8,128)}, f32[512,768]{1,0:T(8,128)}, bf16[6,128,128]{2,1,0:T(8,128)(2,1)}, f32[6,128,128]{2,1,0:T(8,128)}) custom-call(f32[6,128,128]{2,1,0:T(8,128)} %convolution_bitcast_fusion.adj_ref, bf16[512,768]{1,0:T(8,128)(2,1)} %q_hbm.1, bf16[512,768]{1,0:T(8,128)(2,1)} %k_ref.1, ...), custom_call_target="tpu_custom_call" | custom-call | tf_op jit(solution)/shard_map/pallas_call | solution.py:157
  191.9 4.6 %shard_map.103 = (bf16[512,768]{1,0:T(8,128)(2,1)}, bf16[512,768]{1,0:T(8,128)(2,1)}, bf16[512,768]{1,0:T(8,128)(2,1)}) custom-call(bf16[512,768]{1,0:T(8,128)(2,1)} %get-tuple-element.23.gq_in, f32[512,768]{1,0:T(8,128)} %get-tuple-element.24.gk_acc, f32[512,768]{1,0:T(8,128)} %get-tuple-element.25.gv_acc, bf16[512,768]{1,0:T(8,128)(2,1)} %v_ref.1, ...), custom_call_target="tpu_custom_call" | custom-call | tf_op jit(solution)/shard_map/pallas_call | solution.py:171
  196.5 0.7 copy.34
  (13 shorter events, 0.1 us)
Async XLA Ops:
  7.2 4.7 %copy-start = (bf16[512,768]{1,0:T(8,128)(2,1)S(1)}, bf16[512,768]{1,0:T(8,128)(2,1)}, u32[]{:S(2)}) copy-start(bf16[512,768]{1,0:T(8,128)(2,1)} %v_ref.1) | copy-start | bytes 2359300
  7.2 121.0 %all-gather.2.cloned.1.call-start = ((), (), s32[]{:S(2)}) async-start(), calls=%async_computation.1 | async-start | bytes 4866048 | tf_op jit(solution)/shard_map/all_gather | solution.py:317
  9.0 187.5 %reduce-scatter.2.cloned.1.call-start = ((), (), s32[]{:S(2)}) async-start(), calls=%async_computation.2 | async-start | bytes 7077888 | tf_op jit(solution)/shard_map/reduce_scatter | solution.py:339
  12.2 110.4 %copy-start.1 = (bf16[512,768]{0,1:T(8,128)(2,1)}, bf16[512,768]{0,1:T(8,128)(2,1)S(1)}, u32[]{:S(2)}) copy-start(bf16[512,768]{0,1:T(8,128)(2,1)S(1)} %copy.21) | copy-start | bytes 2359300
  122.6 5.4 %copy-start.2 = (bf16[6,128,128]{2,1,0:T(8,128)(2,1)}, bf16[6,128,128]{2,1,0:T(8,128)(2,1)S(1)}, u32[]{:S(2)}) copy-start(bf16[6,128,128]{2,1,0:T(8,128)(2,1)S(1)} %add_convert_fusion.sh_ref) | copy-start | bytes 589828
  191.9 4.6 %copy-start.3 = (f32[6,128,128]{2,1,0:T(8,128)S(1)}, f32[6,128,128]{2,1,0:T(8,128)}, u32[]{:S(2)}) copy-start(f32[6,128,128]{2,1,0:T(8,128)} %get-tuple-element.44) | copy-start | bytes 1179652
Sparse Core Ops, SparseCore 0:
  11.2 107.5 all-gather.1
  139.9 41.0 reduce-scatter.1

commit v13 on v12

--- a/solution.py
+++ b/solution.py
@@ -70,8 +70,9 @@
     )(value.astype(jnp.float32))
 
 
-def backward_kernel(adj_ref, q_hbm, k_hbm, v_hbm, ga_hbm, sh_ref, gq_ref, gk_acc, gv_acc, later_ref, total_ref,
-                    sendbuf, recvbuf, send_sem, recv_sem, q_ref, k_ref, v_ref, ga_ref, load_sem):
+def backward_kernel(adj_ref, q_hbm, k_hbm, v_hbm, ga_hbm, sh_ref, gq_hbm, gk_hbm, gv_hbm, later_ref, total_ref,
+                    sendbuf, recvbuf, send_sem, recv_sem, q_ref, k_ref, v_ref, ga_ref, load_sem,
+                    gq_ref, gk_acc, gv_acc, store_sem):
     loads = [pltpu.make_async_copy(src, dst, load_sem.at[i])
              for i, (src, dst) in enumerate([(q_hbm, q_ref), (k_hbm, k_ref), (v_hbm, v_ref), (ga_hbm, ga_ref)])]
     for load in loads:
@@ -127,12 +128,19 @@
                 load.wait()
         for h in order[t]:
             head_work(h)
+        if t == rounds - 1:
+            stores = [pltpu.make_async_copy(src, dst, store_sem.at[i])
+                      for i, (src, dst) in enumerate([(gq_ref, gq_hbm), (gk_acc, gk_hbm), (gv_acc, gv_hbm)])]
+            for store in stores:
+                store.start()
         copy.wait()
         other = recvbuf[t].astype(jnp.float32)
         partial = jnp.where(bit == 0, partial + other, partial)
         total = sent.astype(jnp.float32) + other
     total_ref[...] = total
     later_ref[...] = partial.astype(later_ref.dtype)
+    for store in stores:
+        store.wait()
 
 
 def finish_kernel(gq_in, gk_acc, gv_acc, v_ref, k_ref, later_ref, gq_ref, gk_ref, gv_ref):
@@ -159,13 +167,15 @@
         out_shape=(tokens, accs, accs, jax.ShapeDtypeStruct(own_adjoint.shape, jnp.bfloat16),
                    jax.ShapeDtypeStruct(own_adjoint.shape, jnp.float32)),
         in_specs=[vmem] + [pl.BlockSpec(memory_space=pl.ANY)] * 4 + [vmem],
-        out_specs=(vmem,) * 5,
+        out_specs=(pl.BlockSpec(memory_space=pl.ANY),) * 3 + (vmem, vmem),
         scratch_shapes=[
             pltpu.VMEM((rounds,) + own_adjoint.shape, jnp.bfloat16),
             pltpu.VMEM((rounds,) + own_adjoint.shape, jnp.bfloat16),
             pltpu.SemaphoreType.DMA((rounds,)),
             pltpu.SemaphoreType.DMA((rounds,)),
-        ] + [pltpu.VMEM(query.shape, jnp.bfloat16)] * 4 + [pltpu.SemaphoreType.DMA((4,))],
+        ] + [pltpu.VMEM(query.shape, jnp.bfloat16)] * 4 + [pltpu.SemaphoreType.DMA((4,))]
+        + [pltpu.VMEM(query.shape, jnp.bfloat16), pltpu.VMEM(query.shape, jnp.float32),
+           pltpu.VMEM(query.shape, jnp.float32), pltpu.SemaphoreType.DMA((3,))],
         compiler_params=pltpu.CompilerParams(collective_id=1, has_side_effects=True),
     )(own_adjoint, query, key, value, grad_att, state_half)
     gq, gk, gv = pl.pallas_call(

time: 206 us -> 205 us (level)
  no operation moved by 1% of the time
where the time goes in v13:
time: 205 us; the launch traced here: 203 us
  Pallas kernels  149 us (73%)
  matrix products  30.2 us (15%)
  between operations  14.2 us (7%)
  local copies, waits for them, and re-layouts  6.81 us (3%)
  other arithmetic  2.98 us (1%)
    pallas_call x1, Pallas kernels, gather_and_scan(): pl.pallas_call(functools.partial(gather_kernel, ny, ca), out_shape=(jax.S...  107 us
    pallas_call x1, Pallas kernels, backward_pass(): pl.pallas_call(backward_kernel, out_shape=(tokens, accs, accs, jax.ShapeD...  36.6 us
    dot_general x1, matrix products, shards(): jnp.dot(normed, weight_rows, preferred_element_type=jnp.float32)  11.6 us
    dot_general x1, matrix products, shards(): lax.dot_general(out_grad[:, half:], other_half, contract, preferred_eleme...  5.65 us
    dot_general x1, matrix products, shards(): lax.dot_general(out_grad[:, :half], first_rows, contract, preferred_eleme...  5.48 us
    pallas_call x1, Pallas kernels, backward_pass(): pl.pallas_call(finish_kernel, out_shape=(tokens, tokens, tokens), in_spec...  4.58 us
  transfers between devices with their start and end apart: 2, of which 0 were waited for; matrix products, arithmetic and copies ran while one was open for 13% of the time, Pallas kernels for 73%

profile of v13, /device:TPU:2, one launch (start us, length us, event | category | flops | bytes accessed | tf_op | source)
XLA Modules:
  0.0 202.9 jit_solution(13842422720578329165)
XLA Ops:
  7.2 0.0 all-gather.2.cloned.1.call-start
  7.2 1.8 fusion.23
  9.0 0.0 reduce-scatter.2.cloned.1.call-start
  9.1 1.4 copy.19
  10.5 1.4 copy.20
  11.9 0.3 copy.21
  12.2 1.1 fusion.24.value_ref
  13.3 107.3 %shard_map.101 = (bf16[8,4,24,3072]{3,2,1,0:T(8,128)(2,1)}, f32[6,128,128]{2,1,0:T(8,128)}) custom-call(f32[6,128,128]{2,1,0:T(8,128)} %fusion.24.value_ref, bf16[24,3072]{1,0:T(8,128)(2,1)} %get-tuple-element.32.w_ref), custom_call_target="tpu_custom_call" | custom-call | tf_op jit(solution)/shard_map/pallas_call | solution.py:291
  120.6 0.8 iota_compare_fusion
  121.4 1.2 add_convert_fusion.sh_ref
  122.6 1.6 fusion.25
  124.2 3.8 %multiply_reduce_fusion.1 = (f32[512,6]{0,1:T(8,128)S(1)}, f32[512,6,128]{0,2,1:T(8,128)S(1)}) fusion(f32[6,128,512]{2,1,0:T(8,128)} %fusion.25, bf16[512,6,128]{0,2,1:T(8,128)(2,1)} %bitcast.36, pred[512,512]{1,0:T(8,128)(4,1)} %iota_compare_fusion, bf16[512,6,128]{0,2,1:T(8,128)(2,1)S(1)} %bitcast.28, bf16[512,6,128]{0,2,1:T(8,128)(2,1)S(1)} %bitcast.34), kind=kOutput, calls=%fused_computation.19 | convolution fusion | flops 809628672 | bytes 5779456 | tf_op jit(solution)/shard_map/hts,shj->thj/dot_general | solution.py:334
  128.0 0.2 multiply_convert_fusion
  128.2 0.0 all-gather.2.cloned.1.call-done
  128.2 11.6 %fusion.4 = bf16[512,6144]{1,0:T(8,128)(2,1)} fusion(bf16[512,768]{0,1:T(8,128)(2,1)S(1)} %bitcast.37, bf16[768,3072]{1,0:T(8,128)(2,1)} %all-gather.2.cloned.1.call-done, bf16[768,3072]{1,0:T(8,128)(2,1)} %bitcast.38), kind=kOutput, calls=%fused_computation.4 | convolution fusion | flops 4853858304 | bytes 16515072 | tf_op jit(solution)/shard_map/dot_general | solution.py:343
  139.8 5.7 %fusion.8 = f32[768,512]{1,0:T(8,128)S(1)} fusion(bf16[768,3072]{1,0:T(8,128)(2,1)} %all-gather.2.cloned.1.call-done, bf16[512,6144]{1,0:T(8,128)(2,1)} %param.11), kind=kOutput, calls=%fused_computation.7 | convolution fusion | flops 2415919104 | bytes 9437184 | tf_op jit(solution)/shard_map/dot_general | solution.py:348
  145.5 5.5 %fusion.17 = f32[768,512]{1,0:T(8,128)S(1)} fusion(f32[768,512]{1,0:T(8,128)S(1)} %fusion.8, bf16[768,3072]{1,0:T(8,128)(2,1)} %bitcast.39, bf16[512,6144]{1,0:T(8,128)(2,1)} %param.11), kind=kOutput, calls=%fused_computation.20 | convolution fusion | flops 2416312320 | bytes 11010048 | tf_op jit(solution)/shard_map/dot_general | solution.py:346
  150.9 0.4 multiply_reduce_fusion
  151.3 0.4 fusion.16
  151.8 1.2 copy.27.ga_hbm
  152.9 1.1 convolution_bitcast_fusion.adj_ref
  154.0 36.6 %shard_map.102 = (bf16[512,768]{1,0:T(8,128)(2,1)}, f32[512,768]{1,0:T(8,128)}, f32[512,768]{1,0:T(8,128)}, bf16[6,128,128]{2,1,0:T(8,128)(2,1)}, f32[6,128,128]{2,1,0:T(8,128)}) custom-call(f32[6,128,128]{2,1,0:T(8,128)} %convolution_bitcast_fusion.adj_ref, bf16[512,768]{1,0:T(8,128)(2,1)} %q_hbm.1, bf16[512,768]{1,0:T(8,128)(2,1)} %k_ref.1, ...), custom_call_target="tpu_custom_call" | custom-call | tf_op jit(solution)/shard_map/pallas_call | solution.py:165
  190.7 4.6 %shard_map.103 = (bf16[512,768]{1,0:T(8,128)(2,1)}, bf16[512,768]{1,0:T(8,128)(2,1)}, bf16[512,768]{1,0:T(8,128)(2,1)}) custom-call(bf16[512,768]{1,0:T(8,128)(2,1)} %get-tuple-element.23.gq_in, f32[512,768]{1,0:T(8,128)} %get-tuple-element.24.gk_acc, f32[512,768]{1,0:T(8,128)} %get-tuple-element.25.gv_acc, bf16[512,768]{1,0:T(8,128)(2,1)} %v_ref.1, ...), custom_call_target="tpu_custom_call" | custom-call | tf_op jit(solution)/shard_map/pallas_call | solution.py:181
  195.3 0.7 copy.34
  (13 shorter events, 0.1 us)
Async XLA Ops:
  7.2 4.7 %copy-start = (bf16[512,768]{1,0:T(8,128)(2,1)S(1)}, bf16[512,768]{1,0:T(8,128)(2,1)}, u32[]{:S(2)}) copy-start(bf16[512,768]{1,0:T(8,128)(2,1)} %v_ref.1) | copy-start | bytes 2359300
  7.2 121.0 %all-gather.2.cloned.1.call-start = ((), (), s32[]{:S(2)}) async-start(), calls=%async_computation.1 | async-start | bytes 4866048 | tf_op jit(solution)/shard_map/all_gather | solution.py:327
  9.0 186.3 %reduce-scatter.2.cloned.1.call-start = ((), (), s32[]{:S(2)}) async-start(), calls=%async_computation.2 | async-start | bytes 7077888 | tf_op jit(solution)/shard_map/reduce_scatter | solution.py:349
  12.2 110.4 %copy-start.1 = (bf16[512,768]{0,1:T(8,128)(2,1)}, bf16[512,768]{0,1:T(8,128)(2,1)S(1)}, u32[]{:S(2)}) copy-start(bf16[512,768]{0,1:T(8,128)(2,1)S(1)} %copy.21) | copy-start | bytes 2359300
  122.6 5.4 %copy-start.2 = (bf16[6,128,128]{2,1,0:T(8,128)(2,1)}, bf16[6,128,128]{2,1,0:T(8,128)(2,1)S(1)}, u32[]{:S(2)}) copy-start(bf16[6,128,128]{2,1,0:T(8,128)(2,1)S(1)} %add_convert_fusion.sh_ref) | copy-start | bytes 589828
  190.7 4.6 %copy-start.3 = (f32[6,128,128]{2,1,0:T(8,128)S(1)}, f32[6,128,128]{2,1,0:T(8,128)}, u32[]{:S(2)}) copy-start(f32[6,128,128]{2,1,0:T(8,128)} %get-tuple-element.44) | copy-start | bytes 1179652
Sparse Core Ops, SparseCore 0:
  11.2 107.5 all-gather.1
  139.9 41.0 reduce-scatter.1

commit v14 on v13

--- a/solution.py
+++ b/solution.py
@@ -143,16 +143,26 @@
         store.wait()
 
 
-def finish_kernel(gq_in, gk_acc, gv_acc, v_ref, k_ref, later_ref, gq_ref, gk_ref, gv_ref):
+def finish_kernel(gq_in, gk_hbm, gv_hbm, v_hbm, k_hbm, later_ref, gq_ref, gk_ref, gv_ref,
+                  gk_acc, gv_acc, v_ref, k_ref, sems):
     heads, dim = later_ref.shape[0], later_ref.shape[2]
     nt = (((1,), (1,)), ((), ()))
+    loads = [pltpu.make_async_copy(src, dst, sems.at[i]) for i, (src, dst) in
+             enumerate([(gk_hbm, gk_acc), (v_hbm, v_ref), (gv_hbm, gv_acc), (k_hbm, k_ref)])]
+    for load in loads:
+        load.start()
     gq_ref[...] = gq_in[...]
+    loads[0].wait()
+    loads[1].wait()
     for h in range(heads):
         cols = pl.ds(h * dim, dim)
-        later = later_ref[h]
-        gk = gk_acc[:, cols] + lax.dot_general(v_ref[:, cols], later, nt, preferred_element_type=jnp.float32)
+        gk = gk_acc[:, cols] + lax.dot_general(v_ref[:, cols], later_ref[h], nt, preferred_element_type=jnp.float32)
         gk_ref[:, cols] = gk.astype(gk_ref.dtype)
-        gv = gv_acc[:, cols] + jnp.dot(k_ref[:, cols], later, preferred_element_type=jnp.float32)
+    loads[2].wait()
+    loads[3].wait()
+    for h in range(heads):
+        cols = pl.ds(h * dim, dim)
+        gv = gv_acc[:, cols] + jnp.dot(k_ref[:, cols], later_ref[h], preferred_element_type=jnp.float32)
         gv_ref[:, cols] = gv.astype(gv_ref.dtype)
 
 
@@ -181,8 +191,11 @@
     gq, gk, gv = pl.pallas_call(
         finish_kernel,
         out_shape=(tokens, tokens, tokens),
-        in_specs=[vmem] * 6,
+        in_specs=[vmem] + [pl.BlockSpec(memory_space=pl.ANY)] * 4 + [vmem],
         out_specs=(vmem,) * 3,
+        scratch_shapes=[pltpu.VMEM(query.shape, jnp.float32), pltpu.VMEM(query.shape, jnp.float32),
+                        pltpu.VMEM(query.shape, jnp.bfloat16), pltpu.VMEM(query.shape, jnp.bfloat16),
+                        pltpu.SemaphoreType.DMA((4,))],
     )(gq, gk_acc, gv_acc, value, key, later)
     return gq, gk, gv, total
 

time: 205 us -> 205 us (level)
  no operation moved by 1% of the time
where the time goes in v14:
time: 205 us; the launch traced here: 203 us
  Pallas kernels  149 us (73%)
  matrix products  30.2 us (15%)
  between operations  14.2 us (7%)
  local copies, waits for them, and re-layouts  6.81 us (3%)
  other arithmetic  2.98 us (1%)
    pallas_call x1, Pallas kernels, gather_and_scan(): pl.pallas_call(functools.partial(gather_kernel, ny, ca), out_shape=(jax.S...  107 us
    pallas_call x1, Pallas kernels, backward_pass(): pl.pallas_call(backward_kernel, out_shape=(tokens, accs, accs, jax.ShapeD...  36.6 us
    dot_general x1, matrix products, shards(): jnp.dot(normed, weight_rows, preferred_element_type=jnp.float32)  11.6 us
    dot_general x1, matrix products, shards(): lax.dot_general(out_grad[:, half:], other_half, contract, preferred_eleme...  5.65 us
    dot_general x1, matrix products, shards(): lax.dot_general(out_grad[:, :half], first_rows, contract, preferred_eleme...  5.48 us
    pallas_call x1, Pallas kernels, backward_pass(): pl.pallas_call(finish_kernel, out_shape=(tokens, tokens, tokens), in_spec...  4.96 us
  transfers between devices with their start and end apart: 2, of which 0 were waited for; matrix products, arithmetic and copies ran while one was open for 13% of the time, Pallas kernels for 73%

profile of v14, /device:TPU:2, one launch (start us, length us, event | category | flops | bytes accessed | tf_op | source)
XLA Modules:
  0.0 203.3 jit_solution(8209448600168627017)
XLA Ops:
  7.2 0.0 all-gather.2.cloned.1.call-start
  7.2 1.8 fusion.23
  9.0 0.0 reduce-scatter.2.cloned.1.call-start
  9.1 1.4 copy.19
  10.5 1.4 copy.20
  11.9 0.3 copy.21
  12.2 1.1 fusion.24.value_ref
  13.3 107.3 %shard_map.101 = (bf16[8,4,24,3072]{3,2,1,0:T(8,128)(2,1)}, f32[6,128,128]{2,1,0:T(8,128)}) custom-call(f32[6,128,128]{2,1,0:T(8,128)} %fusion.24.value_ref, bf16[24,3072]{1,0:T(8,128)(2,1)} %get-tuple-element.32.w_ref), custom_call_target="tpu_custom_call" | custom-call | tf_op jit(solution)/shard_map/pallas_call | solution.py:304
  120.6 0.8 iota_compare_fusion
  121.4 1.2 add_convert_fusion.sh_ref
  122.6 1.6 fusion.25
  124.2 3.8 %multiply_reduce_fusion.1 = (f32[512,6]{0,1:T(8,128)S(1)}, f32[512,6,128]{0,2,1:T(8,128)S(1)}) fusion(f32[6,128,512]{2,1,0:T(8,128)} %fusion.25, bf16[512,6,128]{0,2,1:T(8,128)(2,1)} %bitcast.36, pred[512,512]{1,0:T(8,128)(4,1)} %iota_compare_fusion, bf16[512,6,128]{0,2,1:T(8,128)(2,1)S(1)} %bitcast.28, bf16[512,6,128]{0,2,1:T(8,128)(2,1)S(1)} %bitcast.34), kind=kOutput, calls=%fused_computation.19 | convolution fusion | flops 809628672 | bytes 5779456 | tf_op jit(solution)/shard_map/hts,shj->thj/dot_general | solution.py:347
  128.0 0.2 multiply_convert_fusion
  128.2 0.0 all-gather.2.cloned.1.call-done
  128.2 11.6 %fusion.4 = bf16[512,6144]{1,0:T(8,128)(2,1)} fusion(bf16[512,768]{0,1:T(8,128)(2,1)S(1)} %bitcast.37, bf16[768,3072]{1,0:T(8,128)(2,1)} %all-gather.2.cloned.1.call-done, bf16[768,3072]{1,0:T(8,128)(2,1)} %bitcast.38), kind=kOutput, calls=%fused_computation.4 | convolution fusion | flops 4853858304 | bytes 16515072 | tf_op jit(solution)/shard_map/dot_general | solution.py:356
  139.8 5.7 %fusion.8 = f32[768,512]{1,0:T(8,128)S(1)} fusion(bf16[768,3072]{1,0:T(8,128)(2,1)} %all-gather.2.cloned.1.call-done, bf16[512,6144]{1,0:T(8,128)(2,1)} %param.11), kind=kOutput, calls=%fused_computation.7 | convolution fusion | flops 2415919104 | bytes 9437184 | tf_op jit(solution)/shard_map/dot_general | solution.py:361
  145.5 5.5 %fusion.17 = f32[768,512]{1,0:T(8,128)S(1)} fusion(f32[768,512]{1,0:T(8,128)S(1)} %fusion.8, bf16[768,3072]{1,0:T(8,128)(2,1)} %bitcast.39, bf16[512,6144]{1,0:T(8,128)(2,1)} %param.11), kind=kOutput, calls=%fused_computation.20 | convolution fusion | flops 2416312320 | bytes 11010048 | tf_op jit(solution)/shard_map/dot_general | solution.py:359
  150.9 0.4 multiply_reduce_fusion
  151.3 0.4 fusion.16
  151.8 1.2 copy.27.ga_hbm
  152.9 1.1 convolution_bitcast_fusion.adj_ref
  154.0 36.6 %shard_map.102 = (bf16[512,768]{1,0:T(8,128)(2,1)}, f32[512,768]{1,0:T(8,128)}, f32[512,768]{1,0:T(8,128)}, bf16[6,128,128]{2,1,0:T(8,128)(2,1)}, f32[6,128,128]{2,1,0:T(8,128)}) custom-call(f32[6,128,128]{2,1,0:T(8,128)} %convolution_bitcast_fusion.adj_ref, bf16[512,768]{1,0:T(8,128)(2,1)} %q_hbm.1, bf16[512,768]{1,0:T(8,128)(2,1)} %k_hbm.3, ...), custom_call_target="tpu_custom_call" | custom-call | tf_op jit(solution)/shard_map/pallas_call | solution.py:175
  190.7 5.0 %shard_map.103 = (bf16[512,768]{1,0:T(8,128)(2,1)}, bf16[512,768]{1,0:T(8,128)(2,1)}, bf16[512,768]{1,0:T(8,128)(2,1)}) custom-call(bf16[512,768]{1,0:T(8,128)(2,1)} %get-tuple-element.23.gq_in, f32[512,768]{1,0:T(8,128)} %get-tuple-element.24.gk_hbm, f32[512,768]{1,0:T(8,128)} %get-tuple-element.25.gv_hbm, bf16[512,768]{1,0:T(8,128)(2,1)} %v_hbm.3, ...), custom_call_target="tpu_custom_call" | custom-call | tf_op jit(solution)/shard_map/pallas_call | solution.py:191
  195.7 0.7 copy.34
  (13 shorter events, 0.1 us)
Async XLA Ops:
  7.2 4.7 %copy-start = (bf16[512,768]{1,0:T(8,128)(2,1)S(1)}, bf16[512,768]{1,0:T(8,128)(2,1)}, u32[]{:S(2)}) copy-start(bf16[512,768]{1,0:T(8,128)(2,1)} %v_hbm.3) | copy-start | bytes 2359300
  7.2 121.0 %all-gather.2.cloned.1.call-start = ((), (), s32[]{:S(2)}) async-start(), calls=%async_computation.1 | async-start | bytes 4866048 | tf_op jit(solution)/shard_map/all_gather | solution.py:340
  9.0 186.7 %reduce-scatter.2.cloned.1.call-start = ((), (), s32[]{:S(2)}) async-start(), calls=%async_computation.2 | async-start | bytes 7077888 | tf_op jit(solution)/shard_map/reduce_scatter | solution.py:362
  12.2 110.4 %copy-start.1 = (bf16[512,768]{0,1:T(8,128)(2,1)}, bf16[512,768]{0,1:T(8,128)(2,1)S(1)}, u32[]{:S(2)}) copy-start(bf16[512,768]{0,1:T(8,128)(2,1)S(1)} %copy.21) | copy-start | bytes 2359300
  122.6 5.4 %copy-start.2 = (bf16[6,128,128]{2,1,0:T(8,128)(2,1)}, bf16[6,128,128]{2,1,0:T(8,128)(2,1)S(1)}, u32[]{:S(2)}) copy-start(bf16[6,128,128]{2,1,0:T(8,128)(2,1)S(1)} %add_convert_fusion.sh_ref) | copy-start | bytes 589828
  190.7 5.0 %copy-start.3 = (f32[6,128,128]{2,1,0:T(8,128)S(1)}, f32[6,128,128]{2,1,0:T(8,128)}, u32[]{:S(2)}) copy-start(f32[6,128,128]{2,1,0:T(8,128)} %get-tuple-element.44) | copy-start | bytes 1179652
Sparse Core Ops, SparseCore 0:
  11.2 107.5 all-gather.1
  139.9 41.0 reduce-scatter.1

commit v15 on v13

--- a/solution.py
+++ b/solution.py
@@ -187,7 +187,11 @@
     return gq, gk, gv, total
 
 
-def gather_kernel(ny, ca, value_ref, w_ref, rows_ref, partial_ref, sendbuf, recvbuf, send_sem, recv_sem, bf_send, bf_recv, local_sem):
+def gather_kernel(ny, ca, k_hbm, v_hbm, w_ref, rows_ref, partial_ref, sendbuf, recvbuf, send_sem, recv_sem, bf_send, bf_recv, local_sem,
+                  k_ref, v_ref, load_sem):
+    loads = [pltpu.make_async_copy(k_hbm, k_ref, load_sem.at[0]), pltpu.make_async_copy(v_hbm, v_ref, load_sem.at[1])]
+    for load in loads:
+        load.start()
     me = lax.axis_index("seq")
     head = lax.axis_index("head")
     count = lax.axis_size("seq")
@@ -246,7 +250,15 @@
          (R.at[pl.ds(0, hz), yy(-1), :, B], R.at[pl.ds(0, hz), yy(-1), :, B], yr),
          (R.at[pl.ds(hz, nz - hz), yy(1), :, B], R.at[pl.ds(hz, nz - hz), yy(1), :, B], yl)],
     ]
-    total = value_ref[...]
+    for load in loads:
+        load.wait()
+    heads, dim = partial_ref.shape[0], partial_ref.shape[2]
+    tn = (((0,), (0,)), ((), ()))
+    total = jnp.stack([
+        lax.dot_general(k_ref[:, pl.ds(h * dim, dim)], v_ref[:, pl.ds(h * dim, dim)], tn,
+                        preferred_element_type=jnp.float32)
+        for h in range(heads)
+    ])
     partial = jnp.zeros_like(total)
     n = 0
     for t, moves in enumerate(ticks):
@@ -281,7 +293,7 @@
     partial_ref[...] = partial
 
 
-def gather_and_scan(value, weight):
+def gather_and_scan(key, val, heads, dim, weight):
     count = lax.axis_size("seq")
     ny = 4
     piece, cols = weight.shape
@@ -292,21 +304,24 @@
         functools.partial(gather_kernel, ny, ca),
         out_shape=(
             jax.ShapeDtypeStruct((count // ny, ny, piece, cols), weight.dtype),
-            jax.ShapeDtypeStruct(value.shape, jnp.float32),
+            jax.ShapeDtypeStruct((heads, dim, dim), jnp.float32),
         ),
-        in_specs=[pl.BlockSpec(memory_space=pltpu.VMEM), pl.BlockSpec(memory_space=pl.ANY)],
+        in_specs=[pl.BlockSpec(memory_space=pl.ANY)] * 3,
         out_specs=(pl.BlockSpec(memory_space=pl.ANY), pl.BlockSpec(memory_space=pltpu.VMEM)),
         scratch_shapes=[
-            pltpu.VMEM((rounds,) + value.shape, jnp.bfloat16),
-            pltpu.VMEM((rounds,) + value.shape, jnp.bfloat16),
+            pltpu.VMEM((rounds, heads, dim, dim), jnp.bfloat16),
+            pltpu.VMEM((rounds, heads, dim, dim), jnp.bfloat16),
             pltpu.SemaphoreType.DMA((n_copies,)),
             pltpu.SemaphoreType.DMA((n_copies,)),
             pltpu.SemaphoreType.DMA((rounds,)),
             pltpu.SemaphoreType.DMA((rounds,)),
             pltpu.SemaphoreType.DMA(()),
+            pltpu.VMEM(key.shape, key.dtype),
+            pltpu.VMEM(val.shape, val.dtype),
+            pltpu.SemaphoreType.DMA((2,)),
         ],
         compiler_params=pltpu.CompilerParams(collective_id=2, has_side_effects=True),
-    )(value.astype(jnp.float32), weight)
+    )(key, val, weight)
 
 
 def normalize(attended):
@@ -321,9 +336,8 @@
     queries = query.reshape(tok_rows, heads_here, head_dim)
     key_rows = key.reshape(tok_rows, heads_here, head_dim)
     val_rows = value.reshape(tok_rows, heads_here, head_dim)
-    local_state = jnp.einsum("thi,thj->hij", key_rows, val_rows, preferred_element_type=jnp.float32)
     half = out_weight.shape[1] // 2
-    gathered, earlier = gather_and_scan(local_state, out_weight[:, :half])
+    gathered, earlier = gather_and_scan(key, value, heads_here, head_dim, out_weight[:, :half])
     other_half = lax.all_gather(out_weight[:, half:], "seq", axis=0, tiled=True)
     state_half = (init_state + earlier).astype(jnp.bfloat16)
     row_index = lax.broadcasted_iota(jnp.int32, (tok_rows, tok_rows), 0)

time: 205 us -> 206 us (level)
  transfers between devices with their start and end apart: 2 -> 2, of which waited for: 0 -> 0; matrix products, arithmetic and copies ran while one was open for 13% -> 12% of each run, Pallas kernels for 73% -> 74%
where the time goes in v15:
time: 206 us; the launch traced here: 205 us
  Pallas kernels  151 us (73%)
  matrix products  29.1 us (14%)
  between operations  14.2 us (7%)
  local copies, waits for them, and re-layouts  7.73 us (4%)
  other arithmetic  2.86 us (1%)
    pallas_call x1, Pallas kernels, gather_and_scan(): pl.pallas_call(functools.partial(gather_kernel, ny, ca), out_shape=(jax.S...  108 us
    pallas_call x1, Pallas kernels, backward_pass(): pl.pallas_call(backward_kernel, out_shape=(tokens, accs, accs, jax.ShapeD...  38.4 us
    dot_general x1, matrix products, shards(): jnp.dot(normed, weight_rows, preferred_element_type=jnp.float32)  11.6 us
    dot_general x1, matrix products, shards(): lax.dot_general(out_grad[:, half:], other_half, contract, preferred_eleme...  5.65 us
    dot_general x1, matrix products, shards(): lax.dot_general(out_grad[:, :half], first_rows, contract, preferred_eleme...  5.48 us
    unnamed x12, local copies, waits for them, and re-layouts  4.8 us
    pallas_call x1, Pallas kernels, backward_pass(): pl.pallas_call(finish_kernel, out_shape=(tokens, tokens, tokens), in_spec...  4.58 us
  transfers between devices with their start and end apart: 2, of which 0 were waited for; matrix products, arithmetic and copies ran while one was open for 12% of the time, Pallas kernels for 74%

profile of v15, /device:TPU:2, one launch (start us, length us, event | category | flops | bytes accessed | tf_op | source)
XLA Modules:
  0.0 205.4 jit_solution(11588938120293037933)
XLA Ops:
  7.2 0.0 all-gather.2.cloned.1.call-start
  7.2 1.8 fusion.23
  9.0 0.0 all-gather.2.cloned.1.call-update
  9.0 0.0 reduce-scatter.2.cloned.1.call-start
  9.1 1.5 copy.17
  10.5 1.4 copy.18
  12.0 1.2 copy.19
  13.1 108.3 %shard_map.101 = (bf16[8,4,24,3072]{3,2,1,0:T(8,128)(2,1)}, f32[6,128,128]{2,1,0:T(8,128)}) custom-call(bf16[512,768]{1,0:T(8,128)(2,1)} %k_ref.1, bf16[512,768]{1,0:T(8,128)(2,1)} %v_ref.1, bf16[24,3072]{1,0:T(8,128)(2,1)} %get-tuple-element.32.w_ref), custom_call_target="tpu_custom_call" | custom-call | tf_op jit(solution)/shard_map/pallas_call | solution.py:303
  121.5 0.8 iota_compare_fusion
  122.2 1.0 add_convert_fusion.sh_ref
  123.3 1.6 fusion.24
  124.9 3.8 %multiply_reduce_fusion.1 = (f32[512,6]{0,1:T(8,128)S(1)}, f32[512,6,128]{0,2,1:T(8,128)S(1)}) fusion(f32[6,128,512]{2,1,0:T(8,128)} %fusion.24, bf16[512,6,128]{0,2,1:T(8,128)(2,1)} %bitcast.32, pred[512,512]{1,0:T(8,128)(4,1)} %iota_compare_fusion, bf16[512,6,128]{0,2,1:T(8,128)(2,1)S(1)} %bitcast.26, bf16[512,6,128]{0,2,1:T(8,128)(2,1)S(1)} %bitcast.31), kind=kOutput, calls=%fused_computation.19 | convolution fusion | flops 809628672 | bytes 5779456 | tf_op jit(solution)/shard_map/hts,shj->thj/dot_general | solution.py:348
  128.7 0.2 multiply_convert_fusion
  128.9 0.0 all-gather.2.cloned.1.call-done
  128.9 11.6 %fusion.4 = bf16[512,6144]{1,0:T(8,128)(2,1)} fusion(bf16[512,768]{0,1:T(8,128)(2,1)S(1)} %bitcast.33, bf16[768,3072]{1,0:T(8,128)(2,1)} %all-gather.2.cloned.1.call-done, bf16[768,3072]{1,0:T(8,128)(2,1)} %bitcast.34), kind=kOutput, calls=%fused_computation.4 | convolution fusion | flops 4853858304 | bytes 16515072 | tf_op jit(solution)/shard_map/dot_general | solution.py:357
  140.5 5.6 %fusion.8 = f32[768,512]{1,0:T(8,128)S(1)} fusion(bf16[768,3072]{1,0:T(8,128)(2,1)} %all-gather.2.cloned.1.call-done, bf16[512,6144]{1,0:T(8,128)(2,1)} %param.11), kind=kOutput, calls=%fused_computation.7 | convolution fusion | flops 2415919104 | bytes 9437184 | tf_op jit(solution)/shard_map/dot_general | solution.py:362
  146.1 5.5 %fusion.17 = f32[768,512]{1,0:T(8,128)S(1)} fusion(f32[768,512]{1,0:T(8,128)S(1)} %fusion.8, bf16[768,3072]{1,0:T(8,128)(2,1)} %bitcast.35, bf16[512,6144]{1,0:T(8,128)(2,1)} %param.11), kind=kOutput, calls=%fused_computation.20 | convolution fusion | flops 2416312320 | bytes 11010048 | tf_op jit(solution)/shard_map/dot_general | solution.py:360
  151.6 0.4 multiply_reduce_fusion
  152.0 0.4 fusion.16
  152.5 1.2 copy.24.ga_hbm
  153.6 1.1 convolution_bitcast_fusion.adj_ref
  154.7 38.4 %shard_map.102 = (bf16[512,768]{1,0:T(8,128)(2,1)}, f32[512,768]{1,0:T(8,128)}, f32[512,768]{1,0:T(8,128)}, bf16[6,128,128]{2,1,0:T(8,128)(2,1)}, f32[6,128,128]{2,1,0:T(8,128)}) custom-call(f32[6,128,128]{2,1,0:T(8,128)} %convolution_bitcast_fusion.adj_ref, bf16[512,768]{1,0:T(8,128)(2,1)} %q_hbm.1, bf16[512,768]{1,0:T(8,128)(2,1)} %k_ref.1, ...), custom_call_target="tpu_custom_call" | custom-call | tf_op jit(solution)/shard_map/pallas_call | solution.py:165
  193.2 4.6 %shard_map.103 = (bf16[512,768]{1,0:T(8,128)(2,1)}, bf16[512,768]{1,0:T(8,128)(2,1)}, bf16[512,768]{1,0:T(8,128)(2,1)}) custom-call(bf16[512,768]{1,0:T(8,128)(2,1)} %get-tuple-element.23.gq_in, f32[512,768]{1,0:T(8,128)} %get-tuple-element.24.gk_acc, f32[512,768]{1,0:T(8,128)} %get-tuple-element.25.gv_acc, bf16[512,768]{1,0:T(8,128)(2,1)} %v_ref.1, ...), custom_call_target="tpu_custom_call" | custom-call | tf_op jit(solution)/shard_map/pallas_call | solution.py:181
  197.8 0.7 copy.30
  (12 shorter events, 0.1 us)
Async XLA Ops:
  7.2 4.8 %copy-start = (bf16[512,768]{1,0:T(8,128)(2,1)S(1)}, bf16[512,768]{1,0:T(8,128)(2,1)}, u32[]{:S(2)}) copy-start(bf16[512,768]{1,0:T(8,128)(2,1)} %v_ref.1) | copy-start | bytes 2359300
  7.2 121.7 %all-gather.2.cloned.1.call-start = ((), (), s32[]{:S(2)}) async-start(), calls=%async_computation.1 | async-start | bytes 4866048 | tf_op jit(solution)/shard_map/all_gather | solution.py:341
  9.0 113.2 %copy-start.3 = (f32[6,128,128]{2,1,0:T(8,128)S(1)}, f32[6,128,128]{2,1,0:T(8,128)}, u32[]{:S(2)}) copy-start(f32[6,128,128]{2,1,0:T(8,128)} %param.9) | copy-start | bytes 1179652
  9.0 188.7 %reduce-scatter.2.cloned.1.call-start = ((), (), s32[]{:S(2)}) async-start(), calls=%async_computation.2 | async-start | bytes 7077888 | tf_op jit(solution)/shard_map/reduce_scatter | solution.py:363
  123.3 5.4 %copy-start.1 = (bf16[6,128,128]{2,1,0:T(8,128)(2,1)}, bf16[6,128,128]{2,1,0:T(8,128)(2,1)S(1)}, u32[]{:S(2)}) copy-start(bf16[6,128,128]{2,1,0:T(8,128)(2,1)S(1)} %add_convert_fusion.sh_ref) | copy-start | bytes 589828
  193.2 4.6 %copy-start.2 = (f32[6,128,128]{2,1,0:T(8,128)S(1)}, f32[6,128,128]{2,1,0:T(8,128)}, u32[]{:S(2)}) copy-start(f32[6,128,128]{2,1,0:T(8,128)} %get-tuple-element.44) | copy-start | bytes 1179652
Sparse Core Ops, SparseCore 0:
  11.2 108.3 all-gather.1
  140.6 41.1 reduce-scatter.1

commit v16 on v13

--- a/solution.py
+++ b/solution.py
@@ -107,8 +107,8 @@
         gq = jnp.dot(gs, kh, preferred_element_type=jnp.float32)
         gq = gq + lax.dot_general(gah, sh_ref[h], nt, preferred_element_type=jnp.float32)
         gq_ref[:, cols] = gq.astype(gq_ref.dtype)
-        gk_acc[:, cols] = lax.dot_general(gs, qh, tn, preferred_element_type=jnp.float32)
-        gv_acc[:, cols] = lax.dot_general(aw, gah, tn, preferred_element_type=jnp.float32)
+        gk_acc[:, cols] = lax.dot_general(gs, qh, tn, preferred_element_type=jnp.float32).astype(gk_acc.dtype)
+        gv_acc[:, cols] = lax.dot_general(aw, gah, tn, preferred_element_type=jnp.float32).astype(gv_acc.dtype)
 
     order = [[] for _ in range(rounds)]
     for h in range(heads):
@@ -150,9 +150,9 @@
     for h in range(heads):
         cols = pl.ds(h * dim, dim)
         later = later_ref[h]
-        gk = gk_acc[:, cols] + lax.dot_general(v_ref[:, cols], later, nt, preferred_element_type=jnp.float32)
+        gk = gk_acc[:, cols].astype(jnp.float32) + lax.dot_general(v_ref[:, cols], later, nt, preferred_element_type=jnp.float32)
         gk_ref[:, cols] = gk.astype(gk_ref.dtype)
-        gv = gv_acc[:, cols] + jnp.dot(k_ref[:, cols], later, preferred_element_type=jnp.float32)
+        gv = gv_acc[:, cols].astype(jnp.float32) + jnp.dot(k_ref[:, cols], later, preferred_element_type=jnp.float32)
         gv_ref[:, cols] = gv.astype(gv_ref.dtype)
 
 
@@ -161,7 +161,7 @@
     rounds = count.bit_length() - 1
     tokens = jax.ShapeDtypeStruct(query.shape, jnp.bfloat16)
     vmem = pl.BlockSpec(memory_space=pltpu.VMEM)
-    accs = jax.ShapeDtypeStruct(query.shape, jnp.float32)
+    accs = jax.ShapeDtypeStruct(query.shape, jnp.bfloat16)
     gq, gk_acc, gv_acc, later, total = pl.pallas_call(
         backward_kernel,
         out_shape=(tokens, accs, accs, jax.ShapeDtypeStruct(own_adjoint.shape, jnp.bfloat16),
@@ -174,8 +174,8 @@
             pltpu.SemaphoreType.DMA((rounds,)),
             pltpu.SemaphoreType.DMA((rounds,)),
         ] + [pltpu.VMEM(query.shape, jnp.bfloat16)] * 4 + [pltpu.SemaphoreType.DMA((4,))]
-        + [pltpu.VMEM(query.shape, jnp.bfloat16), pltpu.VMEM(query.shape, jnp.float32),
-           pltpu.VMEM(query.shape, jnp.float32), pltpu.SemaphoreType.DMA((3,))],
+        + [pltpu.VMEM(query.shape, jnp.bfloat16), pltpu.VMEM(query.shape, jnp.bfloat16),
+           pltpu.VMEM(query.shape, jnp.bfloat16), pltpu.SemaphoreType.DMA((3,))],
         compiler_params=pltpu.CompilerParams(collective_id=1, has_side_effects=True),
     )(own_adjoint, query, key, value, grad_att, state_half)
     gq, gk, gv = pl.pallas_call(

time: 205 us -> 204 us (level)
  no operation moved by 1% of the time
where the time goes in v16:
time: 204 us; the launch traced here: 202 us
  Pallas kernels  148 us (73%)
  matrix products  30.2 us (15%)
  between operations  14.2 us (7%)
  local copies, waits for them, and re-layouts  6.81 us (3%)
  other arithmetic  2.98 us (1%)
    pallas_call x1, Pallas kernels, gather_and_scan(): pl.pallas_call(functools.partial(gather_kernel, ny, ca), out_shape=(jax.S...  107 us
    pallas_call x1, Pallas kernels, backward_pass(): pl.pallas_call(backward_kernel, out_shape=(tokens, accs, accs, jax.ShapeD...  36.7 us
    dot_general x1, matrix products, shards(): jnp.dot(normed, weight_rows, preferred_element_type=jnp.float32)  11.6 us
    dot_general x1, matrix products, shards(): lax.dot_general(out_grad[:, half:], other_half, contract, preferred_eleme...  5.65 us
    dot_general x1, matrix products, shards(): lax.dot_general(out_grad[:, :half], first_rows, contract, preferred_eleme...  5.48 us
    pallas_call x1, Pallas kernels, backward_pass(): pl.pallas_call(finish_kernel, out_shape=(tokens, tokens, tokens), in_spec...  4.12 us
  transfers between devices with their start and end apart: 2, of which 0 were waited for; matrix products, arithmetic and copies ran while one was open for 13% of the time, Pallas kernels for 73%

profile of v16, /device:TPU:2, one launch (start us, length us, event | category | flops | bytes accessed | tf_op | source)
XLA Modules:
  0.0 202.5 jit_solution(12615686826430166772)
XLA Ops:
  7.2 0.0 all-gather.2.cloned.1.call-start
  7.2 1.8 fusion.23
  9.0 0.0 reduce-scatter.2.cloned.1.call-start
  9.1 1.4 copy.19
  10.5 1.4 copy.20
  11.9 0.3 copy.21
  12.2 1.1 fusion.24.value_ref
  13.3 107.3 %shard_map.101 = (bf16[8,4,24,3072]{3,2,1,0:T(8,128)(2,1)}, f32[6,128,128]{2,1,0:T(8,128)}) custom-call(f32[6,128,128]{2,1,0:T(8,128)} %fusion.24.value_ref, bf16[24,3072]{1,0:T(8,128)(2,1)} %get-tuple-element.32.w_ref), custom_call_target="tpu_custom_call" | custom-call | tf_op jit(solution)/shard_map/pallas_call | solution.py:291
  120.6 0.8 iota_compare_fusion
  121.4 1.2 add_convert_fusion.sh_ref
  122.6 1.6 fusion.25
  124.2 3.8 %multiply_reduce_fusion.1 = (f32[512,6]{0,1:T(8,128)S(1)}, f32[512,6,128]{0,2,1:T(8,128)S(1)}) fusion(f32[6,128,512]{2,1,0:T(8,128)} %fusion.25, bf16[512,6,128]{0,2,1:T(8,128)(2,1)} %bitcast.36, pred[512,512]{1,0:T(8,128)(4,1)} %iota_compare_fusion, bf16[512,6,128]{0,2,1:T(8,128)(2,1)S(1)} %bitcast.28, bf16[512,6,128]{0,2,1:T(8,128)(2,1)S(1)} %bitcast.34), kind=kOutput, calls=%fused_computation.19 | convolution fusion | flops 809628672 | bytes 5779456 | tf_op jit(solution)/shard_map/hts,shj->thj/dot_general | solution.py:334
  128.0 0.2 multiply_convert_fusion
  128.2 0.0 all-gather.2.cloned.1.call-done
  128.2 11.6 %fusion.4 = bf16[512,6144]{1,0:T(8,128)(2,1)} fusion(bf16[512,768]{0,1:T(8,128)(2,1)S(1)} %bitcast.37, bf16[768,3072]{1,0:T(8,128)(2,1)} %all-gather.2.cloned.1.call-done, bf16[768,3072]{1,0:T(8,128)(2,1)} %bitcast.38), kind=kOutput, calls=%fused_computation.4 | convolution fusion | flops 4853858304 | bytes 16515072 | tf_op jit(solution)/shard_map/dot_general | solution.py:343
  139.8 5.7 %fusion.8 = f32[768,512]{1,0:T(8,128)S(1)} fusion(bf16[768,3072]{1,0:T(8,128)(2,1)} %all-gather.2.cloned.1.call-done, bf16[512,6144]{1,0:T(8,128)(2,1)} %param.11), kind=kOutput, calls=%fused_computation.7 | convolution fusion | flops 2415919104 | bytes 9437184 | tf_op jit(solution)/shard_map/dot_general | solution.py:348
  145.5 5.5 %fusion.17 = f32[768,512]{1,0:T(8,128)S(1)} fusion(f32[768,512]{1,0:T(8,128)S(1)} %fusion.8, bf16[768,3072]{1,0:T(8,128)(2,1)} %bitcast.39, bf16[512,6144]{1,0:T(8,128)(2,1)} %param.11), kind=kOutput, calls=%fused_computation.20 | convolution fusion | flops 2416312320 | bytes 11010048 | tf_op jit(solution)/shard_map/dot_general | solution.py:346
  150.9 0.4 multiply_reduce_fusion
  151.3 0.4 fusion.16
  151.8 1.2 copy.27.ga_hbm
  152.9 1.1 convolution_bitcast_fusion.adj_ref
  154.0 36.7 %shard_map.102 = (bf16[512,768]{1,0:T(8,128)(2,1)}, bf16[512,768]{1,0:T(8,128)(2,1)}, bf16[512,768]{1,0:T(8,128)(2,1)}, bf16[6,128,128]{2,1,0:T(8,128)(2,1)}, f32[6,128,128]{2,1,0:T(8,128)}) custom-call(f32[6,128,128]{2,1,0:T(8,128)} %convolution_bitcast_fusion.adj_ref, bf16[512,768]{1,0:T(8,128)(2,1)} %q_hbm.1, bf16[512,768]{1,0:T(8,128)(2,1)} %k_ref.1, ...), custom_call_target="tpu_custom_call" | custom-call | tf_op jit(solution)/shard_map/pallas_call | solution.py:165
  190.8 4.1 %shard_map.103 = (bf16[512,768]{1,0:T(8,128)(2,1)}, bf16[512,768]{1,0:T(8,128)(2,1)}, bf16[512,768]{1,0:T(8,128)(2,1)}) custom-call(bf16[512,768]{1,0:T(8,128)(2,1)} %get-tuple-element.23.gq_in, bf16[512,768]{1,0:T(8,128)(2,1)} %get-tuple-element.24.gk_acc, bf16[512,768]{1,0:T(8,128)(2,1)} %get-tuple-element.25.gv_acc, bf16[512,768]{1,0:T(8,128)(2,1)} %v_ref.1, ...), custom_call_target="tpu_custom_call" | custom-call | tf_op jit(solution)/shard_map/pallas_call | solution.py:181
  194.9 0.7 copy.34
  (13 shorter events, 0.1 us)
Async XLA Ops:
  7.2 4.7 %copy-start = (bf16[512,768]{1,0:T(8,128)(2,1)S(1)}, bf16[512,768]{1,0:T(8,128)(2,1)}, u32[]{:S(2)}) copy-start(bf16[512,768]{1,0:T(8,128)(2,1)} %v_ref.1) | copy-start | bytes 2359300
  7.2 121.0 %all-gather.2.cloned.1.call-start = ((), (), s32[]{:S(2)}) async-start(), calls=%async_computation.1 | async-start | bytes 4866048 | tf_op jit(solution)/shard_map/all_gather | solution.py:327
  9.0 185.8 %reduce-scatter.2.cloned.1.call-start = ((), (), s32[]{:S(2)}) async-start(), calls=%async_computation.2 | async-start | bytes 7077888 | tf_op jit(solution)/shard_map/reduce_scatter | solution.py:349
  12.2 110.4 %copy-start.1 = (bf16[512,768]{0,1:T(8,128)(2,1)}, bf16[512,768]{0,1:T(8,128)(2,1)S(1)}, u32[]{:S(2)}) copy-start(bf16[512,768]{0,1:T(8,128)(2,1)S(1)} %copy.21) | copy-start | bytes 2359300
  122.6 5.4 %copy-start.2 = (bf16[6,128,128]{2,1,0:T(8,128)(2,1)}, bf16[6,128,128]{2,1,0:T(8,128)(2,1)S(1)}, u32[]{:S(2)}) copy-start(bf16[6,128,128]{2,1,0:T(8,128)(2,1)S(1)} %add_convert_fusion.sh_ref) | copy-start | bytes 589828
  190.7 4.1 %copy-start.3 = (f32[6,128,128]{2,1,0:T(8,128)S(1)}, f32[6,128,128]{2,1,0:T(8,128)}, u32[]{:S(2)}) copy-start(f32[6,128,128]{2,1,0:T(8,128)} %get-tuple-element.44) | copy-start | bytes 1179652
Sparse Core Ops, SparseCore 0:
  11.2 107.5 all-gather.1
  139.9 41.0 reduce-scatter.1

commit v17 on v16

--- a/solution.py
+++ b/solution.py
@@ -70,7 +70,7 @@
     )(value.astype(jnp.float32))
 
 
-def backward_kernel(adj_ref, q_hbm, k_hbm, v_hbm, ga_hbm, sh_ref, gq_hbm, gk_hbm, gv_hbm, later_ref, total_ref,
+def backward_kernel(q_hbm, k_hbm, v_hbm, ga_hbm, sh_ref, gq_hbm, gk_hbm, gv_hbm, later_ref, total_ref,
                     sendbuf, recvbuf, send_sem, recv_sem, q_ref, k_ref, v_ref, ga_ref, load_sem,
                     gq_ref, gk_acc, gv_acc, store_sem):
     loads = [pltpu.make_async_copy(src, dst, load_sem.at[i])
@@ -113,7 +113,13 @@
     order = [[] for _ in range(rounds)]
     for h in range(heads):
         order[min(h, rounds - 1)].append(h)
-    total = adj_ref[...]
+    for load in loads:
+        load.wait()
+    total = jnp.stack([
+        lax.dot_general(q_ref[:, pl.ds(h * dim, dim)], ga_ref[:, pl.ds(h * dim, dim)], tn,
+                        preferred_element_type=jnp.float32)
+        for h in range(heads)
+    ])
     partial = jnp.zeros_like(total)
     for t, (partner, bit) in enumerate(partners):
         sent = total.astype(jnp.bfloat16)
@@ -123,9 +129,6 @@
             recv_sem=recv_sem.at[t], device_id=(partner, head), device_id_type=MESH,
         )
         copy.start()
-        if t == 0:
-            for load in loads:
-                load.wait()
         for h in order[t]:
             head_work(h)
         if t == rounds - 1:
@@ -156,7 +159,8 @@
         gv_ref[:, cols] = gv.astype(gv_ref.dtype)
 
 
-def backward_pass(own_adjoint, query, key, value, grad_att, state_half):
+def backward_pass(query, key, value, grad_att, state_half):
+    own_adjoint = jax.ShapeDtypeStruct(state_half.shape, jnp.float32)
     count = lax.axis_size("seq")
     rounds = count.bit_length() - 1
     tokens = jax.ShapeDtypeStruct(query.shape, jnp.bfloat16)
@@ -166,7 +170,7 @@
         backward_kernel,
         out_shape=(tokens, accs, accs, jax.ShapeDtypeStruct(own_adjoint.shape, jnp.bfloat16),
                    jax.ShapeDtypeStruct(own_adjoint.shape, jnp.float32)),
-        in_specs=[vmem] + [pl.BlockSpec(memory_space=pl.ANY)] * 4 + [vmem],
+        in_specs=[pl.BlockSpec(memory_space=pl.ANY)] * 4 + [vmem],
         out_specs=(pl.BlockSpec(memory_space=pl.ANY),) * 3 + (vmem, vmem),
         scratch_shapes=[
             pltpu.VMEM((rounds,) + own_adjoint.shape, jnp.bfloat16),
@@ -177,7 +181,7 @@
         + [pltpu.VMEM(query.shape, jnp.bfloat16), pltpu.VMEM(query.shape, jnp.bfloat16),
            pltpu.VMEM(query.shape, jnp.bfloat16), pltpu.SemaphoreType.DMA((3,))],
         compiler_params=pltpu.CompilerParams(collective_id=1, has_side_effects=True),
-    )(own_adjoint, query, key, value, grad_att, state_half)
+    )(query, key, value, grad_att, state_half)
     gq, gk, gv = pl.pallas_call(
         finish_kernel,
         out_shape=(tokens, tokens, tokens),
@@ -353,9 +357,8 @@
     grad_att = norm_back(grad_normed.reshape(tok_rows, heads_here, head_dim))[0].astype(
         jnp.bfloat16
     )
-    own_adjoint = jnp.einsum("thi,thj->hij", queries, grad_att, preferred_element_type=jnp.float32)
     grad_query, grad_key, grad_value, init_grad = backward_pass(
-        own_adjoint, query, key, value, grad_att.reshape(tok_rows, width), state_half
+        query, key, value, grad_att.reshape(tok_rows, width), state_half
     )
     return (mixed, grad_query, grad_key, grad_value, init_grad)
 

time: 204 us -> 205 us (level)
  Pallas kernels: 148 us -> 151 us
    pallas_call x1, Pallas kernels: 36.7 us -> 39.6 us  [backward_pass(): pl.pallas_call(backward_kernel, out_shape=(tokens, accs, accs, jax.ShapeD...]
  transfers between devices with their start and end apart: 2 -> 2, of which waited for: 0 -> 0; matrix products, arithmetic and copies ran while one was open for 13% -> 12% of each run, Pallas kernels for 73% -> 74%
where the time goes in v17:
time: 205 us; the launch traced here: 204 us
  Pallas kernels  151 us (74%)
  matrix products  29.1 us (14%)
  between operations  14.2 us (7%)
  local copies, waits for them, and re-layouts  6.81 us (3%)
  other arithmetic  2.98 us (1%)
    pallas_call x1, Pallas kernels, gather_and_scan(): pl.pallas_call(functools.partial(gather_kernel, ny, ca), out_shape=(jax.S...  107 us
    pallas_call x1, Pallas kernels, backward_pass(): pl.pallas_call(backward_kernel, out_shape=(tokens, accs, accs, jax.ShapeD...  39.6 us
    dot_general x1, matrix products, shards(): jnp.dot(normed, weight_rows, preferred_element_type=jnp.float32)  11.6 us
    dot_general x1, matrix products, shards(): lax.dot_general(out_grad[:, half:], other_half, contract, preferred_eleme...  5.65 us
    dot_general x1, matrix products, shards(): lax.dot_general(out_grad[:, :half], first_rows, contract, preferred_eleme...  5.48 us
    pallas_call x1, Pallas kernels, backward_pass(): pl.pallas_call(finish_kernel, out_shape=(tokens, tokens, tokens), in_spec...  4.12 us
  transfers between devices with their start and end apart: 2, of which 0 were waited for; matrix products, arithmetic and copies ran while one was open for 12% of the time, Pallas kernels for 74%

profile of v17, /device:TPU:2, one launch (start us, length us, event | category | flops | bytes accessed | tf_op | source)
XLA Modules:
  0.0 204.3 jit_solution(4791856501390548400)
XLA Ops:
  7.2 0.0 all-gather.2.cloned.1.call-start
  7.2 1.8 fusion.23
  9.0 0.0 all-gather.2.cloned.1.call-update
  9.0 0.0 reduce-scatter.2.cloned.1.call-start
  9.1 1.4 copy.17
  10.5 1.4 copy.18
  11.9 0.3 copy.19
  12.2 1.1 fusion.24.value_ref
  13.3 107.3 %shard_map.101 = (bf16[8,4,24,3072]{3,2,1,0:T(8,128)(2,1)}, f32[6,128,128]{2,1,0:T(8,128)}) custom-call(f32[6,128,128]{2,1,0:T(8,128)} %fusion.24.value_ref, bf16[24,3072]{1,0:T(8,128)(2,1)} %get-tuple-element.32.w_ref), custom_call_target="tpu_custom_call" | custom-call | tf_op jit(solution)/shard_map/pallas_call | solution.py:295
  120.6 0.8 iota_compare_fusion
  121.4 1.2 add_convert_fusion.sh_ref
  122.6 1.6 fusion.25
  124.2 3.8 %multiply_reduce_fusion.1 = (f32[512,6]{0,1:T(8,128)S(1)}, f32[512,6,128]{0,2,1:T(8,128)S(1)}) fusion(f32[6,128,512]{2,1,0:T(8,128)} %fusion.25, bf16[512,6,128]{0,2,1:T(8,128)(2,1)} %bitcast.30, pred[512,512]{1,0:T(8,128)(4,1)} %iota_compare_fusion, bf16[512,6,128]{0,2,1:T(8,128)(2,1)S(1)} %bitcast.26, bf16[512,6,128]{0,2,1:T(8,128)(2,1)S(1)} %bitcast.28), kind=kOutput, calls=%fused_computation.19 | convolution fusion | flops 809628672 | bytes 5779456 | tf_op jit(solution)/shard_map/hts,shj->thj/dot_general | solution.py:338
  128.0 0.2 multiply_convert_fusion
  128.2 0.0 all-gather.2.cloned.1.call-done
  128.2 11.6 %fusion.4 = bf16[512,6144]{1,0:T(8,128)(2,1)} fusion(bf16[512,768]{0,1:T(8,128)(2,1)S(1)} %bitcast.32, bf16[768,3072]{1,0:T(8,128)(2,1)} %all-gather.2.cloned.1.call-done, bf16[768,3072]{1,0:T(8,128)(2,1)} %bitcast.33), kind=kOutput, calls=%fused_computation.4 | convolution fusion | flops 4853858304 | bytes 16515072 | tf_op jit(solution)/shard_map/dot_general | solution.py:347
  139.8 5.7 %fusion.8 = f32[768,512]{1,0:T(8,128)S(1)} fusion(bf16[768,3072]{1,0:T(8,128)(2,1)} %all-gather.2.cloned.1.call-done, bf16[512,6144]{1,0:T(8,128)(2,1)} %param.11), kind=kOutput, calls=%fused_computation.7 | convolution fusion | flops 2415919104 | bytes 9437184 | tf_op jit(solution)/shard_map/dot_general | solution.py:352
  145.5 5.5 %fusion.17 = f32[768,512]{1,0:T(8,128)S(1)} fusion(f32[768,512]{1,0:T(8,128)S(1)} %fusion.8, bf16[768,3072]{1,0:T(8,128)(2,1)} %bitcast.34, bf16[512,6144]{1,0:T(8,128)(2,1)} %param.11), kind=kOutput, calls=%fused_computation.20 | convolution fusion | flops 2416312320 | bytes 11010048 | tf_op jit(solution)/shard_map/dot_general | solution.py:350
  150.9 0.4 multiply_reduce_fusion
  151.3 0.4 fusion.16
  151.8 1.2 copy.23.ga_hbm
  152.9 39.6 %shard_map.102 = (bf16[512,768]{1,0:T(8,128)(2,1)}, bf16[512,768]{1,0:T(8,128)(2,1)}, bf16[512,768]{1,0:T(8,128)(2,1)}, bf16[6,128,128]{2,1,0:T(8,128)(2,1)}, f32[6,128,128]{2,1,0:T(8,128)}) custom-call(bf16[512,768]{1,0:T(8,128)(2,1)} %q_hbm.1, bf16[512,768]{1,0:T(8,128)(2,1)} %k_ref.1, bf16[512,768]{1,0:T(8,128)(2,1)} %v_ref.1, ...), custom_call_target="tpu_custom_call" | custom-call | tf_op jit(solution)/shard_map/pallas_call | solution.py:169
  192.6 4.1 %shard_map.103 = (bf16[512,768]{1,0:T(8,128)(2,1)}, bf16[512,768]{1,0:T(8,128)(2,1)}, bf16[512,768]{1,0:T(8,128)(2,1)}) custom-call(bf16[512,768]{1,0:T(8,128)(2,1)} %get-tuple-element.23.gq_in, bf16[512,768]{1,0:T(8,128)(2,1)} %get-tuple-element.24.gk_acc, bf16[512,768]{1,0:T(8,128)(2,1)} %get-tuple-element.25.gv_acc, bf16[512,768]{1,0:T(8,128)(2,1)} %v_ref.1, ...), custom_call_target="tpu_custom_call" | custom-call | tf_op jit(solution)/shard_map/pallas_call | solution.py:185
  196.7 0.7 copy.28
  (12 shorter events, 0.1 us)
Async XLA Ops:
  7.2 4.7 %copy-start = (bf16[512,768]{1,0:T(8,128)(2,1)S(1)}, bf16[512,768]{1,0:T(8,128)(2,1)}, u32[]{:S(2)}) copy-start(bf16[512,768]{1,0:T(8,128)(2,1)} %v_ref.1) | copy-start | bytes 2359300
  7.2 121.0 %all-gather.2.cloned.1.call-start = ((), (), s32[]{:S(2)}) async-start(), calls=%async_computation.1 | async-start | bytes 4866048 | tf_op jit(solution)/shard_map/all_gather | solution.py:331
  9.0 187.7 %reduce-scatter.2.cloned.1.call-start = ((), (), s32[]{:S(2)}) async-start(), calls=%async_computation.2 | async-start | bytes 7077888 | tf_op jit(solution)/shard_map/reduce_scatter | solution.py:353
  12.2 110.4 %copy-start.1 = (bf16[512,768]{0,1:T(8,128)(2,1)}, bf16[512,768]{0,1:T(8,128)(2,1)S(1)}, u32[]{:S(2)}) copy-start(bf16[512,768]{0,1:T(8,128)(2,1)S(1)} %copy.19) | copy-start | bytes 2359300
  122.6 5.4 %copy-start.2 = (bf16[6,128,128]{2,1,0:T(8,128)(2,1)}, bf16[6,128,128]{2,1,0:T(8,128)(2,1)S(1)}, u32[]{:S(2)}) copy-start(bf16[6,128,128]{2,1,0:T(8,128)(2,1)S(1)} %add_convert_fusion.sh_ref) | copy-start | bytes 589828
  192.5 4.1 %copy-start.3 = (f32[6,128,128]{2,1,0:T(8,128)S(1)}, f32[6,128,128]{2,1,0:T(8,128)}, u32[]{:S(2)}) copy-start(f32[6,128,128]{2,1,0:T(8,128)} %get-tuple-element.44) | copy-start | bytes 1179652
Sparse Core Ops, SparseCore 0:
  11.2 107.5 all-gather.1
  139.9 41.0 reduce-scatter.1
